TPU v7x, 32 devices: a whole 2x2x4 slice. The times are simulated.
32 devices in a mesh: space: 8 (over z, core), chan: 4 (over y, x).
Axes of the slice: x: 2, y: 2, z: 4, core: 2. Of those that a mesh axis runs over, the one named last changes fastest.
Arguments:
- tensor_field: bfloat16 [16, 512, 4096], P('space', 'chan'), may hold values from -6 to 6
- radial: bfloat16 [5, 4, 128, 128], replicated, may hold values from -0.078125 to 0.078125
Outputs:
- convolved: bfloat16 [16, 512, 4096], P('space', 'chan')
All inputs are finite; a program needn't handle non-finite values.
Results may differ from a plain program's by a relative error of at most 0.006.
Values may be sent and summed in bfloat16 or wider, within the bound.
No kernel may reach another device: no remote copies, remote signals or barrier semaphores. Data moves between devices by JAX's collectives and lax.ppermute only.
A program may use at most 192 MiB of HBM per device.

v0:
```python
import jax
import jax.numpy as jnp
import numpy as np
from jax import lax
from jax.sharding import PartitionSpec as P

NY = 64


def shifted(x, axis, by):
    count = lax.axis_size(axis)
    return lax.ppermute(x, axis, [(i, (i + by) % count) for i in range(count)])


def offset_table():
    listed = []
    for step_depth in (-1, 0, 1):
        for step_row in (-1, 0, 1):
            for step_col in (-1, 0, 1):
                listed.append((step_depth, step_row, step_col))
    return np.array(listed, dtype=np.int64)


def kernel_table(radial):
    offsets = offset_table()
    shells = np.abs(offsets).sum(axis=1)
    scaled = offsets / np.sqrt(np.maximum(shells, 1))[:, None]
    direction = jnp.asarray(scaled, dtype=jnp.float32)
    weights = radial.astype(jnp.float32)[:, shells]
    units = [
        direction[:, 2][:, None, None],
        direction[:, 1][:, None, None],
        direction[:, 0][:, None, None],
    ]
    scalar_w = weights[0]
    vector_w = weights[1]
    lift_w = weights[2]
    project_w = weights[3]
    tensor_w = weights[4]
    scalar_rows = jnp.concatenate([scalar_w] + [unit * lift_w for unit in units], axis=2)
    row_sets = [scalar_rows]
    for first in range(3):
        blocks = [units[first] * project_w]
        for second in range(3):
            block = units[first] * units[second] * tensor_w
            if first == second:
                block = block + vector_w
            blocks.append(block)
        row_sets.append(jnp.concatenate(blocks, axis=2))
    kernels = jnp.concatenate(row_sets, axis=1)
    return kernels.astype(jnp.bfloat16)


def plane_shift(source_layer, step_row, step_col):
    dims_in = source_layer.shape
    lattice = source_layer.reshape(dims_in[:-1] + (NY, dims_in[-1] // NY))
    lattice = jnp.roll(lattice, (-step_row, -step_col), axis=(lattice.ndim - 2, lattice.ndim - 1))
    return lattice.reshape(dims_in)


def unfold_layer(source_layer):
    blocks = []
    for step_row in (-1, 0, 1):
        for step_col in (-1, 0, 1):
            blocks.append(plane_shift(source_layer, step_row, step_col))
    return jnp.concatenate(blocks, axis=1)


def shards(tensor_field, radial):
    kernels = kernel_table(radial)
    per_group = tensor_field.shape[1]
    planes = tensor_field.shape[0]
    components = kernels.shape[1]
    group_index = lax.axis_index("chan")
    own_rows = lax.dynamic_slice_in_dim(kernels, group_index * per_group, per_group, 1)
    stacked = unfold_layer(tensor_field)
    layers = []
    for depth_slot in range(3):
        rows_here = own_rows[9 * depth_slot : 9 * depth_slot + 9].reshape(9 * per_group, components)
        layers.append(
            jnp.einsum("io,zip->zop", rows_here, stacked, preferred_element_type=jnp.float32)
        )
    from_below = shifted(layers[0][planes - 1].astype(jnp.bfloat16), "space", 1).astype(jnp.float32)
    from_above = shifted(layers[2][0].astype(jnp.bfloat16), "space", -1).astype(jnp.float32)
    interior = layers[1]
    interior = interior.at[1:].add(layers[0][: planes - 1])
    interior = interior.at[: planes - 1].add(layers[2][1:])
    interior = interior.at[0].add(from_below)
    interior = interior.at[planes - 1].add(from_above)
    result = lax.psum_scatter(interior, "chan", scatter_dimension=1, tiled=True)
    return result.astype(jnp.bfloat16)


def solution(mesh):
    placed = (P("space", "chan", None), P())
    return jax.shard_map(
        shards, mesh=mesh, in_specs=placed, out_specs=P("space", "chan", None), check_vma=False
    )
```

profile of v0, /device:TPU:0, one launch (start us, length us, event | category | flops | bytes accessed | tf_op | source)
XLA Modules:
  0.0 364.8 jit_solution(9418409334430522977)
XLA Ops:
  6.5 1.2 convert_element_type.17
  7.8 0.7 pad_clamp_fusion
  8.4 4.6 %gather_fusion = f32[27,5,128,128]{3,2,1,0:T(8,128)} fusion(f32[5,4,128,128]{3,2,1,0:T(8,128)S(1)} %convert_element_type.17, s32[1024]{0:T(1024)S(1)} %pad_clamp_fusion), kind=kCustom, calls=%fused_computation | custom fusion | bytes 17694828 | tf_op jit(solution)/shard_map/gather | solution.py:29
  13.0 5.1 %fusion.29 = (f32[1,27,128,128]{3,2,0,1:T(8,128)}, f32[1,27,128,128]{3,2,0,1:T(8,128)}, f32[1,27,128,128]{3,2,0,1:T(8,128)}) fusion(f32[5,27,128,128]{3,2,0,1:T(8,128)} %bitcast.89), kind=kLoop, calls=%fused_computation.103 | loop fusion | bytes 10616832 | tf_op jit(solution)/shard_map/slice | solution.py:36
  18.1 1.6 fusion.24
  19.7 3.1 copy.20
  22.9 1.0 fusion.31
  24.3 3.7 %fusion.21 = (bf16[2,128,64,63]{1,3,2,0:T(8,128)(2,1)}, bf16[2,128,64,63]{1,3,2,0:T(8,128)(2,1)}, bf16[2,128,64,63]{1,3,2,0:T(8,128)(2,1)}, bf16[2,128,64,63]{1,3,2,0:T(8,128)(2,1)}) fusion(bf16[2,128,1,64]{1,3,2,0:T(8,128)(2,1)S(1)} %get-tuple-element.71, bf16[2,128,63,64]{1,3,2,0:T(8,128)(2,1)S(1)} %get-tuple-element.69, ...), kind=kLoop, calls=%fused_computation.57 | loop fusion | flops 4128768 | bytes 12451840 | tf_op jit(solution)/shard_map/jit(_roll_static)/concatenate | solution.py:57
  27.9 2.4 pad_maximum_fusion
  30.4 3.4 fusion.33
  34.0 4.8 %add_convert_fusion = (bf16[27,128,128]{2,1,0:T(8,128)(2,1)S(1)}, bf16[27,128,128]{2,1,0:T(8,128)(2,1)S(1)}, bf16[27,128,128]{2,1,0:T(8,128)(2,1)S(1)}, bf16[27,...) fusion(f32[1,27,128,128]{3,2,0,1:T(8,128)} %get-tuple-element.5, ...), kind=kLoop, calls=%fused_computation.71 | loop fusion | flops 11943936 | bytes 17695692 | tf_op jit(solution)/shard_map/convert.11
  38.8 7.7 %fusion.10 = bf16[27,128,512]{2,1,0:T(8,128)(2,1)S(1)} fusion(s32[]{:T(128)S(6)} %select_n.7, bf16[27,128,128]{2,1,0:T(8,128)(2,1)S(1)} %fusion.24, bf16[27,128,128]{2,1,0:T(8,128)(2,1)S(1)} %get-tuple-element.101, bf16[27,128,128]{2,1,0:T(8,128)(2,1)S(1)} %get-tuple-element.102, bf16[27,128,128]{2,1,0:T(8,128)(2,1)S(1)} %get-tuple-element.103, ...), kind=kLoop, calls=%fused_computation.46 | loop fusion | flops 56623104 | bytes 15040516 | tf_op jit(solution)/shard_map/concatenate | solution.py:50
  46.5 1.9 fusion.30
  48.4 0.8 copy-done.7
  49.2 1.3 pad_maximum_fusion.2
  50.9 0.5 constant_dynamic-update-slice_fusion.7
  51.4 0.8 copy-done.6
  52.6 0.5 constant_dynamic-update-slice_fusion.6
  53.1 0.7 copy-done.9
  53.8 0.6 copy-done.10
  54.4 1.6 pad_maximum_fusion.4
  56.0 0.5 constant_dynamic-update-slice_fusion.5
  56.5 0.5 constant_dynamic-update-slice_fusion.4
  57.0 0.5 constant_dynamic-update-slice_fusion.3
  57.6 0.6 copy-done.5
  58.1 1.3 pad_maximum_fusion.6
  59.4 0.5 constant_dynamic-update-slice_fusion.2
  59.9 0.5 constant_dynamic-update-slice_fusion.1
  60.4 0.6 copy-done.3
  61.5 0.5 constant_dynamic-update-slice_fusion
  62.0 6.4 %copy-done.11 = bf16[2,1152,4096]{1,2,0:T(8,128)(2,1)} copy-done((bf16[2,1152,4096]{1,2,0:T(8,128)(2,1)}, bf16[2,1152,4096]{1,2,0:T(8,128)(2,1)S(1)}, u32[]{:S(2)}) %copy-start.11) | copy-done | bytes 18874392
  68.4 15.1 %convolution_bitcast_fusion.1 = f32[2,512,4096]{1,2,0:T(8,128)S(1)} fusion(bf16[2,1152,4096]{1,2,0:T(8,128)(2,1)} %copy-done.11, bf16[1152,512,1]{1,0,2:T(8,128)(2,1)} %bitcast.102), kind=kOutput, calls=%fused_computation.18 | convolution fusion | flops 9663676416 | bytes 36831232 | tf_op jit(solution)/shard_map/io,zip->zop/dot_general | solution.py:81
  83.6 2.9 fusion.3
  86.5 0.5 collective-permute-start
  87.0 22.2 %convolution_bitcast_fusion = f32[2,512,4096]{1,2,0:T(8,128)} fusion(bf16[2,1152,4096]{1,2,0:T(8,128)(2,1)} %copy-done.11, bf16[1152,512,1]{1,0,2:T(8,128)(2,1)} %bitcast.101), kind=kOutput, calls=%fused_computation.17 | convolution fusion | flops 9663676416 | bytes 36831232 | tf_op jit(solution)/shard_map/io,zip->zop/dot_general | solution.py:81
  109.2 6.0 %fusion.4 = bf16[512,4096]{0,1:T(8,128)(2,1)} fusion(f32[2,512,4096]{1,2,0:T(8,128)} %convolution_bitcast_fusion), kind=kLoop, calls=%fused_computation.40 | loop fusion | bytes 8388608 | tf_op jit(solution)/shard_map/convert_element_type | solution.py:84
  115.2 4.5 %collective-permute-start.1 = (bf16[512,4096]{0,1:T(8,128)(2,1)}, bf16[512,4096]{0,1:T(8,128)(2,1)}, u32[]{:S(2)}, u32[]{:S(2)}) collective-permute-start(bf16[512,4096]{0,1:T(8,128)(2,1)} %fusion.4), channel_id=1, source_target_pairs={{0,28},{4,0},{8,4},{12,8},{16,12},{20,16},{24,20},{28,24},{1,29},{... | collective-permute-start | bytes 12582920 | tf_op jit(solution)/shard_map/ppermute | solution.py:12
  119.8 15.2 %fusion.35 = f32[2,4096,512]{2,1,0:T(8,128)S(1)} fusion(bf16[2,1152,4096]{1,2,0:T(8,128)(2,1)} %copy-done.11, bf16[1152,512,1]{1,0,2:T(8,128)(2,1)} %bitcast.100), kind=kOutput, calls=%fused_computation.109 | convolution fusion | flops 9663676416 | bytes 36831232 | tf_op jit(solution)/shard_map/io,zip->zop/dot_general | solution.py:81
  135.0 5.7 %copy-done.1 = f32[2,4096,512]{2,1,0:T(8,128)} copy-done((f32[2,4096,512]{2,1,0:T(8,128)}, f32[2,4096,512]{2,1,0:T(8,128)S(1)}, u32[]{:S(2)}) %copy-start.1) | copy-done | bytes 16777240
  140.7 5.8 %copy.63 = f32[2,512,4096]{1,2,0:T(8,128)} copy(f32[2,512,4096]{1,2,0:T(8,128)S(1)} %bitcast.88) | data formatting | bytes 33554432
  146.5 11.1 %fusion.1 = f32[2,512,4096]{1,2,0:T(8,128)} fusion(f32[2,512,4096]{1,2,0:T(8,128)} %copy.63, f32[2,512,4096]{1,2,0:T(8,128)} %copy-done.2, f32[2,4096,512]{2,1,0:T(8,128)} %copy-done.1), kind=kLoop, calls=%fused_computation.25 | loop fusion | flops 2097152 | bytes 25165824 | tf_op jit(solution)/shard_map/scatter-add | solution.py:86
  157.6 11.2 %slice_add_fusion.1 = f32[1,512,4096]{1,2,0:T(8,128)} fusion(f32[2,512,4096]{1,2,0:T(8,128)} %convolution_bitcast_fusion, f32[2,512,4096]{1,2,0:T(8,128)} %fusion.1), kind=kLoop, calls=%fused_computation.23 | loop fusion | flops 2097152 | bytes 25165824 | tf_op jit(solution)/shard_map/add | solution.py:87
  168.8 7.8 %constant_dynamic-update-slice_fusion.9 = f32[2,512,4096]{1,2,0:T(8,128)} fusion(f32[2,512,4096]{1,2,0:T(8,128)} %fusion.1, f32[1,512,4096]{1,2,0:T(8,128)} %slice_add_fusion.1), kind=kLoop, calls=%fused_computation.101 | loop fusion | bytes 16777216 | tf_op jit(solution)/shard_map/scatter-add | solution.py:87
  176.6 6.8 %fusion.2 = f32[2,512,4096]{1,2,0:T(8,128)} fusion(f32[2,512,4096]{1,2,0:T(8,128)} %constant_dynamic-update-slice_fusion.9, f32[1,512,4096]{1,2,0:T(8,128)S(1)} %copy-done, bf16[512,4096]{0,1:T(8,128)(2,1)} %collective-permute-done), kind=kLoop, calls=%fused_computation.28 | loop fusion | flops 4194304 | bytes 20971520 | tf_op jit(solution)/shard_map/scatter-add | solution.py:88
  183.4 9.2 %fusion = f32[2,512,4096]{1,2,0:T(8,128)} fusion(f32[2,512,4096]{1,2,0:T(8,128)} %fusion.2, bf16[512,4096]{0,1:T(8,128)(2,1)} %collective-permute-done.1), kind=kLoop, calls=%fused_computation.21 | loop fusion | flops 4194304 | bytes 20971520 | tf_op jit(solution)/shard_map/scatter-add | solution.py:89
  192.6 159.7 %reduce-scatter.2.cloned.1.call-done = f32[2,128,4096]{1,2,0:T(8,128)} async-done(((f32[2,512,4096]{1,2,0:T(8,128)}), f32[2,128,4096]{1,2,0:T(8,128)}) %reduce-scatter.2.cloned.1.call-update) | async-done | bytes 4194320 | tf_op jit(solution)/shard_map/reduce_scatter | solution.py:90
  352.3 2.5 convert_element_type.20
  354.8 2.7 copy.26
  (44 shorter events, 1.7 us)
Async XLA Ops:
  6.5 345.8 %reduce-scatter.2.cloned.1.call-start = ((), (), s32[]{:S(2)}) async-start(), calls=%async_computation.1 | async-start | bytes 20971520 | tf_op jit(solution)/shard_map/reduce_scatter | solution.py:90
  30.4 3.6 copy-start.12
  30.4 3.6 copy-start.13
  30.4 3.6 copy-start.14
  30.4 3.6 copy-start.15
  30.4 3.6 copy-start.16
  30.4 3.6 copy-start.17
  30.4 3.6 copy-start.18
  30.4 3.6 copy-start.19
  30.4 3.6 copy-start.20
  46.4 2.8 copy-start.7
  49.2 1.6 copy-start.8
  50.5 1.7 copy-start.6
  52.2 1.6 copy-start.9
  52.2 2.2 copy-start.10
  56.5 1.6 copy-start.5
  58.1 1.8 copy-start.4
  59.4 1.7 copy-start.3
  62.0 6.4 %copy-start.11 = (bf16[2,1152,4096]{1,2,0:T(8,128)(2,1)}, bf16[2,1152,4096]{1,2,0:T(8,128)(2,1)S(1)}, u32[]{:S(2)}) copy-start(bf16[2,1152,4096]{1,2,0:T(8,128)(2,1)S(1)} %constant_dynamic-update-slice_fusion) | copy-start | bytes 56623108
  83.6 25.6 %copy-start.2 = (f32[2,512,4096]{1,2,0:T(8,128)}, f32[2,512,4096]{1,2,0:T(8,128)S(1)}, u32[]{:S(2)}) copy-start(f32[2,512,4096]{1,2,0:T(8,128)S(1)} %convolution_bitcast_fusion.1) | copy-start | bytes 50331652
  86.5 90.1 %collective-permute-start = (bf16[512,4096]{0,1:T(8,128)(2,1)}, bf16[512,4096]{0,1:T(8,128)(2,1)}, u32[]{:S(2)}, u32[]{:S(2)}) collective-permute-start(bf16[512,4096]{0,1:T(8,128)(2,1)} %fusion.3), channel_id=1, source_target_pairs={{0,4},{4,8},{8,12},{12,16},{16,20},{20,24},{24,28},{28,0},{1,5},{5... | collective-permute-start | bytes 12582920 | tf_op jit(solution)/shard_map/ppermute | solution.py:12
  115.2 68.2 %collective-permute-start.1 = (bf16[512,4096]{0,1:T(8,128)(2,1)}, bf16[512,4096]{0,1:T(8,128)(2,1)}, u32[]{:S(2)}, u32[]{:S(2)}) collective-permute-start(bf16[512,4096]{0,1:T(8,128)(2,1)} %fusion.4), channel_id=1, source_target_pairs={{0,28},{4,0},{8,4},{12,8},{16,12},{20,16},{24,20},{28,24},{1,29},{... | collective-permute-start | bytes 12582920 | tf_op jit(solution)/shard_map/ppermute | solution.py:12
  135.0 5.8 %copy-start.1 = (f32[2,4096,512]{2,1,0:T(8,128)}, f32[2,4096,512]{2,1,0:T(8,128)S(1)}, u32[]{:S(2)}) copy-start(f32[2,4096,512]{2,1,0:T(8,128)S(1)} %fusion.35) | copy-start | bytes 50331652
  168.8 7.9 %copy-start = (f32[1,512,4096]{1,2,0:T(8,128)S(1)}, f32[1,512,4096]{1,2,0:T(8,128)}, u32[]{:S(2)}) copy-start(f32[1,512,4096]{1,2,0:T(8,128)} %slice_add_fusion.1) | copy-start | bytes 25165828
Sparse Core Ops, SparseCore 0:
  192.7 159.5 reduce-scatter.1
where the time goes:
time: 371 us; the launch traced here: 365 us
  waiting for transfers between devices  160 us (43%)
  local copies, waits for them, and re-layouts  66.9 us (18%)
  other arithmetic  66.4 us (18%)
  matrix products  52.6 us (14%)
  between operations  14.2 us (4%)
  starting transfers between devices  5.01 us (1%)
    reduce_scatter x1, waiting for transfers between devices, shards(): result = lax.psum_scatter(interior, 'chan', scatter_dimension=1, tiled=True)  160 us
    dot_general x3, matrix products, shards(): jnp.einsum('io,zip->zop', rows_here, stacked, preferred_element_type=jnp....  52.6 us
    unnamed x52, local copies, waits for them, and re-layouts  29.1 us
    concatenate x8, other arithmetic, plane_shift(): jnp.roll(lattice, (-step_row, -step_col), axis=(lattice.ndim - 2, lattice...  11.4 us
    add x1, other arithmetic, shards(): interior = interior.at[:planes - 1].add(layers[2][1:])  11.2 us
    scatter-add x1, other arithmetic, shards(): interior = interior.at[1:].add(layers[0][:planes - 1])  11.1 us
    scatter-add x1, other arithmetic, shards(): interior = interior.at[planes - 1].add(from_above)  9.16 us
    scatter-add x1, local copies, waits for them, and re-layouts, shards(): interior = interior.at[:planes - 1].add(layers[2][1:])  7.85 us
  transfers between devices with their start and end apart: 3, of which 1 were waited for; matrix products, arithmetic and copies ran while one was open for 24% of the time, Pallas kernels for 0%

commit v1 on v0

v1 whole, which is shorter than its diff:
```python
import functools

import jax
import jax.numpy as jnp
import numpy as np
from jax import lax
from jax.experimental import pallas as pl
from jax.experimental.pallas import tpu as pltpu
from jax.sharding import PartitionSpec as P


CS = 128
LANES = 128
HALF = 2048
SLAB = HALF + LANES
CHUNK = 512


def weight_tables():
    index = np.zeros((8, 4, 8, 2), np.int32)
    scale = np.zeros((8, 4, 8, 2), np.float32)
    for comp in range(4):
        for odd in range(2):
            gathered = comp ^ (2 if odd else 1)
            reduced = comp ^ (1 if odd else 2)
            pairs = [(comp, comp), (comp, reduced), (gathered, reduced), (gathered, comp)]
            for slot, (i, o) in enumerate(pairs):
                z_odd = (i == 3) != (o == 3)
                for t in range(2):
                    for f in range(4):
                        if z_odd and f >= 2:
                            continue
                        d = (t, f % 2, 1 if (z_odd or f >= 2) else 0)
                        s = sum(d)
                        u = np.float32(np.array(d) / np.sqrt(max(s, 1)))
                        sign = np.float32(-1.0 if (z_odd and odd) else 1.0)
                        kind, first, second = 0, np.float32(0.0), np.float32(0.0)
                        if i == 0 and o == 0:
                            kind, first = 0, np.float32(1.0)
                        elif i == 0:
                            kind, first = 2, u[o - 1]
                        elif o == 0:
                            kind, first = 3, u[i - 1]
                        else:
                            kind = 1
                            first = np.float32(1.0 if i == o else 0.0)
                            second = u[i - 1] * u[o - 1]
                        index[comp * 2 + odd, slot, t * 4 + f] = (kind * 4 + s, 16 + s)
                        scale[comp * 2 + odd, slot, t * 4 + f] = (sign * first, sign * second)
    return index.reshape(8, 64), scale.reshape(8, 64)


def weights_kernel(role_ref, index_ref, scale_ref, radial_ref, out_ref):
    role = role_ref[0]
    for slot in range(4):
        for t in range(2):
            for f in range(4):
                at = (slot * 8 + t * 4 + f) * 2
                first = radial_ref[index_ref[role, at]].astype(jnp.float32) * scale_ref[role, at]
                second = radial_ref[index_ref[role, at + 1]].astype(jnp.float32) * scale_ref[role, at + 1]
                block = jnp.transpose(first + second).astype(jnp.bfloat16)
                out_ref[slot, t * CS : (t + 1) * CS, f * CS : (f + 1) * CS] = block


def weights(role, radial):
    index, scale = weight_tables()
    smem = pl.BlockSpec(memory_space=pltpu.SMEM)
    vmem = pl.BlockSpec(memory_space=pltpu.VMEM)
    return pl.pallas_call(
        weights_kernel,
        out_shape=jax.ShapeDtypeStruct((4, 2 * CS, 4 * CS), jnp.bfloat16),
        in_specs=[smem, smem, smem, vmem],
        out_specs=vmem,
        cost_estimate=pl.CostEstimate(flops=0, bytes_accessed=4 << 20, transcendentals=0),
        name="weights",
    )(role, jnp.asarray(index), jnp.asarray(scale), radial.reshape(20, CS, CS))


def slab_kernel(role_ref, field_ref, keep_ref, give_ref):
    odd = role_ref[0] % 2
    low = lax.broadcasted_iota(jnp.int32, (field_ref.shape[1], LANES), 1) < LANES // 2
    parts = []
    for half in range(2):
        start = half * HALF
        after = field_ref[0, :, (start + HALF) % (2 * HALF) : (start + HALF) % (2 * HALF) + LANES]
        before = field_ref[0, :, (start - LANES) % (2 * HALF) : (start - LANES) % (2 * HALF) + LANES]
        parts.append((field_ref[0, :, start : start + HALF], jnp.where(low, after, before)))
    for parity in range(2):

        @pl.when(odd == parity)
        def _():
            for ref, half in ((keep_ref, parity), (give_ref, 1 - parity)):
                ref[0, :, :HALF] = parts[half][0]
                ref[0, :, HALF:] = parts[half][1]


def slabs(role, field):
    rows = 32
    slab = jax.ShapeDtypeStruct((2, CS, SLAB), jnp.bfloat16)
    block = pl.BlockSpec((1, rows, SLAB), lambda p, r, role: (p, r, 0))
    return pl.pallas_call(
        slab_kernel,
        out_shape=(slab, slab),
        grid_spec=pltpu.PrefetchScalarGridSpec(
            num_scalar_prefetch=1,
            grid=(2, CS // rows),
            in_specs=[pl.BlockSpec((1, rows, 2 * HALF), lambda p, r, role: ((p + role[0]) % 2, r, 0))],
            out_specs=(block, block),
        ),
        cost_estimate=pl.CostEstimate(flops=0, bytes_accessed=5 << 20, transcendentals=0),
        name="slabs",
    )(role, field)


def tile_roll(block, by):
    return jnp.concatenate(
        [pltpu.roll(block[:, at : at + LANES], by, 1) for at in range(0, block.shape[1], LANES)], axis=1
    )


def pair_chunk(chunk, triple, weight, sigma, tau, z_odd):
    lane = lax.broadcasted_iota(jnp.int32, (CS, CHUNK), 1)
    low = lane % LANES < LANES // 2
    tiles = CHUNK // LANES
    before = lax.rem(chunk * tiles + SLAB // LANES - 1, SLAB // LANES)

    def load(ref):
        return jnp.concatenate(
            [
                ref[:, pl.ds(pl.multiple_of(before * LANES, LANES), LANES)],
                ref[:, pl.ds(pl.multiple_of(chunk * CHUNK, LANES), CHUNK + LANES)],
            ],
            axis=1,
        ).astype(jnp.float32)

    below, here, above = triple
    if z_odd:
        sources = [load(above) - load(below)]
    else:
        sources = [load(here), load(above) + load(below)]
    features = []
    for source in sources:
        features.append(source[:, LANES:-LANES].astype(jnp.bfloat16))
        summed = source[:, LANES:] + sigma * source[:, :-LANES]
        chosen = jnp.where(low, summed[:, LANES:], summed[:, :-LANES])
        features.append(tile_roll(chosen, LANES // 2).astype(jnp.bfloat16))
    stacked = jnp.concatenate(features, axis=0)
    total = jnp.dot(weight, stacked, preferred_element_type=jnp.float32)
    centre, side = total[:CS], total[CS:]
    swapped = tile_roll(side, LANES // 2)
    right = tile_roll(jnp.where(lane % 64 == 0, swapped, side), LANES - 1)
    left = tile_roll(jnp.where(lane % 64 == 63, swapped, side), 1)
    return centre + right + tau * left


def conv_kernel(jobs, n_planes, n_accs, role_ref, *refs):
    role = role_ref[0]
    comp, odd = role // 2, role % 2
    gathered = comp ^ (1 + odd)
    reduced = comp ^ (2 - odd)
    pairs = [(comp, comp), (comp, reduced), (gathered, reduced), (gathered, comp)]
    weight_ref = refs[0]
    planes = refs[1 : 1 + n_planes]
    accs = refs[1 + n_planes : 1 + n_planes + n_accs]
    outs = refs[1 + n_planes + n_accs :]
    for triple, slot, acc, out in jobs:
        i, o = pairs[slot]

        def differ(at):
            return (i == at).astype(jnp.int32) != (o == at).astype(jnp.int32)

        tau = jnp.where(differ(1), -1.0, 1.0)
        sigma = jnp.where(differ(2), -1.0, 1.0)
        refs_here = tuple(planes[at] for at in triple)

        def run(z_odd, columns, slot=slot, acc=acc, out=out, refs_here=refs_here, tau=tau, sigma=sigma):
            def body(chunk, carry):
                weight = weight_ref[slot, :, :columns]
                value = pair_chunk(chunk, refs_here, weight, sigma, tau, z_odd)
                where = pl.ds(pl.multiple_of(chunk * CHUNK, CHUNK), CHUNK)
                if acc is not None:
                    value = value + accs[acc][:, where].astype(jnp.float32)
                outs[out][:, where] = value.astype(outs[out].dtype)
                return carry

            lax.fori_loop(0, HALF // CHUNK, body, 0)

        odd_in_z = differ(3)

        @pl.when(odd_in_z)
        def _():
            run(True, 2 * CS)

        @pl.when(jnp.logical_not(odd_in_z))
        def _():
            run(False, 4 * CS)


def conv(name, role, weight, planes, accs, jobs, out_types):
    vmem = pl.BlockSpec(memory_space=pltpu.VMEM)
    flops = len(jobs) * 2 * 256 * 512 * HALF
    size = sum(a.size * a.dtype.itemsize for a in (*planes, *accs)) + len(out_types) * CS * HALF * 4
    return pl.pallas_call(
        functools.partial(conv_kernel, jobs, len(planes), len(accs)),
        out_shape=tuple(jax.ShapeDtypeStruct((CS, HALF), t) for t in out_types),
        in_specs=[pl.BlockSpec(memory_space=pltpu.SMEM)] + [vmem] * (1 + len(planes) + len(accs)),
        out_specs=tuple(vmem for _ in out_types),
        compiler_params=pltpu.CompilerParams(vmem_limit_bytes=48 << 20),
        cost_estimate=pl.CostEstimate(flops=flops, bytes_accessed=size, transcendentals=0),
        name=name,
    )(role, weight, *planes, *accs)


def final_kernel(role_ref, *refs):
    own, others, out_ref = refs[:4], refs[4:8], refs[8]
    plane, side = pl.program_id(0), pl.program_id(1)
    for p in range(2):

        @pl.when((plane == p) & (side == 0))
        def _():
            out_ref[0] = (own[p][...].astype(jnp.float32) + own[2 + p][...].astype(jnp.float32)).astype(out_ref.dtype)

        @pl.when((plane == p) & (side == 1))
        def _():
            out_ref[0] = (others[p][...].astype(jnp.float32) + others[2 + p][...].astype(jnp.float32)).astype(
                out_ref.dtype
            )


def final(role, own, others):
    def at(plane, side, role):
        odd = role[0] % 2
        return ((plane + odd) % 2, 0, (side + odd) % 2)

    vmem = pl.BlockSpec(memory_space=pltpu.VMEM)
    return pl.pallas_call(
        final_kernel,
        out_shape=jax.ShapeDtypeStruct((2, CS, 2 * HALF), jnp.bfloat16),
        grid_spec=pltpu.PrefetchScalarGridSpec(
            num_scalar_prefetch=1,
            grid=(2, 2),
            in_specs=[vmem] * 8,
            out_specs=pl.BlockSpec((1, CS, HALF), at),
        ),
        compiler_params=pltpu.CompilerParams(vmem_limit_bytes=48 << 20),
        cost_estimate=pl.CostEstimate(flops=0, bytes_accessed=8 << 20, transcendentals=0),
        name="final",
    )(role, *own, *others)


def shards(tensor_field, radial):
    n_space, n_chan = lax.axis_size("space"), lax.axis_size("chan")
    sub = n_chan // 4
    chips = n_space // 2
    field = tensor_field
    if sub > 1:
        groups = [[g * sub + h for h in range(sub)] for g in range(4)]
        field = lax.all_gather(field, "chan", axis_index_groups=groups, axis=1, tiled=True)

    def permute(value, place):
        pairs = []
        for s in range(n_space):
            for c in range(4):
                to_s, to_c = place(s // 2, s % 2, c)
                for h in range(sub):
                    pairs.append((s * n_chan + c * sub + h, to_s * n_chan + to_c * sub + h))
        return lax.ppermute(value, ("space", "chan"), pairs)

    def outward(z, k):
        return (z + (1 if k else -1)) % chips

    def gather_group(k, c):
        return c ^ (2 if k else 1)

    def reduce_group(k, c):
        return c ^ (1 if k else 2)

    role = ((lax.axis_index("chan") // sub) * 2 + lax.axis_index("space") % 2).astype(jnp.int32).reshape(1)

    keep, give = slabs(role, field)
    gather_near = permute(keep, lambda z, k, c: (2 * z + k, gather_group(k, c)))
    halo_near = permute(give[0], lambda z, k, c: (2 * outward(z, k) + 1 - k, c))
    halo_far = permute(keep[0], lambda z, k, c: (2 * outward(z, k) + k, c))
    gather_far = permute(give, lambda z, k, c: (2 * z + 1 - k, gather_group(1 - k, c)))
    other = permute(give, lambda z, k, c: (2 * z + 1 - k, c))
    weight = weights(role, radial)

    own = [halo_near, keep[0], keep[1], other[1], other[0], halo_far]
    f32, bf16 = jnp.float32, jnp.bfloat16
    kept, lent = {}, {}
    kept[2], kept[3], lent[2], lent[3] = conv(
        "own_inner", role, weight, own[1:5], [],
        [((0, 1, 2), 0, None, 0), ((1, 2, 3), 0, None, 1), ((0, 1, 2), 1, None, 2), ((1, 2, 3), 1, None, 3)],
        [f32] * 4,
    )
    halos = permute(jnp.stack([halo_near, halo_far]), lambda z, k, c: (2 * z + k, gather_group(k, c)))
    near = [halos[0], gather_near[0], gather_near[1], gather_far[1], gather_far[0], halos[1]]

    def reduce_near(value):
        return permute(value, lambda z, k, c: (2 * z + k, reduce_group(k, c)))

    def reduce_far(value):
        return permute(value, lambda z, k, c: (2 * z + 1 - k, reduce_group(k, c)))

    def swap(value):
        return permute(value, lambda z, k, c: (2 * z + 1 - k, c))

    sent2, sent3 = conv(
        "sent_inner", role, weight, near[1:5], [lent[2], lent[3]],
        [((0, 1, 2), 2, 0, 0), ((1, 2, 3), 2, 1, 1)], [bf16] * 2,
    )
    got_inner_near = reduce_near(sent2)
    got_inner_far = reduce_far(sent3)
    kept[1], kept[4], lent[1], lent[4] = conv(
        "own_boundary", role, weight, own, [],
        [((0, 1, 2), 0, None, 0), ((3, 4, 5), 0, None, 1), ((0, 1, 2), 1, None, 2), ((3, 4, 5), 1, None, 3)],
        [f32] * 4,
    )
    sent1, sent4 = conv(
        "sent_boundary", role, weight, near, [lent[1], lent[4]],
        [((0, 1, 2), 2, 0, 0), ((3, 4, 5), 2, 1, 1)], [bf16] * 2,
    )
    got_boundary_near = reduce_near(sent1)
    got_boundary_far = reduce_far(sent4)
    total2, total3, total1, total4 = conv(
        "kept", role, weight, near, [kept[2], kept[3], kept[1], kept[4]],
        [((1, 2, 3), 3, 0, 0), ((2, 3, 4), 3, 1, 1), ((0, 1, 2), 3, 2, 2), ((3, 4, 5), 3, 3, 3)],
        [f32, bf16, f32, bf16],
    )
    crossed = swap(jnp.stack([total4, total3]))
    out = final(
        role,
        [total1, total2, got_boundary_near, got_inner_near],
        [crossed[0], crossed[1], got_boundary_far, got_inner_far],
    )
    if sub > 1:
        out = lax.dynamic_slice_in_dim(out, lax.axis_index("chan") % sub * tensor_field.shape[1], tensor_field.shape[1], 1)
    return out


def solution(mesh):
    placed = (P("space", "chan", None), P())
    return jax.shard_map(
        shards, mesh=mesh, in_specs=placed, out_specs=P("space", "chan", None), check_vma=False
    )
```

time: 371 us -> 119 us (0.32); the launches traced: 365 us -> 119 us
  waiting for transfers between devices: 160 us -> 31.8 us
  other arithmetic: 66.4 us -> 0.21 us
  Pallas kernels: 0 us -> 62.6 us
  local copies, waits for them, and re-layouts: 66.9 us -> 9.41 us
  matrix products: 52.6 us -> 0 us
  between operations: 14.2 us -> 0.11 us
  starting transfers between devices: 5.01 us -> 14.8 us
    reduce_scatter x1 -> x0, waiting for transfers between devices: 160 us -> none  [shards(): result = lax.psum_scatter(interior, 'chan', scatter_dimension=1, tiled=True)]
    pallas_call x0 -> x8, Pallas kernels: none -> 62.6 us  [the longest x5 52.1 us: conv(): pl.pallas_call(functools.partial(conv_kernel, jobs, len(planes), len(accs...]
    dot_general x3 -> x0, matrix products: 52.6 us -> none  [shards(): jnp.einsum('io,zip->zop', rows_here, stacked, preferred_element_type=jnp....]
    ppermute x2 -> x11, waiting for transfers between devices: 0.01 us -> 31.8 us  [permute(): return lax.ppermute(value, ('space', 'chan'), pairs)]
    scatter-add x3 -> x0, other arithmetic: 27.1 us -> none  [the longest x1 11.1 us: shards(): interior = interior.at[1:].add(layers[0][:planes - 1])]
    unnamed x52 -> x12, local copies, waits for them, and re-layouts: 29.1 us -> 3.33 us
    concatenate x9 -> x0, other arithmetic: 19 us -> none  [the longest x8 11.4 us: plane_shift(): jnp.roll(lattice, (-step_row, -step_col), axis=(lattice.ndim - 2, lattice...]
    convert_element_type x3 -> x0, local copies, waits for them, and re-layouts: 11.7 us -> none  [the longest x1 6.03 us: shards(): layers[2][0].astype(jnp.bfloat16)]
  transfers between devices with their start and end apart: 3 -> 11, of which waited for: 1 -> 5; matrix products, arithmetic and copies ran while one was open for 24% -> 4% of each run, Pallas kernels for 0% -> 34%
where the time goes in v1:
time: 119 us
  Pallas kernels  62.6 us (53%)
  waiting for transfers between devices  31.8 us (27%)
  starting transfers between devices  14.8 us (12%)
  local copies, waits for them, and re-layouts  9.41 us (8%)
    pallas_call x5, Pallas kernels, conv(): pl.pallas_call(functools.partial(conv_kernel, jobs, len(planes), len(accs...  52.1 us
    ppermute x11, waiting for transfers between devices, permute(): return lax.ppermute(value, ('space', 'chan'), pairs)  31.8 us
    ppermute x11, starting transfers between devices, permute(): return lax.ppermute(value, ('space', 'chan'), pairs)  14.8 us
    pallas_call x1, Pallas kernels, slabs(): pl.pallas_call(slab_kernel, out_shape=(slab, slab), grid_spec=pltpu.Prefe...  5.75 us
    unnamed x12, local copies, waits for them, and re-layouts  3.33 us
    pallas_call x1, Pallas kernels, weights(): pl.pallas_call(weights_kernel, out_shape=jax.ShapeDtypeStruct((4, 2 * CS,...  2.65 us
    squeeze x2, local copies, waits for them, and re-layouts, shards(): own = [halo_near, keep[0], keep[1], other[1], other[0], halo_far]  2.6 us
  transfers between devices with their start and end apart: 11, of which 5 were waited for; matrix products, arithmetic and copies ran while one was open for 4% of the time, Pallas kernels for 34%

profile of v1, /device:TPU:0, one launch (start us, length us, event | category | flops | bytes accessed | tf_op | source)
XLA Modules:
  0.0 118.8 jit_solution(15864155228774801871)
XLA Ops:
  0.0 5.7 %slabs.1 = (bf16[2,128,2176]{2,1,0:T(8,128)(2,1)}, bf16[2,128,2176]{2,1,0:T(8,128)(2,1)}) custom-call(s32[1]{0:T(128)} %bitcast.role_ref, bf16[2,128,4096]{2,1,0:T(8,128)(2,1)} %field_ref.1), custom_call_target="tpu_custom_call" | custom-call | bytes 5242880 | tf_op jit(solution)/shard_map/slabs/pallas_call | solution.py:101
  5.7 1.9 %slice_bitcast_fusion.10 = bf16[128,2176]{1,0:T(8,128)(2,1)} fusion(bf16[2,128,2176]{2,1,0:T(8,128)(2,1)} %get-tuple-element.23), kind=kLoop, calls=%fused_computation.12 | loop fusion | bytes 1114112 | tf_op jit(solution)/shard_map/squeeze | solution.py:282
  7.7 4.5 %collective-permute-start = (bf16[128,2176]{1,0:T(8,128)(2,1)}, bf16[128,2176]{1,0:T(8,128)(2,1)S(1)}, u32[]{:S(2)}, u32[]{:S(2)}) collective-permute-start(bf16[128,2176]{1,0:T(8,128)(2,1)} %slice_bitcast_fusion.10), channel_id=1, source_target_pairs={{0,28},{1,29},{2,30},{3,31},{4,8},{5,9},{6,10},{7,11},{8,4},{9,5},... | collective-permute-start | bytes 1671176 | tf_op jit(solution)/shard_map/ppermute | solution.py:267
  12.1 1.5 %collective-permute-start.3 = (bf16[2,128,2176]{2,1,0:T(8,128)(2,1)}, bf16[2,128,2176]{2,1,0:T(8,128)(2,1)}, u32[]{:S(2)}, u32[]{:S(2)}) collective-permute-start(bf16[2,128,2176]{2,1,0:T(8,128)(2,1)} %get-tuple-element.24), channel_id=1, source_target_pairs={{0,1},{1,0},{2,3},{3,2},{4,6},{5,7},{6,4},{7,5},{8,9},{9,8},{10,11... | collective-permute-start | bytes 3342344 | tf_op jit(solution)/shard_map/ppermute | solution.py:267
  13.6 1.3 %slice_bitcast_fusion.8 = (bf16[128,2176]{1,0:T(8,128)(2,1)S(1)}, bf16[128,2176]{1,0:T(8,128)(2,1)S(1)}) fusion(bf16[2,128,2176]{2,1,0:T(8,128)(2,1)} %get-tuple-element.24), kind=kLoop, calls=%fused_computation.10 | loop fusion | bytes 2228224 | tf_op jit(solution)/shard_map/squeeze | solution.py:288
  14.9 0.6 collective-permute-start.1
  15.6 0.0 collective-permute-start.5
  15.6 1.6 %collective-permute-start.4 = (bf16[2,128,2176]{2,1,0:T(8,128)(2,1)}, bf16[2,128,2176]{2,1,0:T(8,128)(2,1)S(1)}, u32[]{:S(2)}, u32[]{:S(2)}) collective-permute-start(bf16[2,128,2176]{2,1,0:T(8,128)(2,1)} %get-tuple-element.23), channel_id=1, source_target_pairs={{0,6},{1,7},{2,4},{3,5},{4,1},{5,0},{6,3},{7,2},{8,14},{9,15},{10,... | collective-permute-start | bytes 3342344 | tf_op jit(solution)/shard_map/ppermute | solution.py:267
  17.2 2.6 %weights.1.refs_0_ = bf16[4,256,512]{2,1,0:T(8,128)(2,1)} custom-call(s32[1]{0:T(128)} %bitcast.role_ref, s32[8,64]{1,0:T(8,128)} %constant.37.clone.index_ref, f32[8,64]{1,0:T(8,128)} %constant.38.clone.scale_ref, bf16[20,128,128]{2,1,0:T(8,128)(2,1)} %bitcast.36), custom_call_target="tpu_custom_call" | custom-call | bytes 4194304 | tf_op jit(solution)/shard_map/weights/pallas_call | solution.py:69
  19.8 5.7 %collective-permute-done.refs_1_ = bf16[128,2176]{1,0:T(8,128)(2,1)S(1)} collective-permute-done((bf16[128,2176]{1,0:T(8,128)(2,1)}, bf16[128,2176]{1,0:T(8,128)(2,1)S(1)}, u32[]{:S(2)}, u32[]{:S(2)}) %collective-permute-start) | collective-permute-done | bytes 557088 | tf_op jit(solution)/shard_map/ppermute | solution.py:267
  25.5 10.4 %collective-permute-done.1.refs_6_ = bf16[128,2176]{1,0:T(8,128)(2,1)S(1)} collective-permute-done((bf16[128,2176]{1,0:T(8,128)(2,1)S(1)}, bf16[128,2176]{1,0:T(8,128)(2,1)S(1)}, u32[]{:S(2)}, u32[]{:S(2)}) %collective-permute-start.1) | collective-permute-done | bytes 557088 | tf_op jit(solution)/shard_map/ppermute | solution.py:267
  36.0 0.1 pad_maximum_fusion
  36.1 0.9 collective-permute-start.2
  37.0 0.0 collective-permute-done.3
  37.0 1.3 %slice_bitcast_fusion.5 = (bf16[128,2176]{1,0:T(8,128)(2,1)S(1)}, bf16[128,2176]{1,0:T(8,128)(2,1)S(1)}) fusion(bf16[2,128,2176]{2,1,0:T(8,128)(2,1)} %collective-permute-done.3), kind=kLoop, calls=%fused_computation.7 | loop fusion | bytes 2228224 | tf_op jit(solution)/shard_map/squeeze | solution.py:297
  38.3 0.0 collective-permute-done.5
  38.3 1.3 %slice_bitcast_fusion = (bf16[128,2176]{1,0:T(8,128)(2,1)S(1)}, bf16[128,2176]{1,0:T(8,128)(2,1)S(1)}) fusion(bf16[2,128,2176]{2,1,0:T(8,128)(2,1)} %collective-permute-done.5), kind=kLoop, calls=%fused_computation.2 | loop fusion | bytes 2228224 | tf_op jit(solution)/shard_map/squeeze | solution.py:288
  39.6 12.4 %own_inner.1 = (f32[128,2048]{1,0:T(8,128)S(1)}, f32[128,2048]{1,0:T(8,128)S(1)}, f32[128,2048]{1,0:T(8,128)S(1)}, f32[128,2048]{1,0:T(8,128)}) custom-call(s32[1]{0:T(128)} %bitcast.role_ref, bf16[4,256,512]{2,1,0:T(8,128)(2,1)} %weights.1.refs_0_, bf16[128,2176]{1,0:T(8,128)(2,1)S(1)} %get-tuple-element.44.refs_1_.refs_2_, ...), custom_call_target="tpu_custom_call" | custom-call | flops 2147483648 | bytes 6422528 | tf_op jit(solution)/shard_map/own_inner/pallas_call | solution.py:203
  52.0 0.0 copy-start.1
  52.0 1.0 copy-done.1
  53.0 0.0 copy-start.2
  53.0 1.0 copy-done.2
  54.0 12.7 %own_boundary.1 = (f32[128,2048]{1,0:T(8,128)S(1)}, f32[128,2048]{1,0:T(8,128)S(1)}, f32[128,2048]{1,0:T(8,128)}, f32[128,2048]{1,0:T(8,128)}) custom-call(s32[1]{0:T(128)} %bitcast.role_ref, bf16[4,256,512]{2,1,0:T(8,128)(2,1)} %weights.1.refs_0_, bf16[128,2176]{1,0:T(8,128)(2,1)S(1)} %collective-permute-done.refs_1_, ...), custom_call_target="tpu_custom_call" | custom-call | flops 2147483648 | bytes 7536640 | tf_op jit(solution)/shard_map/own_boundary/pallas_call | solution.py:203
  66.7 0.0 collective-permute-done.4
  66.7 0.1 slice_bitcast_fusion.3
  66.8 0.9 copy-done.3
  67.7 0.4 copy-done.4
  68.1 0.0 collective-permute-done.2
  68.1 0.1 slice_bitcast_fusion.2
  68.2 13.8 %kept.1 = (f32[128,2048]{1,0:T(8,128)S(1)}, bf16[128,2048]{1,0:T(8,128)(2,1)S(1)}, f32[128,2048]{1,0:T(8,128)}, bf16[128,2048]{1,0:T(8,128)(2,1)S(1)}) custom-call(s32[1]{0:T(128)} %bitcast.role_ref, bf16[4,256,512]{2,1,0:T(8,128)(2,1)} %weights.1.refs_0_, bf16[128,2176]{1,0:T(8,128)(2,1)S(1)} %get-tuple-element.46.refs_1_, ...), custom_call_target="tpu_custom_call" | custom-call | flops 2147483648 | bytes 11730944 | tf_op jit(solution)/shard_map/kept/pallas_call | solution.py:203
  82.0 0.1 pad_maximum_fusion.1
  82.1 2.0 %collective-permute-start.8 = (bf16[2,128,2048]{2,1,0:T(8,128)(2,1)S(1)}, bf16[2,128,2048]{2,1,0:T(8,128)(2,1)S(1)}, u32[]{:S(2)}, u32[]{:S(2)}) collective-permute-start(bf16[2,128,2048]{2,1,0:T(8,128)(2,1)S(1)} %pad_maximum_fusion.1), channel_id=1, source_target_pairs={{0,4},{1,5},{2,6},{3,7},{4,0},{5,1},{6,2},{7,3},{8,12},{9,13},{10,... | collective-permute-start | bytes 3145736 | tf_op jit(solution)/shard_map/ppermute | solution.py:267
  84.1 0.0 copy-done
  84.1 6.5 %sent_inner.1 = (bf16[128,2048]{1,0:T(8,128)(2,1)S(1)}, bf16[128,2048]{1,0:T(8,128)(2,1)S(1)}) custom-call(s32[1]{0:T(128)} %bitcast.role_ref, bf16[4,256,512]{2,1,0:T(8,128)(2,1)S(1)} %copy-done, bf16[128,2176]{1,0:T(8,128)(2,1)S(1)} %get-tuple-element.50.refs_2_.refs_1_, bf16[128,2176]{1,0:T(8,128)(2,1)S(1)} %get-tuple-element.49.refs_3_.refs_2_, ...), custom_call_target="tpu_custom_call" | custom-call | flops 1073741824 | bytes 6422528 | tf_op jit(solution)/shard_map/sent_inner/pallas_call | solution.py:203
  90.6 0.1 collective-permute-start.7
  90.7 0.2 collective-permute-start.10
  90.9 6.8 %sent_boundary.1 = (bf16[128,2048]{1,0:T(8,128)(2,1)S(1)}, bf16[128,2048]{1,0:T(8,128)(2,1)S(1)}) custom-call(s32[1]{0:T(128)} %bitcast.role_ref, bf16[4,256,512]{2,1,0:T(8,128)(2,1)S(1)} %copy-done, bf16[128,2176]{1,0:T(8,128)(2,1)S(1)} %get-tuple-element.46.refs_1_, bf16[128,2176]{1,0:T(8,128)(2,1)S(1)} %get-tuple-element.50.refs_2_.refs_1_, ...), custom_call_target="tpu_custom_call" | custom-call | flops 1073741824 | bytes 7536640 | tf_op jit(solution)/shard_map/sent_boundary/pallas_call | solution.py:203
  97.7 0.0 copy-start.5
  97.7 2.0 %collective-permute-start.6 = (bf16[128,2048]{1,0:T(8,128)(2,1)S(1)}, bf16[128,2048]{1,0:T(8,128)(2,1)S(1)}, u32[]{:S(2)}, u32[]{:S(2)}) collective-permute-start(bf16[128,2048]{1,0:T(8,128)(2,1)S(1)} %get-tuple-element.33), channel_id=1, source_target_pairs={{0,2},{1,3},{2,0},{3,1},{4,5},{5,4},{6,7},{7,6},{8,10},{9,11},{10,... | collective-permute-start | bytes 1572872 | tf_op jit(solution)/shard_map/ppermute | solution.py:267
  99.7 1.4 %collective-permute-start.9 = (bf16[128,2048]{1,0:T(8,128)(2,1)S(1)}, bf16[128,2048]{1,0:T(8,128)(2,1)S(1)}, u32[]{:S(2)}, u32[]{:S(2)}) collective-permute-start(bf16[128,2048]{1,0:T(8,128)(2,1)S(1)} %get-tuple-element.39), channel_id=1, source_target_pairs={{0,6},{1,7},{2,4},{3,5},{4,1},{5,0},{6,3},{7,2},{8,14},{9,15},{10,... | collective-permute-start | bytes 1572872 | tf_op jit(solution)/shard_map/ppermute | solution.py:267
  101.0 0.0 collective-permute-done.8
  101.0 0.1 slice_bitcast_fusion.11
  101.2 0.0 collective-permute-done.7.refs_3_
  101.2 4.4 %collective-permute-done.10.refs_7_ = bf16[128,2048]{1,0:T(8,128)(2,1)S(1)} collective-permute-done((bf16[128,2048]{1,0:T(8,128)(2,1)S(1)}, bf16[128,2048]{1,0:T(8,128)(2,1)S(1)}, u32[]{:S(2)}, u32[]{:S(2)}) %collective-permute-start.10) | collective-permute-done | bytes 524320 | tf_op jit(solution)/shard_map/ppermute | solution.py:267
  105.6 5.5 %collective-permute-done.6.refs_2_ = bf16[128,2048]{1,0:T(8,128)(2,1)S(1)} collective-permute-done((bf16[128,2048]{1,0:T(8,128)(2,1)S(1)}, bf16[128,2048]{1,0:T(8,128)(2,1)S(1)}, u32[]{:S(2)}, u32[]{:S(2)}) %collective-permute-start.6) | collective-permute-done | bytes 524320 | tf_op jit(solution)/shard_map/ppermute | solution.py:267
  111.1 5.7 %collective-permute-done.9.refs_6_ = bf16[128,2048]{1,0:T(8,128)(2,1)S(1)} collective-permute-done((bf16[128,2048]{1,0:T(8,128)(2,1)S(1)}, bf16[128,2048]{1,0:T(8,128)(2,1)S(1)}, u32[]{:S(2)}, u32[]{:S(2)}) %collective-permute-start.9) | collective-permute-done | bytes 524320 | tf_op jit(solution)/shard_map/ppermute | solution.py:267
  116.8 0.0 copy-done.5
  116.8 2.0 %final.1 = bf16[2,128,4096]{2,1,0:T(8,128)(2,1)} custom-call(s32[1]{0:T(128)} %bitcast.role_ref, f32[128,2048]{1,0:T(8,128)S(1)} %copy-done.5, f32[128,2048]{1,0:T(8,128)S(1)} %get-tuple-element.30.refs_1_, bf16[128,2048]{1,0:T(8,128)(2,1)S(1)} %collective-permute-done.6.refs_2_, bf16[128,2048]{1,0:T(8,128)(2,1)S(1)} %collective-permute-done.7.refs_3_, ...), custom_call_target="tpu_custom_call" | custom-call | bytes 8388608 | tf_op jit(solution)/shard_map/final/pallas_call | solution.py:236
  (3 shorter events, 0.0 us)
Async XLA Ops:
  7.7 17.9 %collective-permute-start = (bf16[128,2176]{1,0:T(8,128)(2,1)}, bf16[128,2176]{1,0:T(8,128)(2,1)S(1)}, u32[]{:S(2)}, u32[]{:S(2)}) collective-permute-start(bf16[128,2176]{1,0:T(8,128)(2,1)} %slice_bitcast_fusion.10), channel_id=1, source_target_pairs={{0,28},{1,29},{2,30},{3,31},{4,8},{5,9},{6,10},{7,11},{8,4},{9,5},... | collective-permute-start | bytes 1671176 | tf_op jit(solution)/shard_map/ppermute | solution.py:267
  12.1 24.9 %collective-permute-start.3 = (bf16[2,128,2176]{2,1,0:T(8,128)(2,1)}, bf16[2,128,2176]{2,1,0:T(8,128)(2,1)}, u32[]{:S(2)}, u32[]{:S(2)}) collective-permute-start(bf16[2,128,2176]{2,1,0:T(8,128)(2,1)} %get-tuple-element.24), channel_id=1, source_target_pairs={{0,1},{1,0},{2,3},{3,2},{4,6},{5,7},{6,4},{7,5},{8,9},{9,8},{10,11... | collective-permute-start | bytes 3342344 | tf_op jit(solution)/shard_map/ppermute | solution.py:267
  14.9 21.0 %collective-permute-start.1 = (bf16[128,2176]{1,0:T(8,128)(2,1)S(1)}, bf16[128,2176]{1,0:T(8,128)(2,1)S(1)}, u32[]{:S(2)}, u32[]{:S(2)}) collective-permute-start(bf16[128,2176]{1,0:T(8,128)(2,1)S(1)} %get-tuple-element.44.refs_1_.refs_2_), channel_id=1, source_target_pairs={{0,24},{1,25},{2,26},{3,27},{4,12},{5,13},{6,14},{7,15},{8,0},{9,1... | collective-permute-start | bytes 1671176 | tf_op jit(solution)/shard_map/ppermute | solution.py:267
  15.6 22.7 %collective-permute-start.5 = (bf16[2,128,2176]{2,1,0:T(8,128)(2,1)}, bf16[2,128,2176]{2,1,0:T(8,128)(2,1)}, u32[]{:S(2)}, u32[]{:S(2)}) collective-permute-start(bf16[2,128,2176]{2,1,0:T(8,128)(2,1)} %get-tuple-element.23), channel_id=1, source_target_pairs={{0,4},{1,5},{2,6},{3,7},{4,0},{5,1},{6,2},{7,3},{8,12},{9,13},{10,... | collective-permute-start | bytes 3342344 | tf_op jit(solution)/shard_map/ppermute | solution.py:267
  15.6 51.2 %collective-permute-start.4 = (bf16[2,128,2176]{2,1,0:T(8,128)(2,1)}, bf16[2,128,2176]{2,1,0:T(8,128)(2,1)S(1)}, u32[]{:S(2)}, u32[]{:S(2)}) collective-permute-start(bf16[2,128,2176]{2,1,0:T(8,128)(2,1)} %get-tuple-element.23), channel_id=1, source_target_pairs={{0,6},{1,7},{2,4},{3,5},{4,1},{5,0},{6,3},{7,2},{8,14},{9,15},{10,... | collective-permute-start | bytes 3342344 | tf_op jit(solution)/shard_map/ppermute | solution.py:267
  36.1 32.0 %collective-permute-start.2 = (bf16[2,128,2176]{2,1,0:T(8,128)(2,1)S(1)}, bf16[2,128,2176]{2,1,0:T(8,128)(2,1)S(1)}, u32[]{:S(2)}, u32[]{:S(2)}) collective-permute-start(bf16[2,128,2176]{2,1,0:T(8,128)(2,1)S(1)} %pad_maximum_fusion), channel_id=1, source_target_pairs={{0,1},{1,0},{2,3},{3,2},{4,6},{5,7},{6,4},{7,5},{8,9},{9,8},{10,11... | collective-permute-start | bytes 3342344 | tf_op jit(solution)/shard_map/ppermute | solution.py:267
  52.0 1.0 copy-start.1
  53.0 1.0 copy-start.2
  66.7 1.0 copy-start.3
  66.7 1.4 %copy-start.4 = (f32[128,2048]{1,0:T(8,128)}, f32[128,2048]{1,0:T(8,128)S(1)}, u32[]{:S(2)}) copy-start(f32[128,2048]{1,0:T(8,128)S(1)} %get-tuple-element.28.refs_10_) | copy-start | bytes 3145732
  82.0 2.1 %copy-start = (bf16[4,256,512]{2,1,0:T(8,128)(2,1)S(1)}, bf16[4,256,512]{2,1,0:T(8,128)(2,1)}, u32[]{:S(2)}) copy-start(bf16[4,256,512]{2,1,0:T(8,128)(2,1)} %weights.1.refs_0_) | copy-start | bytes 3145732
  82.1 18.9 %collective-permute-start.8 = (bf16[2,128,2048]{2,1,0:T(8,128)(2,1)S(1)}, bf16[2,128,2048]{2,1,0:T(8,128)(2,1)S(1)}, u32[]{:S(2)}, u32[]{:S(2)}) collective-permute-start(bf16[2,128,2048]{2,1,0:T(8,128)(2,1)S(1)} %pad_maximum_fusion.1), channel_id=1, source_target_pairs={{0,4},{1,5},{2,6},{3,7},{4,0},{5,1},{6,2},{7,3},{8,12},{9,13},{10,... | collective-permute-start | bytes 3145736 | tf_op jit(solution)/shard_map/ppermute | solution.py:267
  90.6 10.5 %collective-permute-start.7 = (bf16[128,2048]{1,0:T(8,128)(2,1)S(1)}, bf16[128,2048]{1,0:T(8,128)(2,1)S(1)}, u32[]{:S(2)}, u32[]{:S(2)}) collective-permute-start(bf16[128,2048]{1,0:T(8,128)(2,1)S(1)} %get-tuple-element.36), channel_id=1, source_target_pairs={{0,2},{1,3},{2,0},{3,1},{4,5},{5,4},{6,7},{7,6},{8,10},{9,11},{10,... | collective-permute-start | bytes 1572872 | tf_op jit(solution)/shard_map/ppermute | solution.py:267
  90.7 14.9 %collective-permute-start.10 = (bf16[128,2048]{1,0:T(8,128)(2,1)S(1)}, bf16[128,2048]{1,0:T(8,128)(2,1)S(1)}, u32[]{:S(2)}, u32[]{:S(2)}) collective-permute-start(bf16[128,2048]{1,0:T(8,128)(2,1)S(1)} %get-tuple-element.40), channel_id=1, source_target_pairs={{0,6},{1,7},{2,4},{3,5},{4,1},{5,0},{6,3},{7,2},{8,14},{9,15},{10,... | collective-permute-start | bytes 1572872 | tf_op jit(solution)/shard_map/ppermute | solution.py:267
  97.7 19.1 %copy-start.5 = (f32[128,2048]{1,0:T(8,128)S(1)}, f32[128,2048]{1,0:T(8,128)}, u32[]{:S(2)}) copy-start(f32[128,2048]{1,0:T(8,128)} %get-tuple-element.29.refs_0_) | copy-start | bytes 3145732
  97.7 13.4 %collective-permute-start.6 = (bf16[128,2048]{1,0:T(8,128)(2,1)S(1)}, bf16[128,2048]{1,0:T(8,128)(2,1)S(1)}, u32[]{:S(2)}, u32[]{:S(2)}) collective-permute-start(bf16[128,2048]{1,0:T(8,128)(2,1)S(1)} %get-tuple-element.33), channel_id=1, source_target_pairs={{0,2},{1,3},{2,0},{3,1},{4,5},{5,4},{6,7},{7,6},{8,10},{9,11},{10,... | collective-permute-start | bytes 1572872 | tf_op jit(solution)/shard_map/ppermute | solution.py:267
  99.7 17.1 %collective-permute-start.9 = (bf16[128,2048]{1,0:T(8,128)(2,1)S(1)}, bf16[128,2048]{1,0:T(8,128)(2,1)S(1)}, u32[]{:S(2)}, u32[]{:S(2)}) collective-permute-start(bf16[128,2048]{1,0:T(8,128)(2,1)S(1)} %get-tuple-element.39), channel_id=1, source_target_pairs={{0,6},{1,7},{2,4},{3,5},{4,1},{5,0},{6,3},{7,2},{8,14},{9,15},{10,... | collective-permute-start | bytes 1572872 | tf_op jit(solution)/shard_map/ppermute | solution.py:267

commit v2 on v1

v2 whole, which is shorter than its diff:
```python
import functools

import jax
import jax.numpy as jnp
import numpy as np
from jax import lax
from jax.experimental import pallas as pl
from jax.experimental.pallas import tpu as pltpu
from jax.sharding import PartitionSpec as P


CS = 128
LANES = 128
HALF = 2048
ROW = 64
SLAB = HALF + 2 * ROW
CHUNK = 512


def weight_tables():
    index = np.zeros((8, 4, 8, 2), np.int32)
    scale = np.zeros((8, 4, 8, 2), np.float32)
    for comp in range(4):
        for odd in range(2):
            gathered = comp ^ (2 if odd else 1)
            reduced = comp ^ (1 if odd else 2)
            pairs = [(comp, comp), (comp, reduced), (gathered, reduced), (gathered, comp)]
            for slot, (i, o) in enumerate(pairs):
                z_odd = (i == 3) != (o == 3)
                for t in range(2):
                    for f in range(4):
                        if z_odd and f >= 2:
                            continue
                        d = (t, f % 2, 1 if (z_odd or f >= 2) else 0)
                        s = sum(d)
                        u = np.float32(np.array(d) / np.sqrt(max(s, 1)))
                        sign = np.float32(-1.0 if (z_odd and odd) else 1.0)
                        kind, first, second = 0, np.float32(0.0), np.float32(0.0)
                        if i == 0 and o == 0:
                            kind, first = 0, np.float32(1.0)
                        elif i == 0:
                            kind, first = 2, u[o - 1]
                        elif o == 0:
                            kind, first = 3, u[i - 1]
                        else:
                            kind = 1
                            first = np.float32(1.0 if i == o else 0.0)
                            second = u[i - 1] * u[o - 1]
                        index[comp * 2 + odd, slot, t * 4 + f] = (kind * 4 + s, 16 + s)
                        scale[comp * 2 + odd, slot, t * 4 + f] = (sign * first, sign * second)
    return index.reshape(8, 64), scale.reshape(8, 64)


def weights_kernel(role_ref, index_ref, scale_ref, radial_ref, out_ref):
    role = role_ref[0]
    for slot in range(4):
        for t in range(2):
            for f in range(4):
                at = (slot * 8 + t * 4 + f) * 2
                first = radial_ref[index_ref[role, at]].astype(jnp.float32) * scale_ref[role, at]
                second = radial_ref[index_ref[role, at + 1]].astype(jnp.float32) * scale_ref[role, at + 1]
                out_ref[slot, f * CS : (f + 1) * CS, t * CS : (t + 1) * CS] = (first + second).astype(jnp.bfloat16)


def weights(role, radial):
    index, scale = weight_tables()
    smem = pl.BlockSpec(memory_space=pltpu.SMEM)
    vmem = pl.BlockSpec(memory_space=pltpu.VMEM)
    return pl.pallas_call(
        weights_kernel,
        out_shape=jax.ShapeDtypeStruct((4, 4 * CS, 2 * CS), jnp.bfloat16),
        in_specs=[smem, smem, smem, vmem],
        out_specs=vmem,
        cost_estimate=pl.CostEstimate(flops=0, bytes_accessed=4 << 20, transcendentals=0),
        name="weights",
    )(role, jnp.asarray(index), jnp.asarray(scale), radial.reshape(20, CS, CS))


def turn_kernel(role_ref, field_ref, keep_ref, give_ref, keep_edge_ref, give_edge_ref):
    odd, plane = role_ref[0] % 2, pl.program_id(0)
    turned = jnp.transpose(field_ref[0])
    halves = [
        [turned[2 * HALF - ROW :], turned[:HALF], turned[HALF : HALF + ROW]],
        [turned[HALF - ROW : HALF], turned[HALF:], turned[:ROW]],
    ]
    for parity in range(2):

        @pl.when(odd == parity)
        def _():
            for ref, edge, half in ((keep_ref, keep_edge_ref, parity), (give_ref, give_edge_ref, 1 - parity)):
                for value, at in zip(halves[half], (0, ROW, ROW + HALF)):
                    ref[0, at : at + value.shape[0]] = value

                @pl.when(plane == 0)
                def _():
                    for value, at in zip(halves[half], (0, ROW, ROW + HALF)):
                        edge[at : at + value.shape[0]] = value


def turn(role, field):
    slab = jax.ShapeDtypeStruct((2, SLAB, CS), jnp.bfloat16)
    edge = jax.ShapeDtypeStruct((SLAB, CS), jnp.bfloat16)
    block = pl.BlockSpec((1, SLAB, CS), lambda p, role: (p, 0, 0))
    edge_block = pl.BlockSpec((SLAB, CS), lambda p, role: (0, 0))
    return pl.pallas_call(
        turn_kernel,
        out_shape=(slab, slab, edge, edge),
        grid_spec=pltpu.PrefetchScalarGridSpec(
            num_scalar_prefetch=1,
            grid=(2,),
            in_specs=[pl.BlockSpec((1, CS, 2 * HALF), lambda p, role: ((p + role[0]) % 2, 0, 0))],
            out_specs=(block, block, edge_block, edge_block),
        ),
        compiler_params=pltpu.CompilerParams(vmem_limit_bytes=32 << 20),
        cost_estimate=pl.CostEstimate(flops=0, bytes_accessed=6 << 20, transcendentals=0),
        name="turn",
    )(role, field)


def pair_chunk(start, triple, weight, sigma, tau, z_odd):
    def load(ref):
        return ref[start : start + CHUNK + 2 * ROW, :].astype(jnp.float32)

    below, here, above = triple
    if z_odd:
        sources = [load(above) - load(below)]
    else:
        sources = [load(here), load(above) + load(below)]
    features = []
    for source in sources:
        features.append(source[ROW : ROW + CHUNK].astype(jnp.bfloat16))
        features.append((source[2 * ROW :] + sigma * source[:CHUNK]).astype(jnp.bfloat16))
    total = jnp.dot(jnp.concatenate(features, axis=1), weight, preferred_element_type=jnp.float32)
    centre, side = total[:, :CS], total[:, CS:].reshape(CHUNK // ROW, ROW, CS)
    right = pltpu.roll(side, ROW - 1, 1).reshape(CHUNK, CS)
    left = pltpu.roll(side, 1, 1).reshape(CHUNK, CS)
    return centre + right + tau * left


def conv_kernel(jobs, stacks, n_accs, role_ref, weight_ref, *refs):
    role = role_ref[0]
    comp, odd = role // 2, role % 2
    gathered = comp ^ (1 + odd)
    reduced = comp ^ (2 - odd)
    pairs = [(comp, comp), (comp, reduced), (gathered, reduced), (gathered, comp)]
    planes = []
    for ref, stack in zip(refs, stacks):
        planes.append([ref] if stack == 0 else [ref.at[at] for at in range(stack)])
    accs = refs[len(stacks) : len(stacks) + n_accs]
    outs = refs[len(refs) - len(jobs) :]
    for (triple, slot, acc), out in zip(jobs, outs):
        i, o = pairs[slot]

        def differ(at):
            return (i == at).astype(jnp.int32) != (o == at).astype(jnp.int32)

        tau = jnp.where(differ(1), -1.0, 1.0)
        sigma = jnp.where(differ(2), -1.0, 1.0)
        three = [planes[at][index] for at, index in triple]

        def run(z_odd, rows):
            for start in range(0, HALF, CHUNK):
                value = pair_chunk(start, three, weight_ref[slot, :rows, :], sigma, tau, z_odd)
                if acc is not None:
                    value = value + accs[acc][start : start + CHUNK].astype(jnp.float32)
                out[start : start + CHUNK] = value.astype(out.dtype)

        odd_in_z = differ(3)

        @pl.when(odd_in_z)
        def _():
            run(True, 2 * CS)

        @pl.when(jnp.logical_not(odd_in_z))
        def _():
            run(False, 4 * CS)


def conv(name, role, weight, planes, accs, jobs, types, after=()):
    vmem = pl.BlockSpec(memory_space=pltpu.VMEM)
    flops = len(jobs) * 2 * 256 * 512 * HALF
    size = sum(a.size * a.dtype.itemsize for a in (*planes, *accs)) + len(jobs) * CS * HALF * 4
    stacks = [a.shape[0] if a.ndim == 3 else 0 for a in planes]
    return pl.pallas_call(
        functools.partial(conv_kernel, jobs, stacks, len(accs)),
        out_shape=tuple(jax.ShapeDtypeStruct((HALF, CS), t) for t in types),
        in_specs=[pl.BlockSpec(memory_space=pltpu.SMEM)]
        + [vmem] * (1 + len(planes) + len(accs))
        + [pl.BlockSpec(memory_space=pl.ANY)] * len(after),
        out_specs=tuple(vmem for _ in types),
        compiler_params=pltpu.CompilerParams(vmem_limit_bytes=40 << 20),
        cost_estimate=pl.CostEstimate(flops=flops, bytes_accessed=size, transcendentals=0),
        name=name,
    )(role, weight, *planes, *accs, *after)


def final_kernel(role_ref, *refs):
    own, others, out_ref = refs[:4], refs[4:7], refs[7]
    plane, side = pl.program_id(0), pl.program_id(1)

    def put(first, second):
        total = first.astype(jnp.float32) + second.astype(jnp.float32)
        out_ref[0] = jnp.transpose(total.astype(out_ref.dtype))

    for p in range(2):

        @pl.when((plane == p) & (side == 0))
        def _():
            put(own[p][...], own[2 + p][...])

        @pl.when((plane == p) & (side == 1))
        def _():
            put(others[0][p], others[1 + p][...])


def final(role, own, others):
    def at(plane, side, role):
        odd = role[0] % 2
        return ((plane + odd) % 2, 0, (side + odd) % 2)

    vmem = pl.BlockSpec(memory_space=pltpu.VMEM)
    return pl.pallas_call(
        final_kernel,
        out_shape=jax.ShapeDtypeStruct((2, CS, 2 * HALF), jnp.bfloat16),
        grid_spec=pltpu.PrefetchScalarGridSpec(
            num_scalar_prefetch=1,
            grid=(2, 2),
            in_specs=[vmem] * 7,
            out_specs=pl.BlockSpec((1, CS, HALF), at),
        ),
        compiler_params=pltpu.CompilerParams(vmem_limit_bytes=40 << 20),
        cost_estimate=pl.CostEstimate(flops=0, bytes_accessed=8 << 20, transcendentals=0),
        name="final",
    )(role, *own, *others)


def shards(tensor_field, radial):
    n_space, n_chan = lax.axis_size("space"), lax.axis_size("chan")
    sub = n_chan // 4
    chips = n_space // 2
    field = tensor_field
    if sub > 1:
        groups = [[g * sub + h for h in range(sub)] for g in range(4)]
        field = lax.all_gather(field, "chan", axis_index_groups=groups, axis=1, tiled=True)

    def permute(value, place):
        pairs = []
        for s in range(n_space):
            for c in range(4):
                to_s, to_c = place(s // 2, s % 2, c)
                for h in range(sub):
                    pairs.append((s * n_chan + c * sub + h, to_s * n_chan + to_c * sub + h))
        return lax.ppermute(value, ("space", "chan"), pairs)

    def outward(z, k):
        return (z + (1 if k else -1)) % chips

    def gather_group(k, c):
        return c ^ (2 if k else 1)

    def reduce_group(k, c):
        return c ^ (1 if k else 2)

    role = ((lax.axis_index("chan") // sub) * 2 + lax.axis_index("space") % 2).astype(jnp.int32).reshape(1)

    def reduce_near(value):
        return permute(value, lambda z, k, c: (2 * z + k, reduce_group(k, c)))

    def reduce_far(value):
        return permute(value, lambda z, k, c: (2 * z + 1 - k, reduce_group(k, c)))

    def swap(value):
        return permute(value, lambda z, k, c: (2 * z + 1 - k, c))

    keep, give, keep_edge, give_edge = turn(role, field)
    gather_near = permute(keep, lambda z, k, c: (2 * z + k, gather_group(k, c)))
    halo_near = permute(give_edge, lambda z, k, c: (2 * outward(z, k) + 1 - k, c))
    halo_far = permute(keep_edge, lambda z, k, c: (2 * outward(z, k) + k, c))
    gather_far = permute(give, lambda z, k, c: (2 * z + 1 - k, gather_group(1 - k, c)))
    other = swap(give)
    weight = weights(role, radial)

    f32, bf16 = jnp.float32, jnp.bfloat16
    inner = {1: (0, 0), 2: (0, 1), 4: (1, 0), 3: (1, 1)}

    def around(plane, where):
        return tuple(where[at] for at in (plane - 1, plane, plane + 1))

    kept2, kept3, lent2, lent3 = conv(
        "own_inner", role, weight, [keep, other], [],
        [(around(2, inner), 0, None), (around(3, inner), 0, None), (around(2, inner), 1, None), (around(3, inner), 1, None)],
        [f32] * 4,
    )
    halo_near, halo_far, lent2, lent3 = lax.optimization_barrier((halo_near, halo_far, lent2, lent3))
    halos = permute(jnp.stack([halo_near, halo_far]), lambda z, k, c: (2 * z + k, gather_group(k, c)))
    sent2, sent3 = conv(
        "sent_inner", role, weight, [gather_near, gather_far], [lent2, lent3],
        [(around(2, inner), 2, 0), (around(3, inner), 2, 1)], [bf16] * 2,
    )
    got_inner_near = reduce_near(sent2)
    got_inner_far = reduce_far(sent3)
    own_all = inner | {0: (2, 0), 5: (3, 0)}
    kept1, kept4, lent1, lent4 = conv(
        "own_boundary", role, weight, [keep, other, halo_near, halo_far], [],
        [(around(1, own_all), 0, None), (around(4, own_all), 0, None), (around(1, own_all), 1, None), (around(4, own_all), 1, None)],
        [f32] * 4, after=[sent2],
    )
    near_all = inner | {0: (2, 0), 5: (2, 1)}
    sent1, sent4 = conv(
        "sent_boundary", role, weight, [gather_near, gather_far, halos], [lent1, lent4],
        [(around(1, near_all), 2, 0), (around(4, near_all), 2, 1)], [bf16] * 2,
    )
    got_boundary_near = reduce_near(sent1)
    got_boundary_far = reduce_far(sent4)
    total4, total3 = conv(
        "kept_far", role, weight, [gather_near, gather_far, halos], [kept4, kept3],
        [(around(4, near_all), 3, 0), (around(3, near_all), 3, 1)], [bf16] * 2, after=[sent1],
    )
    crossed = swap(jnp.stack([total4, total3]))
    total1, total2 = conv(
        "kept_near", role, weight, [gather_near, gather_far, halos], [kept1, kept2],
        [(around(1, near_all), 3, 0), (around(2, near_all), 3, 1)], [f32] * 2, after=[total4],
    )
    out = final(
        role,
        [total1, total2, got_boundary_near, got_inner_near],
        [crossed, got_boundary_far, got_inner_far],
    )
    if sub > 1:
        out = lax.dynamic_slice_in_dim(out, lax.axis_index("chan") % sub * tensor_field.shape[1], tensor_field.shape[1], 1)
    return out


def solution(mesh):
    placed = (P("space", "chan", None), P())
    return jax.shard_map(
        shards, mesh=mesh, in_specs=placed, out_specs=P("space", "chan", None), check_vma=False
    )
```

time: 119 us -> 80.5 us (0.68)
  Pallas kernels: 62.6 us -> 22.7 us
  waiting for transfers between devices: 31.8 us -> 41.2 us
  local copies, waits for them, and re-layouts: 9.41 us -> 2.82 us
  starting transfers between devices: 14.8 us -> 13.1 us
    pallas_call x7 -> x8, Pallas kernels: 60.5 us -> 20.4 us  [the longest x6 15.2 us: conv(): pl.pallas_call(functools.partial(conv_kernel, jobs, stacks, len(accs)), o...]
    ppermute x11, waiting for transfers between devices: 31.8 us -> 41.2 us  [permute(): return lax.ppermute(value, ('space', 'chan'), pairs)]
    squeeze x7 -> x0, local copies, waits for them, and re-layouts: 6.07 us -> none  [the longest x2 2.6 us: shards(): own = [halo_near, keep[0], keep[1], other[1], other[0], halo_far]]
    ppermute x11, starting transfers between devices: 14.8 us -> 13.1 us  [permute(): return lax.ppermute(value, ('space', 'chan'), pairs)]
    unnamed x12 -> x4, local copies, waits for them, and re-layouts: 3.33 us -> 2.82 us
  transfers between devices with their start and end apart: 11 -> 11, of which waited for: 5 -> 7; matrix products, arithmetic and copies ran while one was open for 4% -> 0% of each run, Pallas kernels for 34% -> 18%
where the time goes in v2:
time: 80.5 us; the launch traced here: 80.2 us
  waiting for transfers between devices  41.2 us (51%)
  Pallas kernels  22.7 us (28%)
  starting transfers between devices  13.1 us (16%)
  local copies, waits for them, and re-layouts  2.82 us (4%)
    ppermute x11, waiting for transfers between devices, permute(): return lax.ppermute(value, ('space', 'chan'), pairs)  41.2 us
    pallas_call x6, Pallas kernels, conv(): pl.pallas_call(functools.partial(conv_kernel, jobs, stacks, len(accs)), o...  15.2 us
    ppermute x11, starting transfers between devices, permute(): return lax.ppermute(value, ('space', 'chan'), pairs)  13.1 us
    unnamed x4, local copies, waits for them, and re-layouts  2.82 us
    pallas_call x1, Pallas kernels, turn(): pl.pallas_call(turn_kernel, out_shape=(slab, slab, edge, edge), grid_spec...  2.7 us
    pallas_call x1, Pallas kernels, weights(): pl.pallas_call(weights_kernel, out_shape=jax.ShapeDtypeStruct((4, 4 * CS,...  2.51 us
    pallas_call x1, Pallas kernels, final(): pl.pallas_call(final_kernel, out_shape=jax.ShapeDtypeStruct((2, CS, 2 * H...  2.28 us
  transfers between devices with their start and end apart: 11, of which 7 were waited for; matrix products, arithmetic and copies ran while one was open for 0% of the time, Pallas kernels for 18%

profile of v2, /device:TPU:0, one launch (start us, length us, event | category | flops | bytes accessed | tf_op | source)
XLA Modules:
  0.0 80.2 jit_solution(14920357056733855438)
XLA Ops:
  0.0 0.0 copy-start.1
  0.0 1.6 %copy-done.1 = bf16[2,128,4096]{2,1,0:T(8,128)(2,1)S(1)} copy-done((bf16[2,128,4096]{2,1,0:T(8,128)(2,1)S(1)}, bf16[2,128,4096]{2,1,0:T(8,128)(2,1)}, u32[]{:S(2)}) %copy-start.1) | copy-done | bytes 2097176
  1.6 2.7 %turn.1 = (bf16[2,2176,128]{2,1,0:T(8,128)(2,1)}, bf16[2,2176,128]{2,1,0:T(8,128)(2,1)}, bf16[2176,128]{1,0:T(8,128)(2,1)}, bf16[2176,128]{1,0:T(8,128)(2,1)}) custom-call(s32[1]{0:T(128)} %bitcast.role_ref, bf16[2,128,4096]{2,1,0:T(8,128)(2,1)S(1)} %copy-done.1), custom_call_target="tpu_custom_call" | custom-call | bytes 6291456 | tf_op jit(solution)/shard_map/turn/pallas_call | solution.py:105
  4.3 0.4 collective-permute-start.4
  4.7 4.7 %collective-permute-start.2 = (bf16[2176,128]{1,0:T(8,128)(2,1)}, bf16[2176,128]{1,0:T(8,128)(2,1)S(1)}, u32[]{:S(2)}, u32[]{:S(2)}) collective-permute-start(bf16[2176,128]{1,0:T(8,128)(2,1)} %get-tuple-element.31), channel_id=1, source_target_pairs={{0,28},{1,29},{2,30},{3,31},{4,8},{5,9},{6,10},{7,11},{8,4},{9,5},... | collective-permute-start | bytes 1671176 | tf_op jit(solution)/shard_map/ppermute | solution.py:253
  9.5 0.4 collective-permute-start.3
  9.9 0.0 collective-permute-start.1
  9.9 1.5 %collective-permute-start = (bf16[2,2176,128]{2,1,0:T(8,128)(2,1)}, bf16[2,2176,128]{2,1,0:T(8,128)(2,1)S(1)}, u32[]{:S(2)}, u32[]{:S(2)}) collective-permute-start(bf16[2,2176,128]{2,1,0:T(8,128)(2,1)} %get-tuple-element.29.refs_0_), channel_id=1, source_target_pairs={{0,1},{1,0},{2,3},{3,2},{4,6},{5,7},{6,4},{7,5},{8,9},{9,8},{10,11... | collective-permute-start | bytes 3342344 | tf_op jit(solution)/shard_map/ppermute | solution.py:253
  11.4 2.5 %weights.1.weight_ref = bf16[4,512,256]{2,1,0:T(8,128)(2,1)} custom-call(s32[1]{0:T(128)} %bitcast.role_ref, s32[8,64]{1,0:T(8,128)} %constant.37.clone.index_ref, f32[8,64]{1,0:T(8,128)} %constant.38.clone.scale_ref, bf16[20,128,128]{2,1,0:T(8,128)(2,1)} %bitcast.10), custom_call_target="tpu_custom_call" | custom-call | bytes 4194304 | tf_op jit(solution)/shard_map/weights/pallas_call | solution.py:69
  13.9 0.0 collective-permute-done.4.refs_1_
  14.0 0.0 copy-start
  14.0 1.2 %copy-done = bf16[4,512,256]{2,1,0:T(8,128)(2,1)S(1)} copy-done((bf16[4,512,256]{2,1,0:T(8,128)(2,1)S(1)}, bf16[4,512,256]{2,1,0:T(8,128)(2,1)}, u32[]{:S(2)}) %copy-start) | copy-done | bytes 1048600
  15.2 4.3 %own_inner.1 = (f32[2048,128]{1,0:T(8,128)S(1)}, f32[2048,128]{1,0:T(8,128)S(1)}, f32[2048,128]{1,0:T(8,128)S(1)}, f32[2048,128]{1,0:T(8,128)S(1)}) custom-call(s32[1]{0:T(128)} %bitcast.role_ref, bf16[4,512,256]{2,1,0:T(8,128)(2,1)S(1)} %copy-done, bf16[2,2176,128]{2,1,0:T(8,128)(2,1)} %get-tuple-element.29.refs_0_, ...), custom_call_target="tpu_custom_call" | custom-call | flops 2147483648 | bytes 6422528 | tf_op jit(solution)/shard_map/own_inner/pallas_call | solution.py:184
  19.5 3.3 %collective-permute-done.2.refs_2_ = bf16[2176,128]{1,0:T(8,128)(2,1)S(1)} collective-permute-done((bf16[2176,128]{1,0:T(8,128)(2,1)}, bf16[2176,128]{1,0:T(8,128)(2,1)S(1)}, u32[]{:S(2)}, u32[]{:S(2)}) %collective-permute-start.2) | collective-permute-done | bytes 557088 | tf_op jit(solution)/shard_map/ppermute | solution.py:253
  22.9 9.3 %collective-permute-done.3.refs_3_ = bf16[2176,128]{1,0:T(8,128)(2,1)S(1)} collective-permute-done((bf16[2176,128]{1,0:T(8,128)(2,1)}, bf16[2176,128]{1,0:T(8,128)(2,1)S(1)}, u32[]{:S(2)}, u32[]{:S(2)}) %collective-permute-start.3) | collective-permute-done | bytes 557088 | tf_op jit(solution)/shard_map/ppermute | solution.py:253
  32.1 0.1 pad_maximum_fusion
  32.2 2.3 %collective-permute-start.5 = (bf16[2,2176,128]{2,1,0:T(8,128)(2,1)S(1)}, bf16[2,2176,128]{2,1,0:T(8,128)(2,1)S(1)}, u32[]{:S(2)}, u32[]{:S(2)}) collective-permute-start(bf16[2,2176,128]{2,1,0:T(8,128)(2,1)S(1)} %pad_maximum_fusion), channel_id=1, source_target_pairs={{0,1},{1,0},{2,3},{3,2},{4,6},{5,7},{6,4},{7,5},{8,9},{9,8},{10,11... | collective-permute-start | bytes 3342344 | tf_op jit(solution)/shard_map/ppermute | solution.py:253
  34.6 2.4 %collective-permute-done.refs_0_ = bf16[2,2176,128]{2,1,0:T(8,128)(2,1)S(1)} collective-permute-done((bf16[2,2176,128]{2,1,0:T(8,128)(2,1)}, bf16[2,2176,128]{2,1,0:T(8,128)(2,1)S(1)}, u32[]{:S(2)}, u32[]{:S(2)}) %collective-permute-start) | collective-permute-done | bytes 1114144 | tf_op jit(solution)/shard_map/ppermute | solution.py:253
  37.0 0.0 collective-permute-done.1.refs_1_
  37.0 1.6 %sent_inner.1 = (bf16[2048,128]{1,0:T(8,128)(2,1)S(1)}, bf16[2048,128]{1,0:T(8,128)(2,1)S(1)}) custom-call(s32[1]{0:T(128)} %bitcast.role_ref, bf16[4,512,256]{2,1,0:T(8,128)(2,1)S(1)} %copy-done, bf16[2,2176,128]{2,1,0:T(8,128)(2,1)S(1)} %collective-permute-done.refs_0_, bf16[2,2176,128]{2,1,0:T(8,128)(2,1)S(1)} %collective-permute-done.1.refs_1_, ...), custom_call_target="tpu_custom_call" | custom-call | flops 1073741824 | bytes 6422528 | tf_op jit(solution)/shard_map/sent_inner/pallas_call | solution.py:184
  38.6 4.5 %own_boundary.1 = (f32[2048,128]{1,0:T(8,128)S(1)}, f32[2048,128]{1,0:T(8,128)S(1)}, f32[2048,128]{1,0:T(8,128)S(1)}, f32[2048,128]{1,0:T(8,128)S(1)}) custom-call(s32[1]{0:T(128)} %bitcast.role_ref, bf16[4,512,256]{2,1,0:T(8,128)(2,1)S(1)} %copy-done, bf16[2,2176,128]{2,1,0:T(8,128)(2,1)} %get-tuple-element.29.refs_0_, ...), custom_call_target="tpu_custom_call" | custom-call | flops 2147483648 | bytes 7536640 | tf_op jit(solution)/shard_map/own_boundary/pallas_call | solution.py:184
  43.1 5.8 %collective-permute-done.5.refs_2_ = bf16[2,2176,128]{2,1,0:T(8,128)(2,1)S(1)} collective-permute-done((bf16[2,2176,128]{2,1,0:T(8,128)(2,1)S(1)}, bf16[2,2176,128]{2,1,0:T(8,128)(2,1)S(1)}, u32[]{:S(2)}, u32[]{:S(2)}) %collective-permute-start.5) | collective-permute-done | bytes 1114144 | tf_op jit(solution)/shard_map/ppermute | solution.py:253
  48.9 1.6 %sent_boundary.1 = (bf16[2048,128]{1,0:T(8,128)(2,1)S(1)}, bf16[2048,128]{1,0:T(8,128)(2,1)S(1)}) custom-call(s32[1]{0:T(128)} %bitcast.role_ref, bf16[4,512,256]{2,1,0:T(8,128)(2,1)S(1)} %copy-done, bf16[2,2176,128]{2,1,0:T(8,128)(2,1)S(1)} %collective-permute-done.refs_0_, bf16[2,2176,128]{2,1,0:T(8,128)(2,1)S(1)} %collective-permute-done.1.refs_1_, ...), custom_call_target="tpu_custom_call" | custom-call | flops 1073741824 | bytes 7536640 | tf_op jit(solution)/shard_map/sent_boundary/pallas_call | solution.py:184
  50.5 1.6 %kept_far.1 = (bf16[2048,128]{1,0:T(8,128)(2,1)S(1)}, bf16[2048,128]{1,0:T(8,128)(2,1)S(1)}) custom-call(s32[1]{0:T(128)} %bitcast.role_ref, bf16[4,512,256]{2,1,0:T(8,128)(2,1)S(1)} %copy-done, bf16[2,2176,128]{2,1,0:T(8,128)(2,1)S(1)} %collective-permute-done.refs_0_, bf16[2,2176,128]{2,1,0:T(8,128)(2,1)S(1)} %collective-permute-done.1.refs_1_, ...), custom_call_target="tpu_custom_call" | custom-call | flops 1073741824 | bytes 7536640 | tf_op jit(solution)/shard_map/kept_far/pallas_call | solution.py:184
  52.2 0.1 pad_maximum_fusion.1
  52.3 0.2 collective-permute-start.8
  52.4 0.8 %collective-permute-start.7 = (bf16[2048,128]{1,0:T(8,128)(2,1)S(1)}, bf16[2048,128]{1,0:T(8,128)(2,1)S(1)}, u32[]{:S(2)}, u32[]{:S(2)}) collective-permute-start(bf16[2048,128]{1,0:T(8,128)(2,1)S(1)} %get-tuple-element.39.refs_4_), channel_id=1, source_target_pairs={{0,2},{1,3},{2,0},{3,1},{4,5},{5,4},{6,7},{7,6},{8,10},{9,11},{10,... | collective-permute-start | bytes 1572872 | tf_op jit(solution)/shard_map/ppermute | solution.py:253
  53.3 1.5 %collective-permute-start.10 = (bf16[2048,128]{1,0:T(8,128)(2,1)S(1)}, bf16[2048,128]{1,0:T(8,128)(2,1)S(1)}, u32[]{:S(2)}, u32[]{:S(2)}) collective-permute-start(bf16[2048,128]{1,0:T(8,128)(2,1)S(1)} %get-tuple-element.52), channel_id=1, source_target_pairs={{0,6},{1,7},{2,4},{3,5},{4,1},{5,0},{6,3},{7,2},{8,14},{9,15},{10,... | collective-permute-start | bytes 1572872 | tf_op jit(solution)/shard_map/ppermute | solution.py:253
  54.8 0.5 collective-permute-start.6
  55.3 0.6 collective-permute-start.9
  55.9 1.6 %kept_near.1 = (f32[2048,128]{1,0:T(8,128)S(1)}, f32[2048,128]{1,0:T(8,128)S(1)}) custom-call(s32[1]{0:T(128)} %bitcast.role_ref, bf16[4,512,256]{2,1,0:T(8,128)(2,1)S(1)} %copy-done, bf16[2,2176,128]{2,1,0:T(8,128)(2,1)S(1)} %collective-permute-done.refs_0_, bf16[2,2176,128]{2,1,0:T(8,128)(2,1)S(1)} %collective-permute-done.1.refs_1_, ...), custom_call_target="tpu_custom_call" | custom-call | flops 1073741824 | bytes 7536640 | tf_op jit(solution)/shard_map/kept_near/pallas_call | solution.py:184
  57.5 9.2 %collective-permute-done.10.refs_6_ = bf16[2048,128]{1,0:T(8,128)(2,1)S(1)} collective-permute-done((bf16[2048,128]{1,0:T(8,128)(2,1)S(1)}, bf16[2048,128]{1,0:T(8,128)(2,1)S(1)}, u32[]{:S(2)}, u32[]{:S(2)}) %collective-permute-start.10) | collective-permute-done | bytes 524320 | tf_op jit(solution)/shard_map/ppermute | solution.py:253
  66.7 0.0 collective-permute-done.7.refs_3_
  66.7 6.2 %collective-permute-done.6.refs_2_ = bf16[2048,128]{1,0:T(8,128)(2,1)S(1)} collective-permute-done((bf16[2048,128]{1,0:T(8,128)(2,1)S(1)}, bf16[2048,128]{1,0:T(8,128)(2,1)S(1)}, u32[]{:S(2)}, u32[]{:S(2)}) %collective-permute-start.6) | collective-permute-done | bytes 524320 | tf_op jit(solution)/shard_map/ppermute | solution.py:253
  72.9 5.0 %collective-permute-done.9.refs_5_ = bf16[2048,128]{1,0:T(8,128)(2,1)S(1)} collective-permute-done((bf16[2048,128]{1,0:T(8,128)(2,1)S(1)}, bf16[2048,128]{1,0:T(8,128)(2,1)S(1)}, u32[]{:S(2)}, u32[]{:S(2)}) %collective-permute-start.9) | collective-permute-done | bytes 524320 | tf_op jit(solution)/shard_map/ppermute | solution.py:253
  77.9 0.0 collective-permute-done.8.refs_4_
  77.9 2.3 %final.1 = bf16[2,128,4096]{2,1,0:T(8,128)(2,1)} custom-call(s32[1]{0:T(128)} %bitcast.role_ref, f32[2048,128]{1,0:T(8,128)S(1)} %get-tuple-element.48.refs_0_, f32[2048,128]{1,0:T(8,128)S(1)} %get-tuple-element.49.refs_1_, bf16[2048,128]{1,0:T(8,128)(2,1)S(1)} %collective-permute-done.6.refs_2_, bf16[2048,128]{1,0:T(8,128)(2,1)S(1)} %collective-permute-done.7.refs_3_, ...), custom_call_target="tpu_custom_call" | custom-call | bytes 8388608 | tf_op jit(solution)/shard_map/final/pallas_call | solution.py:222
Async XLA Ops:
  0.0 1.6 %copy-start.1 = (bf16[2,128,4096]{2,1,0:T(8,128)(2,1)S(1)}, bf16[2,128,4096]{2,1,0:T(8,128)(2,1)}, u32[]{:S(2)}) copy-start(bf16[2,128,4096]{2,1,0:T(8,128)(2,1)} %field_ref.1) | copy-start | bytes 6291460
  4.3 9.7 %collective-permute-start.4 = (bf16[2,2176,128]{2,1,0:T(8,128)(2,1)}, bf16[2,2176,128]{2,1,0:T(8,128)(2,1)}, u32[]{:S(2)}, u32[]{:S(2)}) collective-permute-start(bf16[2,2176,128]{2,1,0:T(8,128)(2,1)} %get-tuple-element.30), channel_id=1, source_target_pairs={{0,4},{1,5},{2,6},{3,7},{4,0},{5,1},{6,2},{7,3},{8,12},{9,13},{10,... | collective-permute-start | bytes 3342344 | tf_op jit(solution)/shard_map/ppermute | solution.py:253
  4.7 18.1 %collective-permute-start.2 = (bf16[2176,128]{1,0:T(8,128)(2,1)}, bf16[2176,128]{1,0:T(8,128)(2,1)S(1)}, u32[]{:S(2)}, u32[]{:S(2)}) collective-permute-start(bf16[2176,128]{1,0:T(8,128)(2,1)} %get-tuple-element.31), channel_id=1, source_target_pairs={{0,28},{1,29},{2,30},{3,31},{4,8},{5,9},{6,10},{7,11},{8,4},{9,5},... | collective-permute-start | bytes 1671176 | tf_op jit(solution)/shard_map/ppermute | solution.py:253
  9.5 22.7 %collective-permute-start.3 = (bf16[2176,128]{1,0:T(8,128)(2,1)}, bf16[2176,128]{1,0:T(8,128)(2,1)S(1)}, u32[]{:S(2)}, u32[]{:S(2)}) collective-permute-start(bf16[2176,128]{1,0:T(8,128)(2,1)} %get-tuple-element.32), channel_id=1, source_target_pairs={{0,24},{1,25},{2,26},{3,27},{4,12},{5,13},{6,14},{7,15},{8,0},{9,1... | collective-permute-start | bytes 1671176 | tf_op jit(solution)/shard_map/ppermute | solution.py:253
  9.9 27.1 %collective-permute-start.1 = (bf16[2,2176,128]{2,1,0:T(8,128)(2,1)}, bf16[2,2176,128]{2,1,0:T(8,128)(2,1)S(1)}, u32[]{:S(2)}, u32[]{:S(2)}) collective-permute-start(bf16[2,2176,128]{2,1,0:T(8,128)(2,1)} %get-tuple-element.30), channel_id=1, source_target_pairs={{0,6},{1,7},{2,4},{3,5},{4,1},{5,0},{6,3},{7,2},{8,14},{9,15},{10,... | collective-permute-start | bytes 3342344 | tf_op jit(solution)/shard_map/ppermute | solution.py:253
  9.9 27.1 %collective-permute-start = (bf16[2,2176,128]{2,1,0:T(8,128)(2,1)}, bf16[2,2176,128]{2,1,0:T(8,128)(2,1)S(1)}, u32[]{:S(2)}, u32[]{:S(2)}) collective-permute-start(bf16[2,2176,128]{2,1,0:T(8,128)(2,1)} %get-tuple-element.29.refs_0_), channel_id=1, source_target_pairs={{0,1},{1,0},{2,3},{3,2},{4,6},{5,7},{6,4},{7,5},{8,9},{9,8},{10,11... | collective-permute-start | bytes 3342344 | tf_op jit(solution)/shard_map/ppermute | solution.py:253
  14.0 1.2 %copy-start = (bf16[4,512,256]{2,1,0:T(8,128)(2,1)S(1)}, bf16[4,512,256]{2,1,0:T(8,128)(2,1)}, u32[]{:S(2)}) copy-start(bf16[4,512,256]{2,1,0:T(8,128)(2,1)} %weights.1.weight_ref) | copy-start | bytes 3145732
  32.2 16.7 %collective-permute-start.5 = (bf16[2,2176,128]{2,1,0:T(8,128)(2,1)S(1)}, bf16[2,2176,128]{2,1,0:T(8,128)(2,1)S(1)}, u32[]{:S(2)}, u32[]{:S(2)}) collective-permute-start(bf16[2,2176,128]{2,1,0:T(8,128)(2,1)S(1)} %pad_maximum_fusion), channel_id=1, source_target_pairs={{0,1},{1,0},{2,3},{3,2},{4,6},{5,7},{6,4},{7,5},{8,9},{9,8},{10,11... | collective-permute-start | bytes 3342344 | tf_op jit(solution)/shard_map/ppermute | solution.py:253
  52.3 25.6 %collective-permute-start.8 = (bf16[2,2048,128]{2,1,0:T(8,128)(2,1)S(1)}, bf16[2,2048,128]{2,1,0:T(8,128)(2,1)S(1)}, u32[]{:S(2)}, u32[]{:S(2)}) collective-permute-start(bf16[2,2048,128]{2,1,0:T(8,128)(2,1)S(1)} %pad_maximum_fusion.1), channel_id=1, source_target_pairs={{0,4},{1,5},{2,6},{3,7},{4,0},{5,1},{6,2},{7,3},{8,12},{9,13},{10,... | collective-permute-start | bytes 3145736 | tf_op jit(solution)/shard_map/ppermute | solution.py:253
  52.4 14.2 %collective-permute-start.7 = (bf16[2048,128]{1,0:T(8,128)(2,1)S(1)}, bf16[2048,128]{1,0:T(8,128)(2,1)S(1)}, u32[]{:S(2)}, u32[]{:S(2)}) collective-permute-start(bf16[2048,128]{1,0:T(8,128)(2,1)S(1)} %get-tuple-element.39.refs_4_), channel_id=1, source_target_pairs={{0,2},{1,3},{2,0},{3,1},{4,5},{5,4},{6,7},{7,6},{8,10},{9,11},{10,... | collective-permute-start | bytes 1572872 | tf_op jit(solution)/shard_map/ppermute | solution.py:253
  53.3 13.4 %collective-permute-start.10 = (bf16[2048,128]{1,0:T(8,128)(2,1)S(1)}, bf16[2048,128]{1,0:T(8,128)(2,1)S(1)}, u32[]{:S(2)}, u32[]{:S(2)}) collective-permute-start(bf16[2048,128]{1,0:T(8,128)(2,1)S(1)} %get-tuple-element.52), channel_id=1, source_target_pairs={{0,6},{1,7},{2,4},{3,5},{4,1},{5,0},{6,3},{7,2},{8,14},{9,15},{10,... | collective-permute-start | bytes 1572872 | tf_op jit(solution)/shard_map/ppermute | solution.py:253
  54.8 18.1 %collective-permute-start.6 = (bf16[2048,128]{1,0:T(8,128)(2,1)S(1)}, bf16[2048,128]{1,0:T(8,128)(2,1)S(1)}, u32[]{:S(2)}, u32[]{:S(2)}) collective-permute-start(bf16[2048,128]{1,0:T(8,128)(2,1)S(1)} %get-tuple-element.46.refs_5_), channel_id=1, source_target_pairs={{0,2},{1,3},{2,0},{3,1},{4,5},{5,4},{6,7},{7,6},{8,10},{9,11},{10,... | collective-permute-start | bytes 1572872 | tf_op jit(solution)/shard_map/ppermute | solution.py:253
  55.3 22.6 %collective-permute-start.9 = (bf16[2048,128]{1,0:T(8,128)(2,1)S(1)}, bf16[2048,128]{1,0:T(8,128)(2,1)S(1)}, u32[]{:S(2)}, u32[]{:S(2)}) collective-permute-start(bf16[2048,128]{1,0:T(8,128)(2,1)S(1)} %get-tuple-element.51), channel_id=1, source_target_pairs={{0,6},{1,7},{2,4},{3,5},{4,1},{5,0},{6,3},{7,2},{8,14},{9,15},{10,... | collective-permute-start | bytes 1572872 | tf_op jit(solution)/shard_map/ppermute | solution.py:253

commit v3 on v2

--- a/solution.py
+++ b/solution.py
@@ -15,6 +15,7 @@
 ROW = 64
 SLAB = HALF + 2 * ROW
 CHUNK = 512
+TURN_VMEM = 60 << 20
 
 
 def weight_tables():
@@ -76,42 +77,47 @@
     )(role, jnp.asarray(index), jnp.asarray(scale), radial.reshape(20, CS, CS))
 
 
-def turn_kernel(role_ref, field_ref, keep_ref, give_ref, keep_edge_ref, give_edge_ref):
+def turn_kernel(role_ref, field_ref, keep_edge_ref, keep_inner_ref, give_ref, give_edge_ref):
     odd, plane = role_ref[0] % 2, pl.program_id(0)
     turned = jnp.transpose(field_ref[0])
     halves = [
         [turned[2 * HALF - ROW :], turned[:HALF], turned[HALF : HALF + ROW]],
         [turned[HALF - ROW : HALF], turned[HALF:], turned[:ROW]],
     ]
+
+    def put(ref, half):
+        for value, at in zip(halves[half], (0, ROW, ROW + HALF)):
+            ref[at : at + value.shape[0]] = value
+
     for parity in range(2):
 
         @pl.when(odd == parity)
         def _():
-            for ref, edge, half in ((keep_ref, keep_edge_ref, parity), (give_ref, give_edge_ref, 1 - parity)):
-                for value, at in zip(halves[half], (0, ROW, ROW + HALF)):
-                    ref[0, at : at + value.shape[0]] = value
-
-                @pl.when(plane == 0)
-                def _():
-                    for value, at in zip(halves[half], (0, ROW, ROW + HALF)):
-                        edge[at : at + value.shape[0]] = value
+            put(give_ref.at[0], 1 - parity)
+
+            @pl.when(plane == 0)
+            def _():
+                put(keep_edge_ref, parity)
+                put(give_edge_ref, 1 - parity)
+
+            @pl.when(plane == 1)
+            def _():
+                put(keep_inner_ref, parity)
 
 
 def turn(role, field):
-    slab = jax.ShapeDtypeStruct((2, SLAB, CS), jnp.bfloat16)
-    edge = jax.ShapeDtypeStruct((SLAB, CS), jnp.bfloat16)
-    block = pl.BlockSpec((1, SLAB, CS), lambda p, role: (p, 0, 0))
-    edge_block = pl.BlockSpec((SLAB, CS), lambda p, role: (0, 0))
+    single = jax.ShapeDtypeStruct((SLAB, CS), jnp.bfloat16)
+    single_block = pl.BlockSpec((SLAB, CS), lambda p, role: (0, 0))
     return pl.pallas_call(
         turn_kernel,
-        out_shape=(slab, slab, edge, edge),
+        out_shape=(single, single, jax.ShapeDtypeStruct((2, SLAB, CS), jnp.bfloat16), single),
         grid_spec=pltpu.PrefetchScalarGridSpec(
             num_scalar_prefetch=1,
             grid=(2,),
             in_specs=[pl.BlockSpec((1, CS, 2 * HALF), lambda p, role: ((p + role[0]) % 2, 0, 0))],
-            out_specs=(block, block, edge_block, edge_block),
+            out_specs=(single_block, single_block, pl.BlockSpec((1, SLAB, CS), lambda p, role: (p, 0, 0)), single_block),
         ),
-        compiler_params=pltpu.CompilerParams(vmem_limit_bytes=32 << 20),
+        compiler_params=pltpu.CompilerParams(vmem_limit_bytes=TURN_VMEM),
         cost_estimate=pl.CostEstimate(flops=0, bytes_accessed=6 << 20, transcendentals=0),
         name="turn",
     )(role, field)
@@ -195,7 +201,7 @@
 
 
 def final_kernel(role_ref, *refs):
-    own, others, out_ref = refs[:4], refs[4:7], refs[7]
+    own, others, out_ref = refs[:4], refs[4:8], refs[8]
     plane, side = pl.program_id(0), pl.program_id(1)
 
     def put(first, second):
@@ -210,7 +216,7 @@
 
         @pl.when((plane == p) & (side == 1))
         def _():
-            put(others[0][p], others[1 + p][...])
+            put(others[p][...], others[2 + p][...])
 
 
 def final(role, own, others):
@@ -225,7 +231,7 @@
         grid_spec=pltpu.PrefetchScalarGridSpec(
             num_scalar_prefetch=1,
             grid=(2, 2),
-            in_specs=[vmem] * 7,
+            in_specs=[vmem] * 8,
             out_specs=pl.BlockSpec((1, CS, HALF), at),
         ),
         compiler_params=pltpu.CompilerParams(vmem_limit_bytes=40 << 20),
@@ -272,60 +278,59 @@
     def swap(value):
         return permute(value, lambda z, k, c: (2 * z + 1 - k, c))
 
-    keep, give, keep_edge, give_edge = turn(role, field)
-    gather_near = permute(keep, lambda z, k, c: (2 * z + k, gather_group(k, c)))
+    def gather_near(value):
+        return permute(value, lambda z, k, c: (2 * z + k, gather_group(k, c)))
+
+    def from_far(value):
+        return permute(value, lambda z, k, c: (2 * outward(z, k) + k, c))
+
+    f32, bf16 = jnp.float32, jnp.bfloat16
+    keep_edge, keep_inner, give, give_edge = turn(role, field)
+    near_edge = gather_near(keep_edge)
     halo_near = permute(give_edge, lambda z, k, c: (2 * outward(z, k) + 1 - k, c))
-    halo_far = permute(keep_edge, lambda z, k, c: (2 * outward(z, k) + k, c))
-    gather_far = permute(give, lambda z, k, c: (2 * z + 1 - k, gather_group(1 - k, c)))
-    other = swap(give)
+    halo_far = from_far(keep_edge)
+    near_inner = gather_near(keep_inner)
+    near_others = permute(give, lambda z, k, c: (2 * z + 1 - k, gather_group(1 - k, c)))
+    others = swap(give)
     weight = weights(role, radial)
 
-    f32, bf16 = jnp.float32, jnp.bfloat16
-    inner = {1: (0, 0), 2: (0, 1), 4: (1, 0), 3: (1, 1)}
-
-    def around(plane, where):
-        return tuple(where[at] for at in (plane - 1, plane, plane + 1))
-
+    inner = {1: (0, 0), 2: (1, 0), 4: (2, 0), 3: (2, 1)}
+    all_planes = inner | {0: (3, 0), 5: (4, 0)}
+
+    def jobs(of, *wanted):
+        return [(tuple(of[at] for at in (plane - 1, plane, plane + 1)), slot, acc) for plane, slot, acc in wanted]
+
+    own = [keep_edge, keep_inner, others]
     kept2, kept3, lent2, lent3 = conv(
-        "own_inner", role, weight, [keep, other], [],
-        [(around(2, inner), 0, None), (around(3, inner), 0, None), (around(2, inner), 1, None), (around(3, inner), 1, None)],
-        [f32] * 4,
-    )
-    halo_near, halo_far, lent2, lent3 = lax.optimization_barrier((halo_near, halo_far, lent2, lent3))
-    halos = permute(jnp.stack([halo_near, halo_far]), lambda z, k, c: (2 * z + k, gather_group(k, c)))
+        "own_inner", role, weight, own, [],
+        jobs(inner, (2, 0, None), (3, 0, None), (2, 1, None), (3, 1, None)), [f32] * 4,
+    )
+    far_halo = from_far(near_edge)
+    near_halo = gather_near(halo_near)
+    near = [near_edge, near_inner, near_others]
     sent2, sent3 = conv(
-        "sent_inner", role, weight, [gather_near, gather_far], [lent2, lent3],
-        [(around(2, inner), 2, 0), (around(3, inner), 2, 1)], [bf16] * 2,
-    )
-    got_inner_near = reduce_near(sent2)
-    got_inner_far = reduce_far(sent3)
-    own_all = inner | {0: (2, 0), 5: (3, 0)}
+        "sent_inner", role, weight, near, [lent2, lent3], jobs(inner, (2, 2, 0), (3, 2, 1)), [bf16] * 2,
+    )
+    got2, got3 = reduce_near(sent2), reduce_far(sent3)
     kept1, kept4, lent1, lent4 = conv(
-        "own_boundary", role, weight, [keep, other, halo_near, halo_far], [],
-        [(around(1, own_all), 0, None), (around(4, own_all), 0, None), (around(1, own_all), 1, None), (around(4, own_all), 1, None)],
-        [f32] * 4, after=[sent2],
-    )
-    near_all = inner | {0: (2, 0), 5: (2, 1)}
-    sent1, sent4 = conv(
-        "sent_boundary", role, weight, [gather_near, gather_far, halos], [lent1, lent4],
-        [(around(1, near_all), 2, 0), (around(4, near_all), 2, 1)], [bf16] * 2,
-    )
-    got_boundary_near = reduce_near(sent1)
-    got_boundary_far = reduce_far(sent4)
-    total4, total3 = conv(
-        "kept_far", role, weight, [gather_near, gather_far, halos], [kept4, kept3],
-        [(around(4, near_all), 3, 0), (around(3, near_all), 3, 1)], [bf16] * 2, after=[sent1],
-    )
-    crossed = swap(jnp.stack([total4, total3]))
-    total1, total2 = conv(
-        "kept_near", role, weight, [gather_near, gather_far, halos], [kept1, kept2],
-        [(around(1, near_all), 3, 0), (around(2, near_all), 3, 1)], [f32] * 2, after=[total4],
-    )
-    out = final(
-        role,
-        [total1, total2, got_boundary_near, got_inner_near],
-        [crossed, got_boundary_far, got_inner_far],
-    )
+        "own_boundary", role, weight, [*own, halo_near, halo_far], [],
+        jobs(all_planes, (1, 0, None), (4, 0, None), (1, 1, None), (4, 1, None)), [f32] * 4, after=[sent2],
+    )
+    total2, total3 = conv(
+        "kept_inner", role, weight, near, [kept2, kept3], jobs(inner, (2, 3, 0), (3, 3, 1)), [f32, bf16], after=[sent2],
+    )
+    crossed3 = swap(total3)
+    near = [*near, near_halo, far_halo]
+    sent1, sent4, total4 = conv(
+        "sent_boundary", role, weight, near, [lent1, lent4, kept4],
+        jobs(all_planes, (1, 2, 0), (4, 2, 1), (4, 3, 2)), [bf16] * 3, after=[total2],
+    )
+    got1, got4 = reduce_near(sent1), reduce_far(sent4)
+    crossed4 = swap(total4)
+    total1, = conv(
+        "kept_boundary", role, weight, near, [kept1], jobs(all_planes, (1, 3, 0)), [f32], after=[sent1, got2, got3],
+    )
+    out = final(role, [total1, total2, got1, got2], [crossed4, crossed3, got4, got3])
     if sub > 1:
         out = lax.dynamic_slice_in_dim(out, lax.axis_index("chan") % sub * tensor_field.shape[1], tensor_field.shape[1], 1)
     return out

time: 80.5 us -> 69.6 us (0.86)
  the two profiles are of different devices: /device:TPU:0 before, /device:TPU:1 now
where the time goes in v3:
time: 69.6 us; the launch traced here: 69.3 us
  waiting for transfers between devices  25.8 us (37%)
  Pallas kernels  22.2 us (32%)
  starting transfers between devices  17.9 us (26%)
  local copies, waits for them, and re-layouts  3.33 us (5%)
    ppermute x14, waiting for transfers between devices, permute(): return lax.ppermute(value, ('space', 'chan'), pairs)  25.8 us
    ppermute x14, starting transfers between devices, permute(): return lax.ppermute(value, ('space', 'chan'), pairs)  17.9 us
    pallas_call x6, Pallas kernels, conv(): pl.pallas_call(functools.partial(conv_kernel, jobs, stacks, len(accs)), o...  13.6 us
    pallas_call x1, Pallas kernels, turn(): pl.pallas_call(turn_kernel, out_shape=(single, single, jax.ShapeDtypeStru...  3.75 us
    unnamed x8, local copies, waits for them, and re-layouts  3.33 us
    pallas_call x1, Pallas kernels, weights(): pl.pallas_call(weights_kernel, out_shape=jax.ShapeDtypeStruct((4, 4 * CS,...  2.51 us
    pallas_call x1, Pallas kernels, final(): pl.pallas_call(final_kernel, out_shape=jax.ShapeDtypeStruct((2, CS, 2 * H...  2.27 us
  transfers between devices with their start and end apart: 14, of which 4 were waited for; matrix products, arithmetic and copies ran while one was open for 0% of the time, Pallas kernels for 23%

profile of v3, /device:TPU:1, one launch (start us, length us, event | category | flops | bytes accessed | tf_op | source)
XLA Modules:
  0.0 69.3 jit_solution(8289920447292249507)
XLA Ops:
  0.0 3.8 %turn.1 = (bf16[2176,128]{1,0:T(8,128)(2,1)}, bf16[2176,128]{1,0:T(8,128)(2,1)}, bf16[2,2176,128]{2,1,0:T(8,128)(2,1)}, bf16[2176,128]{1,0:T(8,128)(2,1)}) custom-call(s32[1]{0:T(128)} %bitcast.role_ref, bf16[2,128,4096]{2,1,0:T(8,128)(2,1)} %field_ref.1), custom_call_target="tpu_custom_call" | custom-call | bytes 6291456 | tf_op jit(solution)/shard_map/turn/pallas_call | solution.py:111
  3.8 0.1 collective-permute-start.6
  3.8 2.6 %collective-permute-start.2 = (bf16[2,2176,128]{2,1,0:T(8,128)(2,1)}, bf16[2,2176,128]{2,1,0:T(8,128)(2,1)S(1)}, u32[]{:S(2)}, u32[]{:S(2)}) collective-permute-start(bf16[2,2176,128]{2,1,0:T(8,128)(2,1)} %get-tuple-element.26), channel_id=1, source_target_pairs={{0,6},{1,7},{2,4},{3,5},{4,1},{5,0},{6,3},{7,2},{8,14},{9,15},{10,... | collective-permute-start | bytes 3342344 | tf_op jit(solution)/shard_map/ppermute | solution.py:259
  6.4 1.2 %collective-permute-start = (bf16[2176,128]{1,0:T(8,128)(2,1)}, bf16[2176,128]{1,0:T(8,128)(2,1)S(1)}, u32[]{:S(2)}, u32[]{:S(2)}) collective-permute-start(bf16[2176,128]{1,0:T(8,128)(2,1)} %get-tuple-element.24.refs_0_), channel_id=1, source_target_pairs={{0,1},{1,0},{2,3},{3,2},{4,6},{5,7},{6,4},{7,5},{8,9},{9,8},{10,11... | collective-permute-start | bytes 1671176 | tf_op jit(solution)/shard_map/ppermute | solution.py:259
  7.6 1.9 %collective-permute-start.3 = (bf16[2176,128]{1,0:T(8,128)(2,1)}, bf16[2176,128]{1,0:T(8,128)(2,1)}, u32[]{:S(2)}, u32[]{:S(2)}) collective-permute-start(bf16[2176,128]{1,0:T(8,128)(2,1)} %get-tuple-element.27), channel_id=1, source_target_pairs={{0,28},{1,29},{2,30},{3,31},{4,8},{5,9},{6,10},{7,11},{8,4},{9,5},... | collective-permute-start | bytes 1671176 | tf_op jit(solution)/shard_map/ppermute | solution.py:259
  9.6 0.2 collective-permute-start.1
  9.8 11.6 %collective-permute-done.refs_0_ = bf16[2176,128]{1,0:T(8,128)(2,1)S(1)} collective-permute-done((bf16[2176,128]{1,0:T(8,128)(2,1)}, bf16[2176,128]{1,0:T(8,128)(2,1)S(1)}, u32[]{:S(2)}, u32[]{:S(2)}) %collective-permute-start) | collective-permute-done | bytes 557088 | tf_op jit(solution)/shard_map/ppermute | solution.py:259
  21.4 1.1 %collective-permute-start.7 = (bf16[2176,128]{1,0:T(8,128)(2,1)}, bf16[2176,128]{1,0:T(8,128)(2,1)}, u32[]{:S(2)}, u32[]{:S(2)}) collective-permute-start(bf16[2176,128]{1,0:T(8,128)(2,1)} %get-tuple-element.24.refs_0_), channel_id=1, source_target_pairs={{0,24},{1,25},{2,26},{3,27},{4,12},{5,13},{6,14},{7,15},{8,0},{9,1... | collective-permute-start | bytes 1671176 | tf_op jit(solution)/shard_map/ppermute | solution.py:259
  22.5 2.5 %weights.1.weight_ref = bf16[4,512,256]{2,1,0:T(8,128)(2,1)} custom-call(s32[1]{0:T(128)} %bitcast.role_ref, s32[8,64]{1,0:T(8,128)} %constant.37.clone.index_ref, f32[8,64]{1,0:T(8,128)} %constant.38.clone.scale_ref, bf16[20,128,128]{2,1,0:T(8,128)(2,1)} %bitcast.2), custom_call_target="tpu_custom_call" | custom-call | bytes 4194304 | tf_op jit(solution)/shard_map/weights/pallas_call | solution.py:70
  25.0 0.0 collective-permute-done.3.refs_3_
  25.0 1.2 %collective-permute-start.4 = (bf16[2176,128]{1,0:T(8,128)(2,1)}, bf16[2176,128]{1,0:T(8,128)(2,1)S(1)}, u32[]{:S(2)}, u32[]{:S(2)}) collective-permute-start(bf16[2176,128]{1,0:T(8,128)(2,1)} %collective-permute-done.3.refs_3_), channel_id=1, source_target_pairs={{0,1},{1,0},{2,3},{3,2},{4,6},{5,7},{6,4},{7,5},{8,9},{9,8},{10,11... | collective-permute-start | bytes 1671176 | tf_op jit(solution)/shard_map/ppermute | solution.py:259
  26.3 0.0 collective-permute-done.6.refs_2_
  26.3 1.4 %collective-permute-start.5 = (bf16[2176,128]{1,0:T(8,128)(2,1)S(1)}, bf16[2176,128]{1,0:T(8,128)(2,1)S(1)}, u32[]{:S(2)}, u32[]{:S(2)}) collective-permute-start(bf16[2176,128]{1,0:T(8,128)(2,1)S(1)} %collective-permute-done.refs_0_), channel_id=1, source_target_pairs={{0,24},{1,25},{2,26},{3,27},{4,12},{5,13},{6,14},{7,15},{8,0},{9,1... | collective-permute-start | bytes 1671176 | tf_op jit(solution)/shard_map/ppermute | solution.py:259
  27.7 0.0 copy-start
  27.7 1.2 %copy-done = bf16[4,512,256]{2,1,0:T(8,128)(2,1)S(1)} copy-done((bf16[4,512,256]{2,1,0:T(8,128)(2,1)S(1)}, bf16[4,512,256]{2,1,0:T(8,128)(2,1)}, u32[]{:S(2)}) %copy-start) | copy-done | bytes 1048600
  28.9 0.0 copy-start.1
  28.9 1.1 %copy-done.1 = bf16[2176,128]{1,0:T(8,128)(2,1)S(1)} copy-done((bf16[2176,128]{1,0:T(8,128)(2,1)S(1)}, bf16[2176,128]{1,0:T(8,128)(2,1)}, u32[]{:S(2)}) %copy-start.1) | copy-done | bytes 557080
  29.9 0.0 copy-start.2
  29.9 1.1 %copy-done.2 = bf16[2176,128]{1,0:T(8,128)(2,1)S(1)} copy-done((bf16[2176,128]{1,0:T(8,128)(2,1)S(1)}, bf16[2176,128]{1,0:T(8,128)(2,1)}, u32[]{:S(2)}) %copy-start.2) | copy-done | bytes 557080
  31.0 2.8 %own_inner.1 = (f32[2048,128]{1,0:T(8,128)S(1)}, f32[2048,128]{1,0:T(8,128)S(1)}, f32[2048,128]{1,0:T(8,128)S(1)}, f32[2048,128]{1,0:T(8,128)S(1)}) custom-call(s32[1]{0:T(128)} %bitcast.role_ref, bf16[4,512,256]{2,1,0:T(8,128)(2,1)S(1)} %copy-done, bf16[2176,128]{1,0:T(8,128)(2,1)S(1)} %copy-done.1, bf16[2176,128]{1,0:T(8,128)(2,1)S(1)} %copy-done.2, ...), custom_call_target="tpu_custom_call" | custom-call | flops 2147483648 | bytes 6422528 | tf_op jit(solution)/shard_map/own_inner/pallas_call | solution.py:190
  33.8 0.0 collective-permute-done.1.refs_1_
  33.8 0.0 collective-permute-done.2.refs_2_
  33.8 1.6 %sent_inner.1 = (bf16[2048,128]{1,0:T(8,128)(2,1)S(1)}, bf16[2048,128]{1,0:T(8,128)(2,1)S(1)}) custom-call(s32[1]{0:T(128)} %bitcast.role_ref, bf16[4,512,256]{2,1,0:T(8,128)(2,1)S(1)} %copy-done, bf16[2176,128]{1,0:T(8,128)(2,1)S(1)} %collective-permute-done.refs_0_, bf16[2176,128]{1,0:T(8,128)(2,1)S(1)} %collective-permute-done.1.refs_1_, ...), custom_call_target="tpu_custom_call" | custom-call | flops 1073741824 | bytes 6422528 | tf_op jit(solution)/shard_map/sent_inner/pallas_call | solution.py:190
  35.5 0.1 collective-permute-start.8
  35.5 3.3 %collective-permute-start.9 = (bf16[2048,128]{1,0:T(8,128)(2,1)S(1)}, bf16[2048,128]{1,0:T(8,128)(2,1)S(1)}, u32[]{:S(2)}, u32[]{:S(2)}) collective-permute-start(bf16[2048,128]{1,0:T(8,128)(2,1)S(1)} %get-tuple-element.39), channel_id=1, source_target_pairs={{0,6},{1,7},{2,4},{3,5},{4,1},{5,0},{6,3},{7,2},{8,14},{9,15},{10,... | collective-permute-start | bytes 1572872 | tf_op jit(solution)/shard_map/ppermute | solution.py:259
  38.8 0.0 copy-start.3
  38.8 1.7 %kept_inner.1 = (f32[2048,128]{1,0:T(8,128)S(1)}, bf16[2048,128]{1,0:T(8,128)(2,1)S(1)}) custom-call(s32[1]{0:T(128)} %bitcast.role_ref, bf16[4,512,256]{2,1,0:T(8,128)(2,1)S(1)} %copy-done, bf16[2176,128]{1,0:T(8,128)(2,1)S(1)} %collective-permute-done.refs_0_, bf16[2176,128]{1,0:T(8,128)(2,1)S(1)} %collective-permute-done.1.refs_1_, ...), custom_call_target="tpu_custom_call" | custom-call | flops 1073741824 | bytes 6422528 | tf_op jit(solution)/shard_map/kept_inner/pallas_call | solution.py:190
  40.5 0.0 collective-permute-done.7.refs_4_
  40.6 0.0 copy-done.3
  40.6 4.1 %own_boundary.1 = (f32[2048,128]{1,0:T(8,128)S(1)}, f32[2048,128]{1,0:T(8,128)S(1)}, f32[2048,128]{1,0:T(8,128)S(1)}, f32[2048,128]{1,0:T(8,128)S(1)}) custom-call(s32[1]{0:T(128)} %bitcast.role_ref, bf16[4,512,256]{2,1,0:T(8,128)(2,1)S(1)} %copy-done, bf16[2176,128]{1,0:T(8,128)(2,1)S(1)} %copy-done.1, bf16[2176,128]{1,0:T(8,128)(2,1)S(1)} %copy-done.3, ...), custom_call_target="tpu_custom_call" | custom-call | flops 2147483648 | bytes 7536640 | tf_op jit(solution)/shard_map/own_boundary/pallas_call | solution.py:190
  44.7 0.0 collective-permute-done.4.refs_3_
  44.7 3.1 %collective-permute-done.5.refs_4_ = bf16[2176,128]{1,0:T(8,128)(2,1)S(1)} collective-permute-done((bf16[2176,128]{1,0:T(8,128)(2,1)S(1)}, bf16[2176,128]{1,0:T(8,128)(2,1)S(1)}, u32[]{:S(2)}, u32[]{:S(2)}) %collective-permute-start.5) | collective-permute-done | bytes 557088 | tf_op jit(solution)/shard_map/ppermute | solution.py:259
  47.8 2.5 %sent_boundary.1 = (bf16[2048,128]{1,0:T(8,128)(2,1)S(1)}, bf16[2048,128]{1,0:T(8,128)(2,1)S(1)}, bf16[2048,128]{1,0:T(8,128)(2,1)S(1)}) custom-call(s32[1]{0:T(128)} %bitcast.role_ref, bf16[4,512,256]{2,1,0:T(8,128)(2,1)S(1)} %copy-done, bf16[2176,128]{1,0:T(8,128)(2,1)S(1)} %collective-permute-done.refs_0_, ...), custom_call_target="tpu_custom_call" | custom-call | flops 1610612736 | bytes 9633792 | tf_op jit(solution)/shard_map/sent_boundary/pallas_call | solution.py:190
  50.3 0.1 collective-permute-start.10
  50.4 2.6 %collective-permute-start.11 = (bf16[2048,128]{1,0:T(8,128)(2,1)S(1)}, bf16[2048,128]{1,0:T(8,128)(2,1)S(1)}, u32[]{:S(2)}, u32[]{:S(2)}) collective-permute-start(bf16[2048,128]{1,0:T(8,128)(2,1)S(1)} %get-tuple-element.40), channel_id=1, source_target_pairs={{0,4},{1,5},{2,6},{3,7},{4,0},{5,1},{6,2},{7,3},{8,12},{9,13},{10,... | collective-permute-start | bytes 1572872 | tf_op jit(solution)/shard_map/ppermute | solution.py:259
  53.0 1.1 %collective-permute-start.13 = (bf16[2048,128]{1,0:T(8,128)(2,1)S(1)}, bf16[2048,128]{1,0:T(8,128)(2,1)S(1)}, u32[]{:S(2)}, u32[]{:S(2)}) collective-permute-start(bf16[2048,128]{1,0:T(8,128)(2,1)S(1)} %get-tuple-element.42), channel_id=1, source_target_pairs={{0,6},{1,7},{2,4},{3,5},{4,1},{5,0},{6,3},{7,2},{8,14},{9,15},{10,... | collective-permute-start | bytes 1572872 | tf_op jit(solution)/shard_map/ppermute | solution.py:259
  54.2 0.0 collective-permute-done.8.refs_7_.refs_3_
  54.2 0.9 %collective-permute-start.12 = (bf16[2048,128]{1,0:T(8,128)(2,1)S(1)}, bf16[2048,128]{1,0:T(8,128)(2,1)S(1)}, u32[]{:S(2)}, u32[]{:S(2)}) collective-permute-start(bf16[2048,128]{1,0:T(8,128)(2,1)S(1)} %get-tuple-element.41), channel_id=1, source_target_pairs={{0,4},{1,5},{2,6},{3,7},{4,0},{5,1},{6,2},{7,3},{8,12},{9,13},{10,... | collective-permute-start | bytes 1572872 | tf_op jit(solution)/shard_map/ppermute | solution.py:259
  55.1 0.0 collective-permute-done.9.refs_8_.refs_7_
  55.1 0.8 %kept_boundary.1.refs_0_ = f32[2048,128]{1,0:T(8,128)S(1)} custom-call(s32[1]{0:T(128)} %bitcast.role_ref, bf16[4,512,256]{2,1,0:T(8,128)(2,1)S(1)} %copy-done, bf16[2176,128]{1,0:T(8,128)(2,1)S(1)} %collective-permute-done.refs_0_, bf16[2176,128]{1,0:T(8,128)(2,1)S(1)} %collective-permute-done.1.refs_1_, ...), custom_call_target="tpu_custom_call" | custom-call | flops 536870912 | bytes 5439488 | tf_op jit(solution)/shard_map/kept_boundary/pallas_call | solution.py:190
  55.9 2.8 %collective-permute-done.10.refs_2_ = bf16[2048,128]{1,0:T(8,128)(2,1)S(1)} collective-permute-done((bf16[2048,128]{1,0:T(8,128)(2,1)S(1)}, bf16[2048,128]{1,0:T(8,128)(2,1)S(1)}, u32[]{:S(2)}, u32[]{:S(2)}) %collective-permute-start.10) | collective-permute-done | bytes 524320 | tf_op jit(solution)/shard_map/ppermute | solution.py:259
  58.7 0.0 collective-permute-done.11.refs_4_
  58.7 8.3 %collective-permute-done.13.refs_6_ = bf16[2048,128]{1,0:T(8,128)(2,1)S(1)} collective-permute-done((bf16[2048,128]{1,0:T(8,128)(2,1)S(1)}, bf16[2048,128]{1,0:T(8,128)(2,1)S(1)}, u32[]{:S(2)}, u32[]{:S(2)}) %collective-permute-start.13) | collective-permute-done | bytes 524320 | tf_op jit(solution)/shard_map/ppermute | solution.py:259
  67.0 0.0 collective-permute-done.12.refs_5_
  67.0 2.3 %final.1 = bf16[2,128,4096]{2,1,0:T(8,128)(2,1)} custom-call(s32[1]{0:T(128)} %bitcast.role_ref, f32[2048,128]{1,0:T(8,128)S(1)} %kept_boundary.1.refs_0_, f32[2048,128]{1,0:T(8,128)S(1)} %get-tuple-element.37.refs_8_.refs_1_, bf16[2048,128]{1,0:T(8,128)(2,1)S(1)} %collective-permute-done.10.refs_2_, ...), custom_call_target="tpu_custom_call" | custom-call | bytes 8388608 | tf_op jit(solution)/shard_map/final/pallas_call | solution.py:228
Async XLA Ops:
  3.8 22.5 %collective-permute-start.6 = (bf16[2,2176,128]{2,1,0:T(8,128)(2,1)}, bf16[2,2176,128]{2,1,0:T(8,128)(2,1)S(1)}, u32[]{:S(2)}, u32[]{:S(2)}) collective-permute-start(bf16[2,2176,128]{2,1,0:T(8,128)(2,1)} %get-tuple-element.26), channel_id=1, source_target_pairs={{0,4},{1,5},{2,6},{3,7},{4,0},{5,1},{6,2},{7,3},{8,12},{9,13},{10,... | collective-permute-start | bytes 3342344 | tf_op jit(solution)/shard_map/ppermute | solution.py:259
  3.8 30.0 %collective-permute-start.2 = (bf16[2,2176,128]{2,1,0:T(8,128)(2,1)}, bf16[2,2176,128]{2,1,0:T(8,128)(2,1)S(1)}, u32[]{:S(2)}, u32[]{:S(2)}) collective-permute-start(bf16[2,2176,128]{2,1,0:T(8,128)(2,1)} %get-tuple-element.26), channel_id=1, source_target_pairs={{0,6},{1,7},{2,4},{3,5},{4,1},{5,0},{6,3},{7,2},{8,14},{9,15},{10,... | collective-permute-start | bytes 3342344 | tf_op jit(solution)/shard_map/ppermute | solution.py:259
  6.4 15.0 %collective-permute-start = (bf16[2176,128]{1,0:T(8,128)(2,1)}, bf16[2176,128]{1,0:T(8,128)(2,1)S(1)}, u32[]{:S(2)}, u32[]{:S(2)}) collective-permute-start(bf16[2176,128]{1,0:T(8,128)(2,1)} %get-tuple-element.24.refs_0_), channel_id=1, source_target_pairs={{0,1},{1,0},{2,3},{3,2},{4,6},{5,7},{6,4},{7,5},{8,9},{9,8},{10,11... | collective-permute-start | bytes 1671176 | tf_op jit(solution)/shard_map/ppermute | solution.py:259
  7.6 17.4 %collective-permute-start.3 = (bf16[2176,128]{1,0:T(8,128)(2,1)}, bf16[2176,128]{1,0:T(8,128)(2,1)}, u32[]{:S(2)}, u32[]{:S(2)}) collective-permute-start(bf16[2176,128]{1,0:T(8,128)(2,1)} %get-tuple-element.27), channel_id=1, source_target_pairs={{0,28},{1,29},{2,30},{3,31},{4,8},{5,9},{6,10},{7,11},{8,4},{9,5},... | collective-permute-start | bytes 1671176 | tf_op jit(solution)/shard_map/ppermute | solution.py:259
  9.6 24.2 %collective-permute-start.1 = (bf16[2176,128]{1,0:T(8,128)(2,1)}, bf16[2176,128]{1,0:T(8,128)(2,1)S(1)}, u32[]{:S(2)}, u32[]{:S(2)}) collective-permute-start(bf16[2176,128]{1,0:T(8,128)(2,1)} %get-tuple-element.25.refs_1_), channel_id=1, source_target_pairs={{0,1},{1,0},{2,3},{3,2},{4,6},{5,7},{6,4},{7,5},{8,9},{9,8},{10,11... | collective-permute-start | bytes 1671176 | tf_op jit(solution)/shard_map/ppermute | solution.py:259
  21.4 19.2 %collective-permute-start.7 = (bf16[2176,128]{1,0:T(8,128)(2,1)}, bf16[2176,128]{1,0:T(8,128)(2,1)}, u32[]{:S(2)}, u32[]{:S(2)}) collective-permute-start(bf16[2176,128]{1,0:T(8,128)(2,1)} %get-tuple-element.24.refs_0_), channel_id=1, source_target_pairs={{0,24},{1,25},{2,26},{3,27},{4,12},{5,13},{6,14},{7,15},{8,0},{9,1... | collective-permute-start | bytes 1671176 | tf_op jit(solution)/shard_map/ppermute | solution.py:259
  25.0 19.7 %collective-permute-start.4 = (bf16[2176,128]{1,0:T(8,128)(2,1)}, bf16[2176,128]{1,0:T(8,128)(2,1)S(1)}, u32[]{:S(2)}, u32[]{:S(2)}) collective-permute-start(bf16[2176,128]{1,0:T(8,128)(2,1)} %collective-permute-done.3.refs_3_), channel_id=1, source_target_pairs={{0,1},{1,0},{2,3},{3,2},{4,6},{5,7},{6,4},{7,5},{8,9},{9,8},{10,11... | collective-permute-start | bytes 1671176 | tf_op jit(solution)/shard_map/ppermute | solution.py:259
  26.3 21.5 %collective-permute-start.5 = (bf16[2176,128]{1,0:T(8,128)(2,1)S(1)}, bf16[2176,128]{1,0:T(8,128)(2,1)S(1)}, u32[]{:S(2)}, u32[]{:S(2)}) collective-permute-start(bf16[2176,128]{1,0:T(8,128)(2,1)S(1)} %collective-permute-done.refs_0_), channel_id=1, source_target_pairs={{0,24},{1,25},{2,26},{3,27},{4,12},{5,13},{6,14},{7,15},{8,0},{9,1... | collective-permute-start | bytes 1671176 | tf_op jit(solution)/shard_map/ppermute | solution.py:259
  27.7 1.2 %copy-start = (bf16[4,512,256]{2,1,0:T(8,128)(2,1)S(1)}, bf16[4,512,256]{2,1,0:T(8,128)(2,1)}, u32[]{:S(2)}) copy-start(bf16[4,512,256]{2,1,0:T(8,128)(2,1)} %weights.1.weight_ref) | copy-start | bytes 3145732
  28.9 1.1 %copy-start.1 = (bf16[2176,128]{1,0:T(8,128)(2,1)S(1)}, bf16[2176,128]{1,0:T(8,128)(2,1)}, u32[]{:S(2)}) copy-start(bf16[2176,128]{1,0:T(8,128)(2,1)} %get-tuple-element.24.refs_0_) | copy-start | bytes 1671172
  29.9 1.1 %copy-start.2 = (bf16[2176,128]{1,0:T(8,128)(2,1)S(1)}, bf16[2176,128]{1,0:T(8,128)(2,1)}, u32[]{:S(2)}) copy-start(bf16[2176,128]{1,0:T(8,128)(2,1)} %get-tuple-element.25.refs_1_) | copy-start | bytes 1671172
  35.5 18.7 %collective-permute-start.8 = (bf16[2048,128]{1,0:T(8,128)(2,1)S(1)}, bf16[2048,128]{1,0:T(8,128)(2,1)S(1)}, u32[]{:S(2)}, u32[]{:S(2)}) collective-permute-start(bf16[2048,128]{1,0:T(8,128)(2,1)S(1)} %get-tuple-element.30.refs_5_), channel_id=1, source_target_pairs={{0,2},{1,3},{2,0},{3,1},{4,5},{5,4},{6,7},{7,6},{8,10},{9,11},{10,... | collective-permute-start | bytes 1572872 | tf_op jit(solution)/shard_map/ppermute | solution.py:259
  35.5 19.6 %collective-permute-start.9 = (bf16[2048,128]{1,0:T(8,128)(2,1)S(1)}, bf16[2048,128]{1,0:T(8,128)(2,1)S(1)}, u32[]{:S(2)}, u32[]{:S(2)}) collective-permute-start(bf16[2048,128]{1,0:T(8,128)(2,1)S(1)} %get-tuple-element.39), channel_id=1, source_target_pairs={{0,6},{1,7},{2,4},{3,5},{4,1},{5,0},{6,3},{7,2},{8,14},{9,15},{10,... | collective-permute-start | bytes 1572872 | tf_op jit(solution)/shard_map/ppermute | solution.py:259
  38.8 1.8 %copy-start.3 = (bf16[2176,128]{1,0:T(8,128)(2,1)S(1)}, bf16[2176,128]{1,0:T(8,128)(2,1)}, u32[]{:S(2)}) copy-start(bf16[2176,128]{1,0:T(8,128)(2,1)} %get-tuple-element.25.refs_1_) | copy-start | bytes 1671172
  50.3 8.4 %collective-permute-start.10 = (bf16[2048,128]{1,0:T(8,128)(2,1)S(1)}, bf16[2048,128]{1,0:T(8,128)(2,1)S(1)}, u32[]{:S(2)}, u32[]{:S(2)}) collective-permute-start(bf16[2048,128]{1,0:T(8,128)(2,1)S(1)} %get-tuple-element.38.refs_6_), channel_id=1, source_target_pairs={{0,2},{1,3},{2,0},{3,1},{4,5},{5,4},{6,7},{7,6},{8,10},{9,11},{10,... | collective-permute-start | bytes 1572872 | tf_op jit(solution)/shard_map/ppermute | solution.py:259
  50.4 8.3 %collective-permute-start.11 = (bf16[2048,128]{1,0:T(8,128)(2,1)S(1)}, bf16[2048,128]{1,0:T(8,128)(2,1)S(1)}, u32[]{:S(2)}, u32[]{:S(2)}) collective-permute-start(bf16[2048,128]{1,0:T(8,128)(2,1)S(1)} %get-tuple-element.40), channel_id=1, source_target_pairs={{0,4},{1,5},{2,6},{3,7},{4,0},{5,1},{6,2},{7,3},{8,12},{9,13},{10,... | collective-permute-start | bytes 1572872 | tf_op jit(solution)/shard_map/ppermute | solution.py:259
  53.0 14.0 %collective-permute-start.13 = (bf16[2048,128]{1,0:T(8,128)(2,1)S(1)}, bf16[2048,128]{1,0:T(8,128)(2,1)S(1)}, u32[]{:S(2)}, u32[]{:S(2)}) collective-permute-start(bf16[2048,128]{1,0:T(8,128)(2,1)S(1)} %get-tuple-element.42), channel_id=1, source_target_pairs={{0,6},{1,7},{2,4},{3,5},{4,1},{5,0},{6,3},{7,2},{8,14},{9,15},{10,... | collective-permute-start | bytes 1572872 | tf_op jit(solution)/shard_map/ppermute | solution.py:259
  54.2 12.9 %collective-permute-start.12 = (bf16[2048,128]{1,0:T(8,128)(2,1)S(1)}, bf16[2048,128]{1,0:T(8,128)(2,1)S(1)}, u32[]{:S(2)}, u32[]{:S(2)}) collective-permute-start(bf16[2048,128]{1,0:T(8,128)(2,1)S(1)} %get-tuple-element.41), channel_id=1, source_target_pairs={{0,4},{1,5},{2,6},{3,7},{4,0},{5,1},{6,2},{7,3},{8,12},{9,13},{10,... | collective-permute-start | bytes 1572872 | tf_op jit(solution)/shard_map/ppermute | solution.py:259

commit v4 on v3

--- a/solution.py
+++ b/solution.py
@@ -16,6 +16,8 @@
 SLAB = HALF + 2 * ROW
 CHUNK = 512
 TURN_VMEM = 60 << 20
+COST = pl.CostEstimate(flops=1000, bytes_accessed=1000, transcendentals=0)
+LONG = pl.CostEstimate(flops=20 * 10**9, bytes_accessed=64 << 20, transcendentals=0)
 
 
 def weight_tables():
@@ -72,53 +74,62 @@
         out_shape=jax.ShapeDtypeStruct((4, 4 * CS, 2 * CS), jnp.bfloat16),
         in_specs=[smem, smem, smem, vmem],
         out_specs=vmem,
-        cost_estimate=pl.CostEstimate(flops=0, bytes_accessed=4 << 20, transcendentals=0),
+        cost_estimate=COST,
         name="weights",
     )(role, jnp.asarray(index), jnp.asarray(scale), radial.reshape(20, CS, CS))
 
 
-def turn_kernel(role_ref, field_ref, keep_edge_ref, keep_inner_ref, give_ref, give_edge_ref):
-    odd, plane = role_ref[0] % 2, pl.program_id(0)
-    turned = jnp.transpose(field_ref[0])
-    halves = [
-        [turned[2 * HALF - ROW :], turned[:HALF], turned[HALF : HALF + ROW]],
-        [turned[HALF - ROW : HALF], turned[HALF:], turned[:ROW]],
-    ]
-
-    def put(ref, half):
-        for value, at in zip(halves[half], (0, ROW, ROW + HALF)):
-            ref[at : at + value.shape[0]] = value
-
-    for parity in range(2):
-
-        @pl.when(odd == parity)
-        def _():
-            put(give_ref.at[0], 1 - parity)
-
-            @pl.when(plane == 0)
-            def _():
-                put(keep_edge_ref, parity)
-                put(give_edge_ref, 1 - parity)
-
-            @pl.when(plane == 1)
-            def _():
-                put(keep_inner_ref, parity)
+def turn_kernel(role_ref, field_ref, keep_ref, give_ref, keep_edge_ref, give_edge_ref, raw, turned, in_sems, out_sems):
+    odd = role_ref[0] % 2
+    quarter = HALF // 2
+    loads, stores = [], []
+    for p in range(2):
+        for q in range(4):
+            cells = slice(q * quarter, (q + 1) * quarter)
+            copy = pltpu.make_async_copy(
+                field_ref.at[(p + odd) % 2, :, cells], raw.at[p, :, cells], in_sems.at[p * 4 + q]
+            )
+            copy.start()
+            loads.append(copy)
+    for p in range(2):
+        for q in range(4):
+            loads[p * 4 + q].wait()
+            block = jnp.transpose(raw[p, :, q * quarter : (q + 1) * quarter])
+            turned[p, ROW + q * quarter : ROW + (q + 1) * quarter] = block
+            if q == 0:
+                turned[p, ROW + 2 * HALF :] = block[:ROW]
+            if q == 3:
+                turned[p, :ROW] = block[-ROW:]
+        kept = turned.at[p, pl.ds(pl.multiple_of(odd * HALF, HALF), SLAB)]
+        given = turned.at[p, pl.ds(pl.multiple_of((1 - odd) * HALF, HALF), SLAB)]
+        wanted = [(given, give_ref.at[p]), (kept, keep_ref.at[p])]
+        if p == 0:
+            wanted += [(given, give_edge_ref), (kept, keep_edge_ref)]
+        for source, target in wanted:
+            copy = pltpu.make_async_copy(source, target, out_sems.at[len(stores)])
+            copy.start()
+            stores.append(copy)
+    for copy in stores:
+        copy.wait()
 
 
 def turn(role, field):
     single = jax.ShapeDtypeStruct((SLAB, CS), jnp.bfloat16)
-    single_block = pl.BlockSpec((SLAB, CS), lambda p, role: (0, 0))
+    double = jax.ShapeDtypeStruct((2, SLAB, CS), jnp.bfloat16)
+    hbm = pl.BlockSpec(memory_space=pl.ANY)
     return pl.pallas_call(
         turn_kernel,
-        out_shape=(single, single, jax.ShapeDtypeStruct((2, SLAB, CS), jnp.bfloat16), single),
-        grid_spec=pltpu.PrefetchScalarGridSpec(
-            num_scalar_prefetch=1,
-            grid=(2,),
-            in_specs=[pl.BlockSpec((1, CS, 2 * HALF), lambda p, role: ((p + role[0]) % 2, 0, 0))],
-            out_specs=(single_block, single_block, pl.BlockSpec((1, SLAB, CS), lambda p, role: (p, 0, 0)), single_block),
-        ),
+        out_shape=(double, double, single, single),
+        in_specs=[pl.BlockSpec(memory_space=pltpu.SMEM), hbm],
+        out_specs=(hbm,) * 4,
+        scratch_shapes=[
+            pltpu.VMEM((2, CS, 2 * HALF), jnp.bfloat16),
+            pltpu.VMEM((2, 2 * HALF + 2 * ROW, CS), jnp.bfloat16),
+            pltpu.SemaphoreType.DMA((8,)),
+            pltpu.SemaphoreType.DMA((6,)),
+        ],
         compiler_params=pltpu.CompilerParams(vmem_limit_bytes=TURN_VMEM),
-        cost_estimate=pl.CostEstimate(flops=0, bytes_accessed=6 << 20, transcendentals=0),
+        cost_estimate=COST,
         name="turn",
     )(role, field)
 
@@ -143,7 +154,7 @@
     return centre + right + tau * left
 
 
-def conv_kernel(jobs, stacks, n_accs, role_ref, weight_ref, *refs):
+def conv_kernel(jobs, stacks, n_accs, n_outs, role_ref, weight_ref, *refs):
     role = role_ref[0]
     comp, odd = role // 2, role % 2
     gathered = comp ^ (1 + odd)
@@ -153,7 +164,9 @@
     for ref, stack in zip(refs, stacks):
         planes.append([ref] if stack == 0 else [ref.at[at] for at in range(stack)])
     accs = refs[len(stacks) : len(stacks) + n_accs]
-    outs = refs[len(refs) - len(jobs) :]
+    outs = refs[len(refs) - n_outs :]
+    if n_outs < len(jobs):
+        outs = [*outs[:-1], outs[-1].at[0], outs[-1].at[1]]
     for (triple, slot, acc), out in zip(jobs, outs):
         i, o = pairs[slot]
 
@@ -182,62 +195,61 @@
             run(False, 4 * CS)
 
 
-def conv(name, role, weight, planes, accs, jobs, types, after=()):
+def conv(name, role, weight, planes, accs, jobs, types, after=(), cost=COST):
     vmem = pl.BlockSpec(memory_space=pltpu.VMEM)
-    flops = len(jobs) * 2 * 256 * 512 * HALF
-    size = sum(a.size * a.dtype.itemsize for a in (*planes, *accs)) + len(jobs) * CS * HALF * 4
     stacks = [a.shape[0] if a.ndim == 3 else 0 for a in planes]
     return pl.pallas_call(
-        functools.partial(conv_kernel, jobs, stacks, len(accs)),
-        out_shape=tuple(jax.ShapeDtypeStruct((HALF, CS), t) for t in types),
+        functools.partial(conv_kernel, jobs, stacks, len(accs), len(types)),
+        out_shape=tuple(
+            jax.ShapeDtypeStruct((2, HALF, CS) if len(types) < len(jobs) and at == len(types) - 1 else (HALF, CS), t)
+            for at, t in enumerate(types)
+        ),
         in_specs=[pl.BlockSpec(memory_space=pltpu.SMEM)]
         + [vmem] * (1 + len(planes) + len(accs))
         + [pl.BlockSpec(memory_space=pl.ANY)] * len(after),
         out_specs=tuple(vmem for _ in types),
         compiler_params=pltpu.CompilerParams(vmem_limit_bytes=40 << 20),
-        cost_estimate=pl.CostEstimate(flops=flops, bytes_accessed=size, transcendentals=0),
+        cost_estimate=cost,
         name=name,
     )(role, weight, *planes, *accs, *after)
 
 
-def final_kernel(role_ref, *refs):
-    own, others, out_ref = refs[:4], refs[4:8], refs[8]
-    plane, side = pl.program_id(0), pl.program_id(1)
-
-    def put(first, second):
-        total = first.astype(jnp.float32) + second.astype(jnp.float32)
-        out_ref[0] = jnp.transpose(total.astype(out_ref.dtype))
-
-    for p in range(2):
-
-        @pl.when((plane == p) & (side == 0))
+def final_kernel(parts, role_ref, *refs):
+    out_ref = refs[-1]
+    for p in range(parts):
+
+        @pl.when(pl.program_id(0) == p)
         def _():
-            put(own[p][...], own[2 + p][...])
-
-        @pl.when((plane == p) & (side == 1))
-        def _():
-            put(others[p][...], others[2 + p][...])
-
-
-def final(role, own, others):
-    def at(plane, side, role):
+            total = refs[p][...].astype(jnp.float32) + refs[parts + p][...].astype(jnp.float32)
+            out_ref[0] = jnp.transpose(total.astype(out_ref.dtype))
+
+
+def final(name, role, places, kept, got, out=None):
+    def at(part, role):
         odd = role[0] % 2
+        plane, side = (sum(jnp.where(part == p, place[d], 0) for p, place in enumerate(places)) for d in (0, 1))
         return ((plane + odd) % 2, 0, (side + odd) % 2)
 
-    vmem = pl.BlockSpec(memory_space=pltpu.VMEM)
+    def whole(value):
+        if isinstance(value, tuple):
+            array, index = value
+            return array, pl.BlockSpec((None, HALF, CS), lambda p, role, index=index: (index, 0, 0))
+        return value, pl.BlockSpec((HALF, CS), lambda p, role: (0, 0))
+
+    arrays, specs = zip(*[whole(value) for value in (*kept, *got)])
+    if out is not None:
+        arrays, specs = (*arrays, out), (*specs, pl.BlockSpec(memory_space=pl.ANY))
     return pl.pallas_call(
-        final_kernel,
+        functools.partial(final_kernel, len(places)),
         out_shape=jax.ShapeDtypeStruct((2, CS, 2 * HALF), jnp.bfloat16),
         grid_spec=pltpu.PrefetchScalarGridSpec(
-            num_scalar_prefetch=1,
-            grid=(2, 2),
-            in_specs=[vmem] * 8,
-            out_specs=pl.BlockSpec((1, CS, HALF), at),
+            num_scalar_prefetch=1, grid=(len(places),), in_specs=list(specs), out_specs=pl.BlockSpec((1, CS, HALF), at)
         ),
+        input_output_aliases={} if out is None else {len(arrays): 0},
         compiler_params=pltpu.CompilerParams(vmem_limit_bytes=40 << 20),
-        cost_estimate=pl.CostEstimate(flops=0, bytes_accessed=8 << 20, transcendentals=0),
-        name="final",
-    )(role, *own, *others)
+        cost_estimate=COST,
+        name=name,
+    )(role, *arrays)
 
 
 def shards(tensor_field, radial):
@@ -285,29 +297,29 @@
         return permute(value, lambda z, k, c: (2 * outward(z, k) + k, c))
 
     f32, bf16 = jnp.float32, jnp.bfloat16
-    keep_edge, keep_inner, give, give_edge = turn(role, field)
-    near_edge = gather_near(keep_edge)
+    keep, give, keep_edge, give_edge = turn(role, field)
+    near = gather_near(keep)
     halo_near = permute(give_edge, lambda z, k, c: (2 * outward(z, k) + 1 - k, c))
     halo_far = from_far(keep_edge)
-    near_inner = gather_near(keep_inner)
     near_others = permute(give, lambda z, k, c: (2 * z + 1 - k, gather_group(1 - k, c)))
     others = swap(give)
     weight = weights(role, radial)
 
-    inner = {1: (0, 0), 2: (1, 0), 4: (2, 0), 3: (2, 1)}
-    all_planes = inner | {0: (3, 0), 5: (4, 0)}
+    inner = {1: (0, 0), 2: (0, 1), 4: (1, 0), 3: (1, 1)}
+    all_planes = inner | {0: (2, 0), 5: (3, 0)}
 
     def jobs(of, *wanted):
         return [(tuple(of[at] for at in (plane - 1, plane, plane + 1)), slot, acc) for plane, slot, acc in wanted]
 
-    own = [keep_edge, keep_inner, others]
+    own = [keep, others]
     kept2, kept3, lent2, lent3 = conv(
         "own_inner", role, weight, own, [],
         jobs(inner, (2, 0, None), (3, 0, None), (2, 1, None), (3, 1, None)), [f32] * 4,
     )
-    far_halo = from_far(near_edge)
-    near_halo = gather_near(halo_near)
-    near = [near_edge, near_inner, near_others]
+    kept2, near_ready, halo_ready = lax.optimization_barrier((kept2, near, halo_near))
+    near_halo = gather_near(halo_ready)
+    far_halo = from_far(near_ready[0])
+    near = [near, near_others]
     sent2, sent3 = conv(
         "sent_inner", role, weight, near, [lent2, lent3], jobs(inner, (2, 2, 0), (3, 2, 1)), [bf16] * 2,
     )
@@ -316,21 +328,23 @@
         "own_boundary", role, weight, [*own, halo_near, halo_far], [],
         jobs(all_planes, (1, 0, None), (4, 0, None), (1, 1, None), (4, 1, None)), [f32] * 4, after=[sent2],
     )
-    total2, total3 = conv(
-        "kept_inner", role, weight, near, [kept2, kept3], jobs(inner, (2, 3, 0), (3, 3, 1)), [f32, bf16], after=[sent2],
-    )
-    crossed3 = swap(total3)
     near = [*near, near_halo, far_halo]
-    sent1, sent4, total4 = conv(
-        "sent_boundary", role, weight, near, [lent1, lent4, kept4],
-        jobs(all_planes, (1, 2, 0), (4, 2, 1), (4, 3, 2)), [bf16] * 3, after=[total2],
-    )
-    got1, got4 = reduce_near(sent1), reduce_far(sent4)
-    crossed4 = swap(total4)
-    total1, = conv(
-        "kept_boundary", role, weight, near, [kept1], jobs(all_planes, (1, 3, 0)), [f32], after=[sent1, got2, got3],
-    )
-    out = final(role, [total1, total2, got1, got2], [crossed4, crossed3, got4, got3])
+    sent1, = conv(
+        "sent_near", role, weight, near[:3], [lent1], jobs(all_planes, (1, 2, 0)), [bf16],
+    )
+    sent4, total = conv(
+        "far", role, weight, near, [lent4, kept4, kept3],
+        jobs(all_planes, (4, 2, 0), (4, 3, 1), (3, 3, 2)), [bf16] * 2, after=[sent1],
+    )
+    got1, got4, crossed = reduce_near(sent1), reduce_far(sent4), swap(total)
+    total1, total2 = conv(
+        "kept_near", role, weight, near, [kept1, kept2],
+        jobs(all_planes, (1, 3, 0), (2, 3, 1)), [f32] * 2, after=[sent1, got2, got3], cost=LONG,
+    )
+    out = final(
+        "final", role, [(0, 0), (1, 0), (1, 1)], [total1, total2, (crossed, 1)], [got1, got2, got3]
+    )
+    out = final("final_edge", role, [(0, 1)], [(crossed, 0)], [got4], out)
     if sub > 1:
         out = lax.dynamic_slice_in_dim(out, lax.axis_index("chan") % sub * tensor_field.shape[1], tensor_field.shape[1], 1)
     return out

time: 69.6 us -> 65 us (0.934)
  the two profiles are of different devices: /device:TPU:1 before, /device:TPU:0 now
where the time goes in v4:
time: 65 us; the launch traced here: 64.6 us
  Pallas kernels  23.5 us (36%)
  starting transfers between devices  20.1 us (31%)
  waiting for transfers between devices  19.7 us (30%)
  local copies, waits for them, and re-layouts  1.27 us (2%)
    ppermute x12, starting transfers between devices, permute(): return lax.ppermute(value, ('space', 'chan'), pairs)  20.1 us
    ppermute x12, waiting for transfers between devices, permute(): return lax.ppermute(value, ('space', 'chan'), pairs)  19.7 us
    pallas_call x6, Pallas kernels, conv(): pl.pallas_call(functools.partial(conv_kernel, jobs, stacks, len(accs), le...  14.7 us
    pallas_call x1, Pallas kernels, turn(): pl.pallas_call(turn_kernel, out_shape=(double, double, single, single), i...  3.29 us
    pallas_call x2, Pallas kernels, final(): pl.pallas_call(functools.partial(final_kernel, len(places)), out_shape=ja...  2.99 us
    pallas_call x1, Pallas kernels, weights(): pl.pallas_call(weights_kernel, out_shape=jax.ShapeDtypeStruct((4, 4 * CS,...  2.51 us
  transfers between devices with their start and end apart: 12, of which 6 were waited for; matrix products, arithmetic and copies ran while one was open for 0% of the time, Pallas kernels for 30%

profile of v4, /device:TPU:0, one launch (start us, length us, event | category | flops | bytes accessed | tf_op | source)
XLA Modules:
  0.0 64.6 jit_solution(9303695394621250304)
XLA Ops:
  0.0 3.3 %turn.1 = (bf16[2,2176,128]{2,1,0:T(8,128)(2,1)}, bf16[2,2176,128]{2,1,0:T(8,128)(2,1)}, bf16[2176,128]{1,0:T(8,128)(2,1)}, bf16[2176,128]{1,0:T(8,128)(2,1)}) custom-call(s32[1]{0:T(128)} %bitcast.role_ref, bf16[2,128,4096]{2,1,0:T(8,128)(2,1)} %field_ref.1), custom_call_target="tpu_custom_call" | custom-call | flops 1000 | bytes 1000 | tf_op jit(solution)/shard_map/turn/pallas_call | solution.py:120
  3.3 0.0 copy-start.1
  3.3 0.5 collective-permute-start.2
  3.8 2.6 %collective-permute-start = (bf16[2,2176,128]{2,1,0:T(8,128)(2,1)}, bf16[2,2176,128]{2,1,0:T(8,128)(2,1)S(1)}, u32[]{:S(2)}, u32[]{:S(2)}) collective-permute-start(bf16[2,2176,128]{2,1,0:T(8,128)(2,1)} %get-tuple-element.26.refs_0_), channel_id=1, source_target_pairs={{0,1},{1,0},{2,3},{3,2},{4,6},{5,7},{6,4},{7,5},{8,9},{9,8},{10,11... | collective-permute-start | bytes 3342344 | tf_op jit(solution)/shard_map/ppermute | solution.py:271
  6.4 3.4 %collective-permute-start.3 = (bf16[2176,128]{1,0:T(8,128)(2,1)}, bf16[2176,128]{1,0:T(8,128)(2,1)}, u32[]{:S(2)}, u32[]{:S(2)}) collective-permute-start(bf16[2176,128]{1,0:T(8,128)(2,1)} %get-tuple-element.29), channel_id=1, source_target_pairs={{0,28},{1,29},{2,30},{3,31},{4,8},{5,9},{6,10},{7,11},{8,4},{9,5},... | collective-permute-start | bytes 1671176 | tf_op jit(solution)/shard_map/ppermute | solution.py:271
  9.8 0.0 collective-permute-start.1
  9.8 1.7 %collective-permute-start.6 = (bf16[2176,128]{1,0:T(8,128)(2,1)}, bf16[2176,128]{1,0:T(8,128)(2,1)}, u32[]{:S(2)}, u32[]{:S(2)}) collective-permute-start(bf16[2176,128]{1,0:T(8,128)(2,1)} %get-tuple-element.32), channel_id=1, source_target_pairs={{0,24},{1,25},{2,26},{3,27},{4,12},{5,13},{6,14},{7,15},{8,0},{9,1... | collective-permute-start | bytes 1671176 | tf_op jit(solution)/shard_map/ppermute | solution.py:271
  11.5 2.5 %weights.1.weight_ref = bf16[4,512,256]{2,1,0:T(8,128)(2,1)} custom-call(s32[1]{0:T(128)} %bitcast.role_ref, s32[8,64]{1,0:T(8,128)} %constant.37.clone.index_ref, f32[8,64]{1,0:T(8,128)} %constant.38.clone.scale_ref, bf16[20,128,128]{2,1,0:T(8,128)(2,1)} %bitcast.4), custom_call_target="tpu_custom_call" | custom-call | flops 1000 | bytes 1000 | tf_op jit(solution)/shard_map/weights/pallas_call | solution.py:72
  14.0 0.0 collective-permute-done.2.refs_1_
  14.0 0.0 copy-done.1
  14.0 0.0 copy-start
  14.0 1.2 %copy-done = bf16[4,512,256]{2,1,0:T(8,128)(2,1)S(1)} copy-done((bf16[4,512,256]{2,1,0:T(8,128)(2,1)S(1)}, bf16[4,512,256]{2,1,0:T(8,128)(2,1)}, u32[]{:S(2)}) %copy-start) | copy-done | bytes 1048600
  15.2 4.0 %own_inner.1 = (f32[2048,128]{1,0:T(8,128)S(1)}, f32[2048,128]{1,0:T(8,128)S(1)}, f32[2048,128]{1,0:T(8,128)S(1)}, f32[2048,128]{1,0:T(8,128)S(1)}) custom-call(s32[1]{0:T(128)} %bitcast.role_ref, bf16[4,512,256]{2,1,0:T(8,128)(2,1)S(1)} %copy-done, bf16[2,2176,128]{2,1,0:T(8,128)(2,1)S(1)} %copy-done.1, bf16[2,2176,128]{2,1,0:T(8,128)(2,1)} %collective-permute-done.2.refs_1_), custom_call_target="tpu_custom_call" | custom-call | flops 1000 | bytes 1000 | tf_op jit(solution)/shard_map/own_inner/pallas_call | solution.py:201
  19.2 4.0 %collective-permute-done.3.refs_2_ = bf16[2176,128]{1,0:T(8,128)(2,1)} collective-permute-done((bf16[2176,128]{1,0:T(8,128)(2,1)}, bf16[2176,128]{1,0:T(8,128)(2,1)}, u32[]{:S(2)}, u32[]{:S(2)}) %collective-permute-start.3) | collective-permute-done | bytes 557088 | tf_op jit(solution)/shard_map/ppermute | solution.py:271
  23.2 4.1 %collective-permute-done.refs_0_ = bf16[2,2176,128]{2,1,0:T(8,128)(2,1)S(1)} collective-permute-done((bf16[2,2176,128]{2,1,0:T(8,128)(2,1)}, bf16[2,2176,128]{2,1,0:T(8,128)(2,1)S(1)}, u32[]{:S(2)}, u32[]{:S(2)}) %collective-permute-start) | collective-permute-done | bytes 1114144 | tf_op jit(solution)/shard_map/ppermute | solution.py:271
  27.3 2.4 %collective-permute-start.4 = (bf16[2176,128]{1,0:T(8,128)(2,1)}, bf16[2176,128]{1,0:T(8,128)(2,1)S(1)}, u32[]{:S(2)}, u32[]{:S(2)}) collective-permute-start(bf16[2176,128]{1,0:T(8,128)(2,1)} %collective-permute-done.3.refs_2_), channel_id=1, source_target_pairs={{0,1},{1,0},{2,3},{3,2},{4,6},{5,7},{6,4},{7,5},{8,9},{9,8},{10,11... | collective-permute-start | bytes 1671176 | tf_op jit(solution)/shard_map/ppermute | solution.py:271
  29.7 6.9 %collective-permute-start.5 = (bf16[2176,128]{1,0:T(8,128)(2,1)S(1)}, bf16[2176,128]{1,0:T(8,128)(2,1)S(1)}, u32[]{:S(2)}, u32[]{:S(2)}) collective-permute-start(bf16[2176,128]{1,0:T(8,128)(2,1)S(1)} %slice_bitcast_fusion), channel_id=1, source_target_pairs={{0,24},{1,25},{2,26},{3,27},{4,12},{5,13},{6,14},{7,15},{8,0},{9,1... | collective-permute-start | bytes 1671176 | tf_op jit(solution)/shard_map/ppermute | solution.py:271
  36.6 0.0 collective-permute-done.1.refs_1_
  36.6 1.5 %sent_inner.1 = (bf16[2048,128]{1,0:T(8,128)(2,1)S(1)}, bf16[2048,128]{1,0:T(8,128)(2,1)S(1)}) custom-call(s32[1]{0:T(128)} %bitcast.role_ref, bf16[4,512,256]{2,1,0:T(8,128)(2,1)S(1)} %copy-done, bf16[2,2176,128]{2,1,0:T(8,128)(2,1)S(1)} %collective-permute-done.refs_0_, bf16[2,2176,128]{2,1,0:T(8,128)(2,1)S(1)} %collective-permute-done.1.refs_1_, ...), custom_call_target="tpu_custom_call" | custom-call | flops 1000 | bytes 1000 | tf_op jit(solution)/shard_map/sent_inner/pallas_call | solution.py:201
  38.1 0.1 collective-permute-start.10
  38.2 2.2 %collective-permute-start.9 = (bf16[2048,128]{1,0:T(8,128)(2,1)S(1)}, bf16[2048,128]{1,0:T(8,128)(2,1)S(1)}, u32[]{:S(2)}, u32[]{:S(2)}) collective-permute-start(bf16[2048,128]{1,0:T(8,128)(2,1)S(1)} %get-tuple-element.35.refs_4_), channel_id=1, source_target_pairs={{0,2},{1,3},{2,0},{3,1},{4,5},{5,4},{6,7},{7,6},{8,10},{9,11},{10,... | collective-permute-start | bytes 1572872 | tf_op jit(solution)/shard_map/ppermute | solution.py:271
  40.4 0.0 collective-permute-done.6.refs_3_
  40.4 4.5 %own_boundary.1 = (f32[2048,128]{1,0:T(8,128)S(1)}, f32[2048,128]{1,0:T(8,128)S(1)}, f32[2048,128]{1,0:T(8,128)S(1)}, f32[2048,128]{1,0:T(8,128)S(1)}) custom-call(s32[1]{0:T(128)} %bitcast.role_ref, bf16[4,512,256]{2,1,0:T(8,128)(2,1)S(1)} %copy-done, bf16[2,2176,128]{2,1,0:T(8,128)(2,1)S(1)} %copy-done.1, ...), custom_call_target="tpu_custom_call" | custom-call | flops 1000 | bytes 1000 | tf_op jit(solution)/shard_map/own_boundary/pallas_call | solution.py:201
  44.9 0.0 collective-permute-done.4.refs_2_
  44.9 0.8 %sent_near.1.refs_7_.refs_6_ = bf16[2048,128]{1,0:T(8,128)(2,1)S(1)} custom-call(s32[1]{0:T(128)} %bitcast.role_ref, bf16[4,512,256]{2,1,0:T(8,128)(2,1)S(1)} %copy-done, bf16[2,2176,128]{2,1,0:T(8,128)(2,1)S(1)} %collective-permute-done.refs_0_, bf16[2,2176,128]{2,1,0:T(8,128)(2,1)S(1)} %collective-permute-done.1.refs_1_, ...), custom_call_target="tpu_custom_call" | custom-call | flops 1000 | bytes 1000 | tf_op jit(solution)/shard_map/sent_near/pallas_call | solution.py:201
  45.7 0.1 collective-permute-start.11
  45.8 2.1 %collective-permute-done.5.refs_3_ = bf16[2176,128]{1,0:T(8,128)(2,1)S(1)} collective-permute-done((bf16[2176,128]{1,0:T(8,128)(2,1)S(1)}, bf16[2176,128]{1,0:T(8,128)(2,1)S(1)}, u32[]{:S(2)}, u32[]{:S(2)}) %collective-permute-start.5) | collective-permute-done | bytes 557088 | tf_op jit(solution)/shard_map/ppermute | solution.py:271
  47.9 2.4 %far.1 = (bf16[2048,128]{1,0:T(8,128)(2,1)S(1)}, bf16[2,2048,128]{2,1,0:T(8,128)(2,1)S(1)}) custom-call(s32[1]{0:T(128)} %bitcast.role_ref, bf16[4,512,256]{2,1,0:T(8,128)(2,1)S(1)} %copy-done, bf16[2,2176,128]{2,1,0:T(8,128)(2,1)S(1)} %collective-permute-done.refs_0_, bf16[2,2176,128]{2,1,0:T(8,128)(2,1)S(1)} %collective-permute-done.1.refs_1_, ...), custom_call_target="tpu_custom_call" | custom-call | flops 1000 | bytes 1000 | tf_op jit(solution)/shard_map/far/pallas_call | solution.py:201
  50.3 0.1 collective-permute-start.7
  50.4 0.3 collective-permute-start.8
  50.7 0.0 collective-permute-done.10.refs_8_.refs_5_
  50.7 2.4 %collective-permute-done.9.refs_7_.refs_4_ = bf16[2048,128]{1,0:T(8,128)(2,1)S(1)} collective-permute-done((bf16[2048,128]{1,0:T(8,128)(2,1)S(1)}, bf16[2048,128]{1,0:T(8,128)(2,1)S(1)}, u32[]{:S(2)}, u32[]{:S(2)}) %collective-permute-start.9) | collective-permute-done | bytes 524320 | tf_op jit(solution)/shard_map/ppermute | solution.py:271
  53.1 1.5 %kept_near.1 = (f32[2048,128]{1,0:T(8,128)S(1)}, f32[2048,128]{1,0:T(8,128)S(1)}) custom-call(s32[1]{0:T(128)} %bitcast.role_ref, bf16[4,512,256]{2,1,0:T(8,128)(2,1)S(1)} %copy-done, bf16[2,2176,128]{2,1,0:T(8,128)(2,1)S(1)} %collective-permute-done.refs_0_, bf16[2,2176,128]{2,1,0:T(8,128)(2,1)S(1)} %collective-permute-done.1.refs_1_, ...), custom_call_target="tpu_custom_call" | custom-call | flops 20000000000 | bytes 67108864 | tf_op jit(solution)/shard_map/kept_near/pallas_call | solution.py:201
  54.6 4.1 %collective-permute-done.11.refs_3_ = bf16[2048,128]{1,0:T(8,128)(2,1)S(1)} collective-permute-done((bf16[2048,128]{1,0:T(8,128)(2,1)S(1)}, bf16[2048,128]{1,0:T(8,128)(2,1)S(1)}, u32[]{:S(2)}, u32[]{:S(2)}) %collective-permute-start.11) | collective-permute-done | bytes 524320 | tf_op jit(solution)/shard_map/ppermute | solution.py:271
  58.7 0.0 collective-permute-done.7.refs_2_.refs_0_
  58.7 2.0 %final.1.refs_2_ = bf16[2,128,4096]{2,1,0:T(8,128)(2,1)} custom-call(s32[1]{0:T(128)} %bitcast.role_ref, f32[2048,128]{1,0:T(8,128)S(1)} %get-tuple-element.45.refs_0_, f32[2048,128]{1,0:T(8,128)S(1)} %get-tuple-element.46.refs_1_, bf16[2,2048,128]{2,1,0:T(8,128)(2,1)S(1)} %collective-permute-done.7.refs_2_.refs_0_, ...), custom_call_target="tpu_custom_call" | custom-call | flops 1000 | bytes 1000 | tf_op jit(solution)/shard_map/final/pallas_call | solution.py:242
  60.7 2.9 %collective-permute-done.8.refs_1_ = bf16[2048,128]{1,0:T(8,128)(2,1)S(1)} collective-permute-done((bf16[2048,128]{1,0:T(8,128)(2,1)S(1)}, bf16[2048,128]{1,0:T(8,128)(2,1)S(1)}, u32[]{:S(2)}, u32[]{:S(2)}) %collective-permute-start.8) | collective-permute-done | bytes 524320 | tf_op jit(solution)/shard_map/ppermute | solution.py:271
  63.6 1.0 %final_edge.1 = bf16[2,128,4096]{2,1,0:T(8,128)(2,1)} custom-call(s32[1]{0:T(128)} %bitcast.role_ref, bf16[2,2048,128]{2,1,0:T(8,128)(2,1)S(1)} %collective-permute-done.7.refs_2_.refs_0_, bf16[2048,128]{1,0:T(8,128)(2,1)S(1)} %collective-permute-done.8.refs_1_, bf16[2,128,4096]{2,1,0:T(8,128)(2,1)} %final.1.refs_2_), custom_call_target="tpu_custom_call", output_to_operand_aliasing={{}: (3, {})} | custom-call | flops 1000 | bytes 1000 | tf_op jit(solution)/shard_map/final_edge/pallas_call | solution.py:242
  (1 shorter events, 0.0 us)
Async XLA Ops:
  3.3 10.7 %copy-start.1 = (bf16[2,2176,128]{2,1,0:T(8,128)(2,1)S(1)}, bf16[2,2176,128]{2,1,0:T(8,128)(2,1)}, u32[]{:S(2)}) copy-start(bf16[2,2176,128]{2,1,0:T(8,128)(2,1)} %get-tuple-element.26.refs_0_) | copy-start | bytes 3342340
  3.3 10.7 %collective-permute-start.2 = (bf16[2,2176,128]{2,1,0:T(8,128)(2,1)}, bf16[2,2176,128]{2,1,0:T(8,128)(2,1)}, u32[]{:S(2)}, u32[]{:S(2)}) collective-permute-start(bf16[2,2176,128]{2,1,0:T(8,128)(2,1)} %get-tuple-element.27), channel_id=1, source_target_pairs={{0,4},{1,5},{2,6},{3,7},{4,0},{5,1},{6,2},{7,3},{8,12},{9,13},{10,... | collective-permute-start | bytes 3342344 | tf_op jit(solution)/shard_map/ppermute | solution.py:271
  3.8 23.5 %collective-permute-start = (bf16[2,2176,128]{2,1,0:T(8,128)(2,1)}, bf16[2,2176,128]{2,1,0:T(8,128)(2,1)S(1)}, u32[]{:S(2)}, u32[]{:S(2)}) collective-permute-start(bf16[2,2176,128]{2,1,0:T(8,128)(2,1)} %get-tuple-element.26.refs_0_), channel_id=1, source_target_pairs={{0,1},{1,0},{2,3},{3,2},{4,6},{5,7},{6,4},{7,5},{8,9},{9,8},{10,11... | collective-permute-start | bytes 3342344 | tf_op jit(solution)/shard_map/ppermute | solution.py:271
  6.4 16.8 %collective-permute-start.3 = (bf16[2176,128]{1,0:T(8,128)(2,1)}, bf16[2176,128]{1,0:T(8,128)(2,1)}, u32[]{:S(2)}, u32[]{:S(2)}) collective-permute-start(bf16[2176,128]{1,0:T(8,128)(2,1)} %get-tuple-element.29), channel_id=1, source_target_pairs={{0,28},{1,29},{2,30},{3,31},{4,8},{5,9},{6,10},{7,11},{8,4},{9,5},... | collective-permute-start | bytes 1671176 | tf_op jit(solution)/shard_map/ppermute | solution.py:271
  9.8 26.8 %collective-permute-start.1 = (bf16[2,2176,128]{2,1,0:T(8,128)(2,1)}, bf16[2,2176,128]{2,1,0:T(8,128)(2,1)S(1)}, u32[]{:S(2)}, u32[]{:S(2)}) collective-permute-start(bf16[2,2176,128]{2,1,0:T(8,128)(2,1)} %get-tuple-element.27), channel_id=1, source_target_pairs={{0,6},{1,7},{2,4},{3,5},{4,1},{5,0},{6,3},{7,2},{8,14},{9,15},{10,... | collective-permute-start | bytes 3342344 | tf_op jit(solution)/shard_map/ppermute | solution.py:271
  9.8 30.6 %collective-permute-start.6 = (bf16[2176,128]{1,0:T(8,128)(2,1)}, bf16[2176,128]{1,0:T(8,128)(2,1)}, u32[]{:S(2)}, u32[]{:S(2)}) collective-permute-start(bf16[2176,128]{1,0:T(8,128)(2,1)} %get-tuple-element.32), channel_id=1, source_target_pairs={{0,24},{1,25},{2,26},{3,27},{4,12},{5,13},{6,14},{7,15},{8,0},{9,1... | collective-permute-start | bytes 1671176 | tf_op jit(solution)/shard_map/ppermute | solution.py:271
  14.0 1.2 %copy-start = (bf16[4,512,256]{2,1,0:T(8,128)(2,1)S(1)}, bf16[4,512,256]{2,1,0:T(8,128)(2,1)}, u32[]{:S(2)}) copy-start(bf16[4,512,256]{2,1,0:T(8,128)(2,1)} %weights.1.weight_ref) | copy-start | bytes 3145732
  27.3 17.6 %collective-permute-start.4 = (bf16[2176,128]{1,0:T(8,128)(2,1)}, bf16[2176,128]{1,0:T(8,128)(2,1)S(1)}, u32[]{:S(2)}, u32[]{:S(2)}) collective-permute-start(bf16[2176,128]{1,0:T(8,128)(2,1)} %collective-permute-done.3.refs_2_), channel_id=1, source_target_pairs={{0,1},{1,0},{2,3},{3,2},{4,6},{5,7},{6,4},{7,5},{8,9},{9,8},{10,11... | collective-permute-start | bytes 1671176 | tf_op jit(solution)/shard_map/ppermute | solution.py:271
  29.7 18.2 %collective-permute-start.5 = (bf16[2176,128]{1,0:T(8,128)(2,1)S(1)}, bf16[2176,128]{1,0:T(8,128)(2,1)S(1)}, u32[]{:S(2)}, u32[]{:S(2)}) collective-permute-start(bf16[2176,128]{1,0:T(8,128)(2,1)S(1)} %slice_bitcast_fusion), channel_id=1, source_target_pairs={{0,24},{1,25},{2,26},{3,27},{4,12},{5,13},{6,14},{7,15},{8,0},{9,1... | collective-permute-start | bytes 1671176 | tf_op jit(solution)/shard_map/ppermute | solution.py:271
  38.1 12.6 %collective-permute-start.10 = (bf16[2048,128]{1,0:T(8,128)(2,1)S(1)}, bf16[2048,128]{1,0:T(8,128)(2,1)S(1)}, u32[]{:S(2)}, u32[]{:S(2)}) collective-permute-start(bf16[2048,128]{1,0:T(8,128)(2,1)S(1)} %get-tuple-element.44), channel_id=1, source_target_pairs={{0,6},{1,7},{2,4},{3,5},{4,1},{5,0},{6,3},{7,2},{8,14},{9,15},{10,... | collective-permute-start | bytes 1572872 | tf_op jit(solution)/shard_map/ppermute | solution.py:271
  38.2 14.9 %collective-permute-start.9 = (bf16[2048,128]{1,0:T(8,128)(2,1)S(1)}, bf16[2048,128]{1,0:T(8,128)(2,1)S(1)}, u32[]{:S(2)}, u32[]{:S(2)}) collective-permute-start(bf16[2048,128]{1,0:T(8,128)(2,1)S(1)} %get-tuple-element.35.refs_4_), channel_id=1, source_target_pairs={{0,2},{1,3},{2,0},{3,1},{4,5},{5,4},{6,7},{7,6},{8,10},{9,11},{10,... | collective-permute-start | bytes 1572872 | tf_op jit(solution)/shard_map/ppermute | solution.py:271
  45.7 13.0 %collective-permute-start.11 = (bf16[2048,128]{1,0:T(8,128)(2,1)S(1)}, bf16[2048,128]{1,0:T(8,128)(2,1)S(1)}, u32[]{:S(2)}, u32[]{:S(2)}) collective-permute-start(bf16[2048,128]{1,0:T(8,128)(2,1)S(1)} %sent_near.1.refs_7_.refs_6_), channel_id=1, source_target_pairs={{0,2},{1,3},{2,0},{3,1},{4,5},{5,4},{6,7},{7,6},{8,10},{9,11},{10,... | collective-permute-start | bytes 1572872 | tf_op jit(solution)/shard_map/ppermute | solution.py:271
  50.3 8.4 %collective-permute-start.7 = (bf16[2,2048,128]{2,1,0:T(8,128)(2,1)S(1)}, bf16[2,2048,128]{2,1,0:T(8,128)(2,1)S(1)}, u32[]{:S(2)}, u32[]{:S(2)}) collective-permute-start(bf16[2,2048,128]{2,1,0:T(8,128)(2,1)S(1)} %get-tuple-element.40), channel_id=1, source_target_pairs={{0,4},{1,5},{2,6},{3,7},{4,0},{5,1},{6,2},{7,3},{8,12},{9,13},{10,... | collective-permute-start | bytes 3145736 | tf_op jit(solution)/shard_map/ppermute | solution.py:271
  50.4 13.2 %collective-permute-start.8 = (bf16[2048,128]{1,0:T(8,128)(2,1)S(1)}, bf16[2048,128]{1,0:T(8,128)(2,1)S(1)}, u32[]{:S(2)}, u32[]{:S(2)}) collective-permute-start(bf16[2048,128]{1,0:T(8,128)(2,1)S(1)} %get-tuple-element.41), channel_id=1, source_target_pairs={{0,6},{1,7},{2,4},{3,5},{4,1},{5,0},{6,3},{7,2},{8,14},{9,15},{10,... | collective-permute-start | bytes 1572872 | tf_op jit(solution)/shard_map/ppermute | solution.py:271

commit v5 on v4

--- a/solution.py
+++ b/solution.py
@@ -79,7 +79,9 @@
     )(role, jnp.asarray(index), jnp.asarray(scale), radial.reshape(20, CS, CS))
 
 
-def turn_kernel(role_ref, field_ref, keep_ref, give_ref, keep_edge_ref, give_edge_ref, raw, turned, in_sems, out_sems):
+def turn_kernel(
+    role_ref, field_ref, keep_ref, give_ref, keep_edge_ref, give_edge_ref, give_inner_ref, raw, turned, in_sems, out_sems
+):
     odd = role_ref[0] % 2
     quarter = HALF // 2
     loads, stores = [], []
@@ -105,6 +107,8 @@
         wanted = [(given, give_ref.at[p]), (kept, keep_ref.at[p])]
         if p == 0:
             wanted += [(given, give_edge_ref), (kept, keep_edge_ref)]
+        else:
+            wanted += [(given, give_inner_ref)]
         for source, target in wanted:
             copy = pltpu.make_async_copy(source, target, out_sems.at[len(stores)])
             copy.start()
@@ -119,14 +123,14 @@
     hbm = pl.BlockSpec(memory_space=pl.ANY)
     return pl.pallas_call(
         turn_kernel,
-        out_shape=(double, double, single, single),
+        out_shape=(double, double, single, single, single),
         in_specs=[pl.BlockSpec(memory_space=pltpu.SMEM), hbm],
-        out_specs=(hbm,) * 4,
+        out_specs=(hbm,) * 5,
         scratch_shapes=[
             pltpu.VMEM((2, CS, 2 * HALF), jnp.bfloat16),
             pltpu.VMEM((2, 2 * HALF + 2 * ROW, CS), jnp.bfloat16),
             pltpu.SemaphoreType.DMA((8,)),
-            pltpu.SemaphoreType.DMA((6,)),
+            pltpu.SemaphoreType.DMA((7,)),
         ],
         compiler_params=pltpu.CompilerParams(vmem_limit_bytes=TURN_VMEM),
         cost_estimate=COST,
@@ -297,16 +301,20 @@
         return permute(value, lambda z, k, c: (2 * outward(z, k) + k, c))
 
     f32, bf16 = jnp.float32, jnp.bfloat16
-    keep, give, keep_edge, give_edge = turn(role, field)
+    def gather_cross(value):
+        return permute(value, lambda z, k, c: (2 * z + 1 - k, gather_group(1 - k, c)))
+
+    keep, give, keep_edge, give_edge, give_inner = turn(role, field)
     near = gather_near(keep)
     halo_near = permute(give_edge, lambda z, k, c: (2 * outward(z, k) + 1 - k, c))
     halo_far = from_far(keep_edge)
-    near_others = permute(give, lambda z, k, c: (2 * z + 1 - k, gather_group(1 - k, c)))
     others = swap(give)
-    weight = weights(role, radial)
-
-    inner = {1: (0, 0), 2: (0, 1), 4: (1, 0), 3: (1, 1)}
-    all_planes = inner | {0: (2, 0), 5: (3, 0)}
+    weight, give_inner = lax.optimization_barrier((weights(role, radial), give_inner))
+    near3 = gather_cross(give_inner)
+
+    own_inner = {1: (0, 0), 2: (0, 1), 4: (1, 0), 3: (1, 1)}
+    own_all = own_inner | {0: (2, 0), 5: (3, 0)}
+    near_all = {1: (0, 0), 2: (0, 1), 3: (1, 0), 4: (2, 0), 0: (3, 0), 5: (4, 0)}
 
     def jobs(of, *wanted):
         return [(tuple(of[at] for at in (plane - 1, plane, plane + 1)), slot, acc) for plane, slot, acc in wanted]
@@ -314,32 +322,37 @@
     own = [keep, others]
     kept2, kept3, lent2, lent3 = conv(
         "own_inner", role, weight, own, [],
-        jobs(inner, (2, 0, None), (3, 0, None), (2, 1, None), (3, 1, None)), [f32] * 4,
-    )
-    kept2, near_ready, halo_ready = lax.optimization_barrier((kept2, near, halo_near))
-    near_halo = gather_near(halo_ready)
-    far_halo = from_far(near_ready[0])
-    near = [near, near_others]
-    sent2, sent3 = conv(
-        "sent_inner", role, weight, near, [lent2, lent3], jobs(inner, (2, 2, 0), (3, 2, 1)), [bf16] * 2,
-    )
-    got2, got3 = reduce_near(sent2), reduce_far(sent3)
+        jobs(own_inner, (2, 0, None), (3, 0, None), (2, 1, None), (3, 1, None)), [f32] * 4,
+    )
+    kept2, near, give_edge = lax.optimization_barrier((kept2, near, give_edge))
+    near4 = gather_cross(give_edge)
+    far_halo = from_far(near[0])
+    sent2, = conv(
+        "sent_2", role, weight, [near, near3], [lent2], jobs(near_all, (2, 2, 0)), [bf16], cost=LONG,
+    )
+    got2 = reduce_near(sent2)
+    near_halo = gather_near(halo_near)
+    near = [near, near3, near4]
+    sent3, = conv(
+        "sent_3", role, weight, near, [lent3], jobs(near_all, (3, 2, 0)), [bf16], after=[sent2],
+    )
+    got3 = reduce_far(sent3)
     kept1, kept4, lent1, lent4 = conv(
         "own_boundary", role, weight, [*own, halo_near, halo_far], [],
-        jobs(all_planes, (1, 0, None), (4, 0, None), (1, 1, None), (4, 1, None)), [f32] * 4, after=[sent2],
+        jobs(own_all, (1, 0, None), (4, 0, None), (1, 1, None), (4, 1, None)), [f32] * 4, after=[sent3],
     )
     near = [*near, near_halo, far_halo]
     sent1, = conv(
-        "sent_near", role, weight, near[:3], [lent1], jobs(all_planes, (1, 2, 0)), [bf16],
+        "sent_near", role, weight, near[:4], [lent1], jobs(near_all, (1, 2, 0)), [bf16],
     )
     sent4, total = conv(
         "far", role, weight, near, [lent4, kept4, kept3],
-        jobs(all_planes, (4, 2, 0), (4, 3, 1), (3, 3, 2)), [bf16] * 2, after=[sent1],
+        jobs(near_all, (4, 2, 0), (4, 3, 1), (3, 3, 2)), [bf16] * 2, after=[sent1],
     )
     got1, got4, crossed = reduce_near(sent1), reduce_far(sent4), swap(total)
     total1, total2 = conv(
         "kept_near", role, weight, near, [kept1, kept2],
-        jobs(all_planes, (1, 3, 0), (2, 3, 1)), [f32] * 2, after=[sent1, got2, got3], cost=LONG,
+        jobs(near_all, (1, 3, 0), (2, 3, 1)), [f32] * 2, after=[sent1, got2, got3], cost=LONG,
     )
     out = final(
         "final", role, [(0, 0), (1, 0), (1, 1)], [total1, total2, (crossed, 1)], [got1, got2, got3]

time: 65 us -> 62.8 us (0.966)
  starting transfers between devices: 20.1 us -> 17.3 us
  waiting for transfers between devices: 19.7 us -> 21.9 us
  Pallas kernels: 23.5 us -> 22 us
    ppermute x12 -> x13, starting transfers between devices: 20.1 us -> 17.3 us  [permute(): return lax.ppermute(value, ('space', 'chan'), pairs)]
    ppermute x12 -> x13, waiting for transfers between devices: 19.7 us -> 21.9 us  [permute(): return lax.ppermute(value, ('space', 'chan'), pairs)]
    pallas_call x6 -> x7, Pallas kernels: 14.7 us -> 13 us  [conv(): pl.pallas_call(functools.partial(conv_kernel, jobs, stacks, len(accs), le...]
  transfers between devices with their start and end apart: 12 -> 13, of which waited for: 6 -> 4; matrix products, arithmetic and copies ran while one was open for 0% -> 0% of each run, Pallas kernels for 30% -> 28%
where the time goes in v5:
time: 62.8 us; the launch traced here: 62.6 us
  Pallas kernels  22 us (35%)
  waiting for transfers between devices  21.9 us (35%)
  starting transfers between devices  17.3 us (28%)
  local copies, waits for them, and re-layouts  1.27 us (2%)
    ppermute x13, waiting for transfers between devices, permute(): return lax.ppermute(value, ('space', 'chan'), pairs)  21.9 us
    ppermute x13, starting transfers between devices, permute(): return lax.ppermute(value, ('space', 'chan'), pairs)  17.3 us
    pallas_call x7, Pallas kernels, conv(): pl.pallas_call(functools.partial(conv_kernel, jobs, stacks, len(accs), le...  13 us
    pallas_call x1, Pallas kernels, turn(): pl.pallas_call(turn_kernel, out_shape=(double, double, single, single, si...  3.5 us
    pallas_call x2, Pallas kernels, final(): pl.pallas_call(functools.partial(final_kernel, len(places)), out_shape=ja...  2.99 us
    pallas_call x1, Pallas kernels, weights(): pl.pallas_call(weights_kernel, out_shape=jax.ShapeDtypeStruct((4, 4 * CS,...  2.49 us
  transfers between devices with their start and end apart: 13, of which 4 were waited for; matrix products, arithmetic and copies ran while one was open for 0% of the time, Pallas kernels for 28%

profile of v5, /device:TPU:0, one launch (start us, length us, event | category | flops | bytes accessed | tf_op | source)
XLA Modules:
  0.0 62.6 jit_solution(8142481386877564437)
XLA Ops:
  0.0 3.5 %turn.1 = (bf16[2,2176,128]{2,1,0:T(8,128)(2,1)}, bf16[2,2176,128]{2,1,0:T(8,128)(2,1)}, bf16[2176,128]{1,0:T(8,128)(2,1)}, bf16[2176,128]{1,0:T(8,128)(2,1)}, bf16[2176,128]{1,0:T(8,128)(2,1)}) custom-call(s32[1]{0:T(128)} %bitcast.role_ref, bf16[2,128,4096]{2,1,0:T(8,128)(2,1)} %field_ref.1), custom_call_target="tpu_custom_call" | custom-call | flops 1000 | bytes 1000 | tf_op jit(solution)/shard_map/turn/pallas_call | solution.py:124
  3.5 0.0 copy-start.1
  3.5 0.5 collective-permute-start
  4.0 2.6 %collective-permute-start.1 = (bf16[2,2176,128]{2,1,0:T(8,128)(2,1)}, bf16[2,2176,128]{2,1,0:T(8,128)(2,1)S(1)}, u32[]{:S(2)}, u32[]{:S(2)}) collective-permute-start(bf16[2,2176,128]{2,1,0:T(8,128)(2,1)} %get-tuple-element.29.refs_0_), channel_id=1, source_target_pairs={{0,1},{1,0},{2,3},{3,2},{4,6},{5,7},{6,4},{7,5},{8,9},{9,8},{10,11... | collective-permute-start | bytes 3342344 | tf_op jit(solution)/shard_map/ppermute | solution.py:275
  6.6 3.4 %collective-permute-start.4 = (bf16[2176,128]{1,0:T(8,128)(2,1)}, bf16[2176,128]{1,0:T(8,128)(2,1)}, u32[]{:S(2)}, u32[]{:S(2)}) collective-permute-start(bf16[2176,128]{1,0:T(8,128)(2,1)} %get-tuple-element.35), channel_id=1, source_target_pairs={{0,28},{1,29},{2,30},{3,31},{4,8},{5,9},{6,10},{7,11},{8,4},{9,5},... | collective-permute-start | bytes 1671176 | tf_op jit(solution)/shard_map/ppermute | solution.py:275
  10.0 2.5 %weights.1.weight_ref = bf16[4,512,256]{2,1,0:T(8,128)(2,1)} custom-call(s32[1]{0:T(128)} %bitcast.role_ref, s32[8,64]{1,0:T(8,128)} %constant.37.clone.index_ref, f32[8,64]{1,0:T(8,128)} %constant.38.clone.scale_ref, bf16[20,128,128]{2,1,0:T(8,128)(2,1)} %bitcast.4), custom_call_target="tpu_custom_call" | custom-call | flops 1000 | bytes 1000 | tf_op jit(solution)/shard_map/weights/pallas_call | solution.py:72
  12.5 0.0 collective-permute-start.2
  12.5 1.7 %collective-permute-start.7 = (bf16[2176,128]{1,0:T(8,128)(2,1)}, bf16[2176,128]{1,0:T(8,128)(2,1)S(1)}, u32[]{:S(2)}, u32[]{:S(2)}) collective-permute-start(bf16[2176,128]{1,0:T(8,128)(2,1)} %get-tuple-element.36), channel_id=1, source_target_pairs={{0,24},{1,25},{2,26},{3,27},{4,12},{5,13},{6,14},{7,15},{8,0},{9,1... | collective-permute-start | bytes 1671176 | tf_op jit(solution)/shard_map/ppermute | solution.py:275
  14.2 9.2 %collective-permute-done.4.refs_2_ = bf16[2176,128]{1,0:T(8,128)(2,1)} collective-permute-done((bf16[2176,128]{1,0:T(8,128)(2,1)}, bf16[2176,128]{1,0:T(8,128)(2,1)}, u32[]{:S(2)}, u32[]{:S(2)}) %collective-permute-start.4) | collective-permute-done | bytes 557088 | tf_op jit(solution)/shard_map/ppermute | solution.py:275
  23.4 1.5 %collective-permute-start.5 = (bf16[2176,128]{1,0:T(8,128)(2,1)}, bf16[2176,128]{1,0:T(8,128)(2,1)S(1)}, u32[]{:S(2)}, u32[]{:S(2)}) collective-permute-start(bf16[2176,128]{1,0:T(8,128)(2,1)} %collective-permute-done.4.refs_2_), channel_id=1, source_target_pairs={{0,1},{1,0},{2,3},{3,2},{4,6},{5,7},{6,4},{7,5},{8,9},{9,8},{10,11... | collective-permute-start | bytes 1671176 | tf_op jit(solution)/shard_map/ppermute | solution.py:275
  24.9 0.0 collective-permute-done.refs_1_
  24.9 0.0 copy-done.1
  24.9 0.0 copy-start
  24.9 1.2 %copy-done = bf16[4,512,256]{2,1,0:T(8,128)(2,1)S(1)} copy-done((bf16[4,512,256]{2,1,0:T(8,128)(2,1)S(1)}, bf16[4,512,256]{2,1,0:T(8,128)(2,1)}, u32[]{:S(2)}) %copy-start) | copy-done | bytes 1048600
  26.1 0.0 copy-start.2
  26.1 2.7 %own_inner.1 = (f32[2048,128]{1,0:T(8,128)S(1)}, f32[2048,128]{1,0:T(8,128)S(1)}, f32[2048,128]{1,0:T(8,128)S(1)}, f32[2048,128]{1,0:T(8,128)S(1)}) custom-call(s32[1]{0:T(128)} %bitcast.role_ref, bf16[4,512,256]{2,1,0:T(8,128)(2,1)S(1)} %copy-done, bf16[2,2176,128]{2,1,0:T(8,128)(2,1)S(1)} %copy-done.1, bf16[2,2176,128]{2,1,0:T(8,128)(2,1)S(1)} %collective-permute-done.refs_1_), custom_call_target="tpu_custom_call" | custom-call | flops 1000 | bytes 1000 | tf_op jit(solution)/shard_map/own_inner/pallas_call | solution.py:205
  28.8 0.0 collective-permute-done.1.refs_0_
  28.9 0.0 copy-done.2
  28.9 0.1 collective-permute-start.3
  29.0 3.6 %collective-permute-start.6 = (bf16[2176,128]{1,0:T(8,128)(2,1)S(1)}, bf16[2176,128]{1,0:T(8,128)(2,1)S(1)}, u32[]{:S(2)}, u32[]{:S(2)}) collective-permute-start(bf16[2176,128]{1,0:T(8,128)(2,1)S(1)} %slice_bitcast_fusion), channel_id=1, source_target_pairs={{0,24},{1,25},{2,26},{3,27},{4,12},{5,13},{6,14},{7,15},{8,0},{9,1... | collective-permute-start | bytes 1671176 | tf_op jit(solution)/shard_map/ppermute | solution.py:275
  32.6 0.0 collective-permute-done.2.refs_1_
  32.6 0.8 %sent_2.1.refs_4_ = bf16[2048,128]{1,0:T(8,128)(2,1)S(1)} custom-call(s32[1]{0:T(128)} %bitcast.role_ref, bf16[4,512,256]{2,1,0:T(8,128)(2,1)S(1)} %copy-done, bf16[2,2176,128]{2,1,0:T(8,128)(2,1)S(1)} %collective-permute-done.1.refs_0_, bf16[2176,128]{1,0:T(8,128)(2,1)S(1)} %collective-permute-done.2.refs_1_, f32[2048,128]{1,0:T(8,128)S(1)} %get-tuple-element.38.refs_2_), custom_call_target="tpu_custom_call" | custom-call | flops 20000000000 | bytes 67108864 | tf_op jit(solution)/shard_map/sent_2/pallas_call | solution.py:205
  33.4 0.7 %collective-permute-start.10 = (bf16[2048,128]{1,0:T(8,128)(2,1)S(1)}, bf16[2048,128]{1,0:T(8,128)(2,1)S(1)}, u32[]{:S(2)}, u32[]{:S(2)}) collective-permute-start(bf16[2048,128]{1,0:T(8,128)(2,1)S(1)} %sent_2.1.refs_4_), channel_id=1, source_target_pairs={{0,2},{1,3},{2,0},{3,1},{4,5},{5,4},{6,7},{7,6},{8,10},{9,11},{10,... | collective-permute-start | bytes 1572872 | tf_op jit(solution)/shard_map/ppermute | solution.py:275
  34.1 5.0 %collective-permute-done.3.refs_2_ = bf16[2176,128]{1,0:T(8,128)(2,1)S(1)} collective-permute-done((bf16[2176,128]{1,0:T(8,128)(2,1)S(1)}, bf16[2176,128]{1,0:T(8,128)(2,1)S(1)}, u32[]{:S(2)}, u32[]{:S(2)}) %collective-permute-start.3) | collective-permute-done | bytes 557088 | tf_op jit(solution)/shard_map/ppermute | solution.py:275
  39.1 0.8 %sent_3.1.refs_4_ = bf16[2048,128]{1,0:T(8,128)(2,1)S(1)} custom-call(s32[1]{0:T(128)} %bitcast.role_ref, bf16[4,512,256]{2,1,0:T(8,128)(2,1)S(1)} %copy-done, bf16[2,2176,128]{2,1,0:T(8,128)(2,1)S(1)} %collective-permute-done.1.refs_0_, bf16[2176,128]{1,0:T(8,128)(2,1)S(1)} %collective-permute-done.2.refs_1_, ...), custom_call_target="tpu_custom_call" | custom-call | flops 1000 | bytes 1000 | tf_op jit(solution)/shard_map/sent_3/pallas_call | solution.py:205
  39.9 0.2 collective-permute-start.11
  40.1 0.0 collective-permute-done.7.refs_3_
  40.1 4.0 %own_boundary.1 = (f32[2048,128]{1,0:T(8,128)S(1)}, f32[2048,128]{1,0:T(8,128)S(1)}, f32[2048,128]{1,0:T(8,128)S(1)}, f32[2048,128]{1,0:T(8,128)S(1)}) custom-call(s32[1]{0:T(128)} %bitcast.role_ref, bf16[4,512,256]{2,1,0:T(8,128)(2,1)S(1)} %copy-done, bf16[2,2176,128]{2,1,0:T(8,128)(2,1)S(1)} %copy-done.1, ...), custom_call_target="tpu_custom_call" | custom-call | flops 1000 | bytes 1000 | tf_op jit(solution)/shard_map/own_boundary/pallas_call | solution.py:205
  44.1 0.0 collective-permute-done.5.refs_3_
  44.1 0.8 %sent_near.1.refs_8_.refs_7_ = bf16[2048,128]{1,0:T(8,128)(2,1)S(1)} custom-call(s32[1]{0:T(128)} %bitcast.role_ref, bf16[4,512,256]{2,1,0:T(8,128)(2,1)S(1)} %copy-done, bf16[2,2176,128]{2,1,0:T(8,128)(2,1)S(1)} %collective-permute-done.1.refs_0_, bf16[2176,128]{1,0:T(8,128)(2,1)S(1)} %collective-permute-done.2.refs_1_, ...), custom_call_target="tpu_custom_call" | custom-call | flops 1000 | bytes 1000 | tf_op jit(solution)/shard_map/sent_near/pallas_call | solution.py:205
  44.9 1.1 %collective-permute-start.12 = (bf16[2048,128]{1,0:T(8,128)(2,1)S(1)}, bf16[2048,128]{1,0:T(8,128)(2,1)S(1)}, u32[]{:S(2)}, u32[]{:S(2)}) collective-permute-start(bf16[2048,128]{1,0:T(8,128)(2,1)S(1)} %sent_near.1.refs_8_.refs_7_), channel_id=1, source_target_pairs={{0,2},{1,3},{2,0},{3,1},{4,5},{5,4},{6,7},{7,6},{8,10},{9,11},{10,... | collective-permute-start | bytes 1572872 | tf_op jit(solution)/shard_map/ppermute | solution.py:275
  46.0 0.0 collective-permute-done.6.refs_4_
  46.0 2.4 %far.1 = (bf16[2048,128]{1,0:T(8,128)(2,1)S(1)}, bf16[2,2048,128]{2,1,0:T(8,128)(2,1)S(1)}) custom-call(s32[1]{0:T(128)} %bitcast.role_ref, bf16[4,512,256]{2,1,0:T(8,128)(2,1)S(1)} %copy-done, bf16[2,2176,128]{2,1,0:T(8,128)(2,1)S(1)} %collective-permute-done.1.refs_0_, bf16[2176,128]{1,0:T(8,128)(2,1)S(1)} %collective-permute-done.2.refs_1_, ...), custom_call_target="tpu_custom_call" | custom-call | flops 1000 | bytes 1000 | tf_op jit(solution)/shard_map/far/pallas_call | solution.py:205
  48.3 0.8 %collective-permute-start.8 = (bf16[2,2048,128]{2,1,0:T(8,128)(2,1)S(1)}, bf16[2,2048,128]{2,1,0:T(8,128)(2,1)S(1)}, u32[]{:S(2)}, u32[]{:S(2)}) collective-permute-start(bf16[2,2048,128]{2,1,0:T(8,128)(2,1)S(1)} %get-tuple-element.43), channel_id=1, source_target_pairs={{0,4},{1,5},{2,6},{3,7},{4,0},{5,1},{6,2},{7,3},{8,12},{9,13},{10,... | collective-permute-start | bytes 3145736 | tf_op jit(solution)/shard_map/ppermute | solution.py:275
  49.1 1.2 %collective-permute-start.9 = (bf16[2048,128]{1,0:T(8,128)(2,1)S(1)}, bf16[2048,128]{1,0:T(8,128)(2,1)S(1)}, u32[]{:S(2)}, u32[]{:S(2)}) collective-permute-start(bf16[2048,128]{1,0:T(8,128)(2,1)S(1)} %get-tuple-element.44), channel_id=1, source_target_pairs={{0,6},{1,7},{2,4},{3,5},{4,1},{5,0},{6,3},{7,2},{8,14},{9,15},{10,... | collective-permute-start | bytes 1572872 | tf_op jit(solution)/shard_map/ppermute | solution.py:275
  50.4 0.0 collective-permute-done.10.refs_8_.refs_4_
  50.4 0.0 collective-permute-done.11.refs_9_.refs_5_
  50.4 1.5 %kept_near.1 = (f32[2048,128]{1,0:T(8,128)S(1)}, f32[2048,128]{1,0:T(8,128)S(1)}) custom-call(s32[1]{0:T(128)} %bitcast.role_ref, bf16[4,512,256]{2,1,0:T(8,128)(2,1)S(1)} %copy-done, bf16[2,2176,128]{2,1,0:T(8,128)(2,1)S(1)} %collective-permute-done.1.refs_0_, bf16[2176,128]{1,0:T(8,128)(2,1)S(1)} %collective-permute-done.2.refs_1_, ...), custom_call_target="tpu_custom_call" | custom-call | flops 20000000000 | bytes 67108864 | tf_op jit(solution)/shard_map/kept_near/pallas_call | solution.py:205
  51.9 2.9 %collective-permute-done.12.refs_3_ = bf16[2048,128]{1,0:T(8,128)(2,1)S(1)} collective-permute-done((bf16[2048,128]{1,0:T(8,128)(2,1)S(1)}, bf16[2048,128]{1,0:T(8,128)(2,1)S(1)}, u32[]{:S(2)}, u32[]{:S(2)}) %collective-permute-start.12) | collective-permute-done | bytes 524320 | tf_op jit(solution)/shard_map/ppermute | solution.py:275
  54.8 0.0 collective-permute-done.8.refs_2_.refs_0_
  54.8 2.0 %final.1.refs_2_ = bf16[2,128,4096]{2,1,0:T(8,128)(2,1)} custom-call(s32[1]{0:T(128)} %bitcast.role_ref, f32[2048,128]{1,0:T(8,128)S(1)} %get-tuple-element.47.refs_0_, f32[2048,128]{1,0:T(8,128)S(1)} %get-tuple-element.48.refs_1_, bf16[2,2048,128]{2,1,0:T(8,128)(2,1)S(1)} %collective-permute-done.8.refs_2_.refs_0_, ...), custom_call_target="tpu_custom_call" | custom-call | flops 1000 | bytes 1000 | tf_op jit(solution)/shard_map/final/pallas_call | solution.py:246
  56.8 4.7 %collective-permute-done.9.refs_1_ = bf16[2048,128]{1,0:T(8,128)(2,1)S(1)} collective-permute-done((bf16[2048,128]{1,0:T(8,128)(2,1)S(1)}, bf16[2048,128]{1,0:T(8,128)(2,1)S(1)}, u32[]{:S(2)}, u32[]{:S(2)}) %collective-permute-start.9) | collective-permute-done | bytes 524320 | tf_op jit(solution)/shard_map/ppermute | solution.py:275
  61.6 1.0 %final_edge.1 = bf16[2,128,4096]{2,1,0:T(8,128)(2,1)} custom-call(s32[1]{0:T(128)} %bitcast.role_ref, bf16[2,2048,128]{2,1,0:T(8,128)(2,1)S(1)} %collective-permute-done.8.refs_2_.refs_0_, bf16[2048,128]{1,0:T(8,128)(2,1)S(1)} %collective-permute-done.9.refs_1_, bf16[2,128,4096]{2,1,0:T(8,128)(2,1)} %final.1.refs_2_), custom_call_target="tpu_custom_call", output_to_operand_aliasing={{}: (3, {})} | custom-call | flops 1000 | bytes 1000 | tf_op jit(solution)/shard_map/final_edge/pallas_call | solution.py:246
  (1 shorter events, 0.0 us)
Async XLA Ops:
  3.5 21.4 %copy-start.1 = (bf16[2,2176,128]{2,1,0:T(8,128)(2,1)S(1)}, bf16[2,2176,128]{2,1,0:T(8,128)(2,1)}, u32[]{:S(2)}) copy-start(bf16[2,2176,128]{2,1,0:T(8,128)(2,1)} %get-tuple-element.29.refs_0_) | copy-start | bytes 3342340
  3.5 21.4 %collective-permute-start = (bf16[2,2176,128]{2,1,0:T(8,128)(2,1)}, bf16[2,2176,128]{2,1,0:T(8,128)(2,1)S(1)}, u32[]{:S(2)}, u32[]{:S(2)}) collective-permute-start(bf16[2,2176,128]{2,1,0:T(8,128)(2,1)} %get-tuple-element.30), channel_id=1, source_target_pairs={{0,4},{1,5},{2,6},{3,7},{4,0},{5,1},{6,2},{7,3},{8,12},{9,13},{10,... | collective-permute-start | bytes 3342344 | tf_op jit(solution)/shard_map/ppermute | solution.py:275
  4.0 24.8 %collective-permute-start.1 = (bf16[2,2176,128]{2,1,0:T(8,128)(2,1)}, bf16[2,2176,128]{2,1,0:T(8,128)(2,1)S(1)}, u32[]{:S(2)}, u32[]{:S(2)}) collective-permute-start(bf16[2,2176,128]{2,1,0:T(8,128)(2,1)} %get-tuple-element.29.refs_0_), channel_id=1, source_target_pairs={{0,1},{1,0},{2,3},{3,2},{4,6},{5,7},{6,4},{7,5},{8,9},{9,8},{10,11... | collective-permute-start | bytes 3342344 | tf_op jit(solution)/shard_map/ppermute | solution.py:275
  6.6 16.8 %collective-permute-start.4 = (bf16[2176,128]{1,0:T(8,128)(2,1)}, bf16[2176,128]{1,0:T(8,128)(2,1)}, u32[]{:S(2)}, u32[]{:S(2)}) collective-permute-start(bf16[2176,128]{1,0:T(8,128)(2,1)} %get-tuple-element.35), channel_id=1, source_target_pairs={{0,28},{1,29},{2,30},{3,31},{4,8},{5,9},{6,10},{7,11},{8,4},{9,5},... | collective-permute-start | bytes 1671176 | tf_op jit(solution)/shard_map/ppermute | solution.py:275
  12.5 20.1 %collective-permute-start.2 = (bf16[2176,128]{1,0:T(8,128)(2,1)}, bf16[2176,128]{1,0:T(8,128)(2,1)S(1)}, u32[]{:S(2)}, u32[]{:S(2)}) collective-permute-start(bf16[2176,128]{1,0:T(8,128)(2,1)} %get-tuple-element.34), channel_id=1, source_target_pairs={{0,6},{1,7},{2,4},{3,5},{4,1},{5,0},{6,3},{7,2},{8,14},{9,15},{10,... | collective-permute-start | bytes 1671176 | tf_op jit(solution)/shard_map/ppermute | solution.py:275
  12.5 27.6 %collective-permute-start.7 = (bf16[2176,128]{1,0:T(8,128)(2,1)}, bf16[2176,128]{1,0:T(8,128)(2,1)S(1)}, u32[]{:S(2)}, u32[]{:S(2)}) collective-permute-start(bf16[2176,128]{1,0:T(8,128)(2,1)} %get-tuple-element.36), channel_id=1, source_target_pairs={{0,24},{1,25},{2,26},{3,27},{4,12},{5,13},{6,14},{7,15},{8,0},{9,1... | collective-permute-start | bytes 1671176 | tf_op jit(solution)/shard_map/ppermute | solution.py:275
  23.4 20.7 %collective-permute-start.5 = (bf16[2176,128]{1,0:T(8,128)(2,1)}, bf16[2176,128]{1,0:T(8,128)(2,1)S(1)}, u32[]{:S(2)}, u32[]{:S(2)}) collective-permute-start(bf16[2176,128]{1,0:T(8,128)(2,1)} %collective-permute-done.4.refs_2_), channel_id=1, source_target_pairs={{0,1},{1,0},{2,3},{3,2},{4,6},{5,7},{6,4},{7,5},{8,9},{9,8},{10,11... | collective-permute-start | bytes 1671176 | tf_op jit(solution)/shard_map/ppermute | solution.py:275
  24.9 1.2 %copy-start = (bf16[4,512,256]{2,1,0:T(8,128)(2,1)S(1)}, bf16[4,512,256]{2,1,0:T(8,128)(2,1)}, u32[]{:S(2)}) copy-start(bf16[4,512,256]{2,1,0:T(8,128)(2,1)} %weights.1.weight_ref) | copy-start | bytes 3145732
  26.1 2.7 %copy-start.2 = (bf16[2176,128]{1,0:T(8,128)(2,1)S(1)}, bf16[2176,128]{1,0:T(8,128)(2,1)}, u32[]{:S(2)}) copy-start(bf16[2176,128]{1,0:T(8,128)(2,1)} %get-tuple-element.35) | copy-start | bytes 1671172
  28.9 10.2 %collective-permute-start.3 = (bf16[2176,128]{1,0:T(8,128)(2,1)S(1)}, bf16[2176,128]{1,0:T(8,128)(2,1)S(1)}, u32[]{:S(2)}, u32[]{:S(2)}) collective-permute-start(bf16[2176,128]{1,0:T(8,128)(2,1)S(1)} %copy-done.2), channel_id=1, source_target_pairs={{0,6},{1,7},{2,4},{3,5},{4,1},{5,0},{6,3},{7,2},{8,14},{9,15},{10,... | collective-permute-start | bytes 1671176 | tf_op jit(solution)/shard_map/ppermute | solution.py:275
  29.0 17.0 %collective-permute-start.6 = (bf16[2176,128]{1,0:T(8,128)(2,1)S(1)}, bf16[2176,128]{1,0:T(8,128)(2,1)S(1)}, u32[]{:S(2)}, u32[]{:S(2)}) collective-permute-start(bf16[2176,128]{1,0:T(8,128)(2,1)S(1)} %slice_bitcast_fusion), channel_id=1, source_target_pairs={{0,24},{1,25},{2,26},{3,27},{4,12},{5,13},{6,14},{7,15},{8,0},{9,1... | collective-permute-start | bytes 1671176 | tf_op jit(solution)/shard_map/ppermute | solution.py:275
  33.4 17.0 %collective-permute-start.10 = (bf16[2048,128]{1,0:T(8,128)(2,1)S(1)}, bf16[2048,128]{1,0:T(8,128)(2,1)S(1)}, u32[]{:S(2)}, u32[]{:S(2)}) collective-permute-start(bf16[2048,128]{1,0:T(8,128)(2,1)S(1)} %sent_2.1.refs_4_), channel_id=1, source_target_pairs={{0,2},{1,3},{2,0},{3,1},{4,5},{5,4},{6,7},{7,6},{8,10},{9,11},{10,... | collective-permute-start | bytes 1572872 | tf_op jit(solution)/shard_map/ppermute | solution.py:275
  39.9 10.5 %collective-permute-start.11 = (bf16[2048,128]{1,0:T(8,128)(2,1)S(1)}, bf16[2048,128]{1,0:T(8,128)(2,1)S(1)}, u32[]{:S(2)}, u32[]{:S(2)}) collective-permute-start(bf16[2048,128]{1,0:T(8,128)(2,1)S(1)} %sent_3.1.refs_4_), channel_id=1, source_target_pairs={{0,6},{1,7},{2,4},{3,5},{4,1},{5,0},{6,3},{7,2},{8,14},{9,15},{10,... | collective-permute-start | bytes 1572872 | tf_op jit(solution)/shard_map/ppermute | solution.py:275
  44.9 9.9 %collective-permute-start.12 = (bf16[2048,128]{1,0:T(8,128)(2,1)S(1)}, bf16[2048,128]{1,0:T(8,128)(2,1)S(1)}, u32[]{:S(2)}, u32[]{:S(2)}) collective-permute-start(bf16[2048,128]{1,0:T(8,128)(2,1)S(1)} %sent_near.1.refs_8_.refs_7_), channel_id=1, source_target_pairs={{0,2},{1,3},{2,0},{3,1},{4,5},{5,4},{6,7},{7,6},{8,10},{9,11},{10,... | collective-permute-start | bytes 1572872 | tf_op jit(solution)/shard_map/ppermute | solution.py:275
  48.3 6.5 %collective-permute-start.8 = (bf16[2,2048,128]{2,1,0:T(8,128)(2,1)S(1)}, bf16[2,2048,128]{2,1,0:T(8,128)(2,1)S(1)}, u32[]{:S(2)}, u32[]{:S(2)}) collective-permute-start(bf16[2,2048,128]{2,1,0:T(8,128)(2,1)S(1)} %get-tuple-element.43), channel_id=1, source_target_pairs={{0,4},{1,5},{2,6},{3,7},{4,0},{5,1},{6,2},{7,3},{8,12},{9,13},{10,... | collective-permute-start | bytes 3145736 | tf_op jit(solution)/shard_map/ppermute | solution.py:275
  49.1 12.4 %collective-permute-start.9 = (bf16[2048,128]{1,0:T(8,128)(2,1)S(1)}, bf16[2048,128]{1,0:T(8,128)(2,1)S(1)}, u32[]{:S(2)}, u32[]{:S(2)}) collective-permute-start(bf16[2048,128]{1,0:T(8,128)(2,1)S(1)} %get-tuple-element.44), channel_id=1, source_target_pairs={{0,6},{1,7},{2,4},{3,5},{4,1},{5,0},{6,3},{7,2},{8,14},{9,15},{10,... | collective-permute-start | bytes 1572872 | tf_op jit(solution)/shard_map/ppermute | solution.py:275

commit v6 on v5

--- a/solution.py
+++ b/solution.py
@@ -83,24 +83,23 @@
     role_ref, field_ref, keep_ref, give_ref, keep_edge_ref, give_edge_ref, give_inner_ref, raw, turned, in_sems, out_sems
 ):
     odd = role_ref[0] % 2
-    quarter = HALF // 2
     loads, stores = [], []
     for p in range(2):
-        for q in range(4):
-            cells = slice(q * quarter, (q + 1) * quarter)
+        for q in range(2):
+            cells = slice(q * HALF, (q + 1) * HALF)
             copy = pltpu.make_async_copy(
-                field_ref.at[(p + odd) % 2, :, cells], raw.at[p, :, cells], in_sems.at[p * 4 + q]
+                field_ref.at[(p + odd) % 2, :, cells], raw.at[p, :, cells], in_sems.at[p * 2 + q]
             )
             copy.start()
             loads.append(copy)
     for p in range(2):
-        for q in range(4):
-            loads[p * 4 + q].wait()
-            block = jnp.transpose(raw[p, :, q * quarter : (q + 1) * quarter])
-            turned[p, ROW + q * quarter : ROW + (q + 1) * quarter] = block
+        for q in range(2):
+            loads[p * 2 + q].wait()
+            block = jnp.transpose(raw[p, :, q * HALF : (q + 1) * HALF])
+            turned[p, ROW + q * HALF : ROW + (q + 1) * HALF] = block
             if q == 0:
                 turned[p, ROW + 2 * HALF :] = block[:ROW]
-            if q == 3:
+            if q == 1:
                 turned[p, :ROW] = block[-ROW:]
         kept = turned.at[p, pl.ds(pl.multiple_of(odd * HALF, HALF), SLAB)]
         given = turned.at[p, pl.ds(pl.multiple_of((1 - odd) * HALF, HALF), SLAB)]
@@ -129,7 +128,7 @@
         scratch_shapes=[
             pltpu.VMEM((2, CS, 2 * HALF), jnp.bfloat16),
             pltpu.VMEM((2, 2 * HALF + 2 * ROW, CS), jnp.bfloat16),
-            pltpu.SemaphoreType.DMA((8,)),
+            pltpu.SemaphoreType.DMA((4,)),
             pltpu.SemaphoreType.DMA((7,)),
         ],
         compiler_params=pltpu.CompilerParams(vmem_limit_bytes=TURN_VMEM),
@@ -345,9 +344,12 @@
     sent1, = conv(
         "sent_near", role, weight, near[:4], [lent1], jobs(near_all, (1, 2, 0)), [bf16],
     )
-    sent4, total = conv(
-        "far", role, weight, near, [lent4, kept4, kept3],
-        jobs(near_all, (4, 2, 0), (4, 3, 1), (3, 3, 2)), [bf16] * 2, after=[sent1],
+    sent4, = conv(
+        "sent_far", role, weight, near, [lent4], jobs(near_all, (4, 2, 0)), [bf16], after=[sent1],
+    )
+    total, = conv(
+        "kept_far", role, weight, near, [kept4, kept3],
+        jobs(near_all, (4, 3, 0), (3, 3, 1)), [bf16], after=[sent4],
     )
     got1, got4, crossed = reduce_near(sent1), reduce_far(sent4), swap(total)
     total1, total2 = conv(

time: 62.8 us -> 62.7 us (level)
    pallas_call x7 -> x8, Pallas kernels: 13 us -> 13 us  [conv(): pl.pallas_call(functools.partial(conv_kernel, jobs, stacks, len(accs), le...]
where the time goes in v6:
time: 62.7 us; the launch traced here: 62.5 us
  Pallas kernels  21.9 us (35%)
  waiting for transfers between devices  21.8 us (35%)
  starting transfers between devices  17.3 us (28%)
  local copies, waits for them, and re-layouts  1.27 us (2%)
    ppermute x13, waiting for transfers between devices, permute(): return lax.ppermute(value, ('space', 'chan'), pairs)  21.8 us
    ppermute x13, starting transfers between devices, permute(): return lax.ppermute(value, ('space', 'chan'), pairs)  17.3 us
    pallas_call x8, Pallas kernels, conv(): pl.pallas_call(functools.partial(conv_kernel, jobs, stacks, len(accs), le...  13 us
    pallas_call x1, Pallas kernels, turn(): pl.pallas_call(turn_kernel, out_shape=(double, double, single, single, si...  3.43 us
    pallas_call x2, Pallas kernels, final(): pl.pallas_call(functools.partial(final_kernel, len(places)), out_shape=ja...  2.99 us
    pallas_call x1, Pallas kernels, weights(): pl.pallas_call(weights_kernel, out_shape=jax.ShapeDtypeStruct((4, 4 * CS,...  2.48 us
  transfers between devices with their start and end apart: 13, of which 4 were waited for; matrix products, arithmetic and copies ran while one was open for 0% of the time, Pallas kernels for 28%

profile of v6, /device:TPU:0, one launch (start us, length us, event | category | flops | bytes accessed | tf_op | source)
XLA Modules:
  0.0 62.5 jit_solution(6939395761613962014)
XLA Ops:
  0.0 3.4 %turn.1 = (bf16[2,2176,128]{2,1,0:T(8,128)(2,1)}, bf16[2,2176,128]{2,1,0:T(8,128)(2,1)}, bf16[2176,128]{1,0:T(8,128)(2,1)}, bf16[2176,128]{1,0:T(8,128)(2,1)}, bf16[2176,128]{1,0:T(8,128)(2,1)}) custom-call(s32[1]{0:T(128)} %bitcast.role_ref, bf16[2,128,4096]{2,1,0:T(8,128)(2,1)} %field_ref.1), custom_call_target="tpu_custom_call" | custom-call | flops 1000 | bytes 1000 | tf_op jit(solution)/shard_map/turn/pallas_call | solution.py:123
  3.4 0.0 copy-start.1
  3.5 0.5 collective-permute-start
  4.0 2.6 %collective-permute-start.1 = (bf16[2,2176,128]{2,1,0:T(8,128)(2,1)}, bf16[2,2176,128]{2,1,0:T(8,128)(2,1)S(1)}, u32[]{:S(2)}, u32[]{:S(2)}) collective-permute-start(bf16[2,2176,128]{2,1,0:T(8,128)(2,1)} %get-tuple-element.27.refs_0_), channel_id=1, source_target_pairs={{0,1},{1,0},{2,3},{3,2},{4,6},{5,7},{6,4},{7,5},{8,9},{9,8},{10,11... | collective-permute-start | bytes 3342344 | tf_op jit(solution)/shard_map/ppermute | solution.py:274
  6.5 3.4 %collective-permute-start.4 = (bf16[2176,128]{1,0:T(8,128)(2,1)}, bf16[2176,128]{1,0:T(8,128)(2,1)}, u32[]{:S(2)}, u32[]{:S(2)}) collective-permute-start(bf16[2176,128]{1,0:T(8,128)(2,1)} %get-tuple-element.33), channel_id=1, source_target_pairs={{0,28},{1,29},{2,30},{3,31},{4,8},{5,9},{6,10},{7,11},{8,4},{9,5},... | collective-permute-start | bytes 1671176 | tf_op jit(solution)/shard_map/ppermute | solution.py:274
  9.9 2.5 %weights.1.weight_ref = bf16[4,512,256]{2,1,0:T(8,128)(2,1)} custom-call(s32[1]{0:T(128)} %bitcast.role_ref, s32[8,64]{1,0:T(8,128)} %constant.37.clone.index_ref, f32[8,64]{1,0:T(8,128)} %constant.38.clone.scale_ref, bf16[20,128,128]{2,1,0:T(8,128)(2,1)} %bitcast.4), custom_call_target="tpu_custom_call" | custom-call | flops 1000 | bytes 1000 | tf_op jit(solution)/shard_map/weights/pallas_call | solution.py:72
  12.4 0.0 collective-permute-start.2
  12.4 1.7 %collective-permute-start.7 = (bf16[2176,128]{1,0:T(8,128)(2,1)}, bf16[2176,128]{1,0:T(8,128)(2,1)S(1)}, u32[]{:S(2)}, u32[]{:S(2)}) collective-permute-start(bf16[2176,128]{1,0:T(8,128)(2,1)} %get-tuple-element.34), channel_id=1, source_target_pairs={{0,24},{1,25},{2,26},{3,27},{4,12},{5,13},{6,14},{7,15},{8,0},{9,1... | collective-permute-start | bytes 1671176 | tf_op jit(solution)/shard_map/ppermute | solution.py:274
  14.1 9.2 %collective-permute-done.4.refs_2_ = bf16[2176,128]{1,0:T(8,128)(2,1)} collective-permute-done((bf16[2176,128]{1,0:T(8,128)(2,1)}, bf16[2176,128]{1,0:T(8,128)(2,1)}, u32[]{:S(2)}, u32[]{:S(2)}) %collective-permute-start.4) | collective-permute-done | bytes 557088 | tf_op jit(solution)/shard_map/ppermute | solution.py:274
  23.3 1.5 %collective-permute-start.5 = (bf16[2176,128]{1,0:T(8,128)(2,1)}, bf16[2176,128]{1,0:T(8,128)(2,1)S(1)}, u32[]{:S(2)}, u32[]{:S(2)}) collective-permute-start(bf16[2176,128]{1,0:T(8,128)(2,1)} %collective-permute-done.4.refs_2_), channel_id=1, source_target_pairs={{0,1},{1,0},{2,3},{3,2},{4,6},{5,7},{6,4},{7,5},{8,9},{9,8},{10,11... | collective-permute-start | bytes 1671176 | tf_op jit(solution)/shard_map/ppermute | solution.py:274
  24.8 0.0 collective-permute-done.refs_1_
  24.8 0.0 copy-done.1
  24.8 0.0 copy-start
  24.8 1.2 %copy-done = bf16[4,512,256]{2,1,0:T(8,128)(2,1)S(1)} copy-done((bf16[4,512,256]{2,1,0:T(8,128)(2,1)S(1)}, bf16[4,512,256]{2,1,0:T(8,128)(2,1)}, u32[]{:S(2)}) %copy-start) | copy-done | bytes 1048600
  26.0 0.0 copy-start.2
  26.1 2.7 %own_inner.1 = (f32[2048,128]{1,0:T(8,128)S(1)}, f32[2048,128]{1,0:T(8,128)S(1)}, f32[2048,128]{1,0:T(8,128)S(1)}, f32[2048,128]{1,0:T(8,128)S(1)}) custom-call(s32[1]{0:T(128)} %bitcast.role_ref, bf16[4,512,256]{2,1,0:T(8,128)(2,1)S(1)} %copy-done, bf16[2,2176,128]{2,1,0:T(8,128)(2,1)S(1)} %copy-done.1, bf16[2,2176,128]{2,1,0:T(8,128)(2,1)S(1)} %collective-permute-done.refs_1_), custom_call_target="tpu_custom_call" | custom-call | flops 1000 | bytes 1000 | tf_op jit(solution)/shard_map/own_inner/pallas_call | solution.py:204
  28.8 0.0 collective-permute-done.1.refs_0_
  28.8 0.0 copy-done.2
  28.8 0.1 collective-permute-start.3
  28.9 3.6 %collective-permute-start.6 = (bf16[2176,128]{1,0:T(8,128)(2,1)S(1)}, bf16[2176,128]{1,0:T(8,128)(2,1)S(1)}, u32[]{:S(2)}, u32[]{:S(2)}) collective-permute-start(bf16[2176,128]{1,0:T(8,128)(2,1)S(1)} %slice_bitcast_fusion), channel_id=1, source_target_pairs={{0,24},{1,25},{2,26},{3,27},{4,12},{5,13},{6,14},{7,15},{8,0},{9,1... | collective-permute-start | bytes 1671176 | tf_op jit(solution)/shard_map/ppermute | solution.py:274
  32.5 0.0 collective-permute-done.2.refs_1_
  32.5 0.8 %sent_2.1.refs_4_ = bf16[2048,128]{1,0:T(8,128)(2,1)S(1)} custom-call(s32[1]{0:T(128)} %bitcast.role_ref, bf16[4,512,256]{2,1,0:T(8,128)(2,1)S(1)} %copy-done, bf16[2,2176,128]{2,1,0:T(8,128)(2,1)S(1)} %collective-permute-done.1.refs_0_, bf16[2176,128]{1,0:T(8,128)(2,1)S(1)} %collective-permute-done.2.refs_1_, f32[2048,128]{1,0:T(8,128)S(1)} %get-tuple-element.36.refs_2_), custom_call_target="tpu_custom_call" | custom-call | flops 20000000000 | bytes 67108864 | tf_op jit(solution)/shard_map/sent_2/pallas_call | solution.py:204
  33.4 0.7 %collective-permute-start.10 = (bf16[2048,128]{1,0:T(8,128)(2,1)S(1)}, bf16[2048,128]{1,0:T(8,128)(2,1)S(1)}, u32[]{:S(2)}, u32[]{:S(2)}) collective-permute-start(bf16[2048,128]{1,0:T(8,128)(2,1)S(1)} %sent_2.1.refs_4_), channel_id=1, source_target_pairs={{0,2},{1,3},{2,0},{3,1},{4,5},{5,4},{6,7},{7,6},{8,10},{9,11},{10,... | collective-permute-start | bytes 1572872 | tf_op jit(solution)/shard_map/ppermute | solution.py:274
  34.1 4.9 %collective-permute-done.3.refs_2_ = bf16[2176,128]{1,0:T(8,128)(2,1)S(1)} collective-permute-done((bf16[2176,128]{1,0:T(8,128)(2,1)S(1)}, bf16[2176,128]{1,0:T(8,128)(2,1)S(1)}, u32[]{:S(2)}, u32[]{:S(2)}) %collective-permute-start.3) | collective-permute-done | bytes 557088 | tf_op jit(solution)/shard_map/ppermute | solution.py:274
  39.0 0.8 %sent_3.1.refs_4_ = bf16[2048,128]{1,0:T(8,128)(2,1)S(1)} custom-call(s32[1]{0:T(128)} %bitcast.role_ref, bf16[4,512,256]{2,1,0:T(8,128)(2,1)S(1)} %copy-done, bf16[2,2176,128]{2,1,0:T(8,128)(2,1)S(1)} %collective-permute-done.1.refs_0_, bf16[2176,128]{1,0:T(8,128)(2,1)S(1)} %collective-permute-done.2.refs_1_, ...), custom_call_target="tpu_custom_call" | custom-call | flops 1000 | bytes 1000 | tf_op jit(solution)/shard_map/sent_3/pallas_call | solution.py:204
  39.9 0.2 collective-permute-start.11
  40.0 0.0 collective-permute-done.7.refs_3_
  40.0 4.0 %own_boundary.1 = (f32[2048,128]{1,0:T(8,128)S(1)}, f32[2048,128]{1,0:T(8,128)S(1)}, f32[2048,128]{1,0:T(8,128)S(1)}, f32[2048,128]{1,0:T(8,128)S(1)}) custom-call(s32[1]{0:T(128)} %bitcast.role_ref, bf16[4,512,256]{2,1,0:T(8,128)(2,1)S(1)} %copy-done, bf16[2,2176,128]{2,1,0:T(8,128)(2,1)S(1)} %copy-done.1, ...), custom_call_target="tpu_custom_call" | custom-call | flops 1000 | bytes 1000 | tf_op jit(solution)/shard_map/own_boundary/pallas_call | solution.py:204
  44.0 0.0 collective-permute-done.5.refs_3_
  44.0 0.8 %sent_near.1.refs_6_.refs_7_ = bf16[2048,128]{1,0:T(8,128)(2,1)S(1)} custom-call(s32[1]{0:T(128)} %bitcast.role_ref, bf16[4,512,256]{2,1,0:T(8,128)(2,1)S(1)} %copy-done, bf16[2,2176,128]{2,1,0:T(8,128)(2,1)S(1)} %collective-permute-done.1.refs_0_, bf16[2176,128]{1,0:T(8,128)(2,1)S(1)} %collective-permute-done.2.refs_1_, ...), custom_call_target="tpu_custom_call" | custom-call | flops 1000 | bytes 1000 | tf_op jit(solution)/shard_map/sent_near/pallas_call | solution.py:204
  44.8 1.1 %collective-permute-start.12 = (bf16[2048,128]{1,0:T(8,128)(2,1)S(1)}, bf16[2048,128]{1,0:T(8,128)(2,1)S(1)}, u32[]{:S(2)}, u32[]{:S(2)}) collective-permute-start(bf16[2048,128]{1,0:T(8,128)(2,1)S(1)} %sent_near.1.refs_6_.refs_7_), channel_id=1, source_target_pairs={{0,2},{1,3},{2,0},{3,1},{4,5},{5,4},{6,7},{7,6},{8,10},{9,11},{10,... | collective-permute-start | bytes 1572872 | tf_op jit(solution)/shard_map/ppermute | solution.py:274
  45.9 0.0 collective-permute-done.6.refs_4_
  45.9 0.8 %sent_far.1.refs_7_ = bf16[2048,128]{1,0:T(8,128)(2,1)S(1)} custom-call(s32[1]{0:T(128)} %bitcast.role_ref, bf16[4,512,256]{2,1,0:T(8,128)(2,1)S(1)} %copy-done, bf16[2,2176,128]{2,1,0:T(8,128)(2,1)S(1)} %collective-permute-done.1.refs_0_, bf16[2176,128]{1,0:T(8,128)(2,1)S(1)} %collective-permute-done.2.refs_1_, ...), custom_call_target="tpu_custom_call" | custom-call | flops 1000 | bytes 1000 | tf_op jit(solution)/shard_map/sent_far/pallas_call | solution.py:204
  46.7 2.0 %collective-permute-start.9 = (bf16[2048,128]{1,0:T(8,128)(2,1)S(1)}, bf16[2048,128]{1,0:T(8,128)(2,1)S(1)}, u32[]{:S(2)}, u32[]{:S(2)}) collective-permute-start(bf16[2048,128]{1,0:T(8,128)(2,1)S(1)} %sent_far.1.refs_7_), channel_id=1, source_target_pairs={{0,6},{1,7},{2,4},{3,5},{4,1},{5,0},{6,3},{7,2},{8,14},{9,15},{10,... | collective-permute-start | bytes 1572872 | tf_op jit(solution)/shard_map/ppermute | solution.py:274
  48.7 1.5 %kept_far.1 = bf16[2,2048,128]{2,1,0:T(8,128)(2,1)S(1)} custom-call(s32[1]{0:T(128)} %bitcast.role_ref, bf16[4,512,256]{2,1,0:T(8,128)(2,1)S(1)} %copy-done, bf16[2,2176,128]{2,1,0:T(8,128)(2,1)S(1)} %collective-permute-done.1.refs_0_, bf16[2176,128]{1,0:T(8,128)(2,1)S(1)} %collective-permute-done.2.refs_1_, ...), custom_call_target="tpu_custom_call" | custom-call | flops 1000 | bytes 1000 | tf_op jit(solution)/shard_map/kept_far/pallas_call | solution.py:204
  50.2 0.1 collective-permute-start.8
  50.3 0.0 collective-permute-done.10.refs_8_.refs_4_
  50.3 0.0 collective-permute-done.11.refs_9_.refs_5_
  50.3 1.5 %kept_near.1 = (f32[2048,128]{1,0:T(8,128)S(1)}, f32[2048,128]{1,0:T(8,128)S(1)}) custom-call(s32[1]{0:T(128)} %bitcast.role_ref, bf16[4,512,256]{2,1,0:T(8,128)(2,1)S(1)} %copy-done, bf16[2,2176,128]{2,1,0:T(8,128)(2,1)S(1)} %collective-permute-done.1.refs_0_, bf16[2176,128]{1,0:T(8,128)(2,1)S(1)} %collective-permute-done.2.refs_1_, ...), custom_call_target="tpu_custom_call" | custom-call | flops 20000000000 | bytes 67108864 | tf_op jit(solution)/shard_map/kept_near/pallas_call | solution.py:204
  51.9 2.9 %collective-permute-done.12.refs_3_ = bf16[2048,128]{1,0:T(8,128)(2,1)S(1)} collective-permute-done((bf16[2048,128]{1,0:T(8,128)(2,1)S(1)}, bf16[2048,128]{1,0:T(8,128)(2,1)S(1)}, u32[]{:S(2)}, u32[]{:S(2)}) %collective-permute-start.12) | collective-permute-done | bytes 524320 | tf_op jit(solution)/shard_map/ppermute | solution.py:274
  54.8 0.0 collective-permute-done.8.refs_2_.refs_0_
  54.8 2.0 %final.1.refs_2_ = bf16[2,128,4096]{2,1,0:T(8,128)(2,1)} custom-call(s32[1]{0:T(128)} %bitcast.role_ref, f32[2048,128]{1,0:T(8,128)S(1)} %get-tuple-element.43.refs_0_, f32[2048,128]{1,0:T(8,128)S(1)} %get-tuple-element.44.refs_1_, bf16[2,2048,128]{2,1,0:T(8,128)(2,1)S(1)} %collective-permute-done.8.refs_2_.refs_0_, ...), custom_call_target="tpu_custom_call" | custom-call | flops 1000 | bytes 1000 | tf_op jit(solution)/shard_map/final/pallas_call | solution.py:245
  56.8 4.7 %collective-permute-done.9.refs_1_ = bf16[2048,128]{1,0:T(8,128)(2,1)S(1)} collective-permute-done((bf16[2048,128]{1,0:T(8,128)(2,1)S(1)}, bf16[2048,128]{1,0:T(8,128)(2,1)S(1)}, u32[]{:S(2)}, u32[]{:S(2)}) %collective-permute-start.9) | collective-permute-done | bytes 524320 | tf_op jit(solution)/shard_map/ppermute | solution.py:274
  61.5 1.0 %final_edge.1 = bf16[2,128,4096]{2,1,0:T(8,128)(2,1)} custom-call(s32[1]{0:T(128)} %bitcast.role_ref, bf16[2,2048,128]{2,1,0:T(8,128)(2,1)S(1)} %collective-permute-done.8.refs_2_.refs_0_, bf16[2048,128]{1,0:T(8,128)(2,1)S(1)} %collective-permute-done.9.refs_1_, bf16[2,128,4096]{2,1,0:T(8,128)(2,1)} %final.1.refs_2_), custom_call_target="tpu_custom_call", output_to_operand_aliasing={{}: (3, {})} | custom-call | flops 1000 | bytes 1000 | tf_op jit(solution)/shard_map/final_edge/pallas_call | solution.py:245
  (1 shorter events, 0.0 us)
Async XLA Ops:
  3.4 21.4 %copy-start.1 = (bf16[2,2176,128]{2,1,0:T(8,128)(2,1)S(1)}, bf16[2,2176,128]{2,1,0:T(8,128)(2,1)}, u32[]{:S(2)}) copy-start(bf16[2,2176,128]{2,1,0:T(8,128)(2,1)} %get-tuple-element.27.refs_0_) | copy-start | bytes 3342340
  3.5 21.4 %collective-permute-start = (bf16[2,2176,128]{2,1,0:T(8,128)(2,1)}, bf16[2,2176,128]{2,1,0:T(8,128)(2,1)S(1)}, u32[]{:S(2)}, u32[]{:S(2)}) collective-permute-start(bf16[2,2176,128]{2,1,0:T(8,128)(2,1)} %get-tuple-element.28), channel_id=1, source_target_pairs={{0,4},{1,5},{2,6},{3,7},{4,0},{5,1},{6,2},{7,3},{8,12},{9,13},{10,... | collective-permute-start | bytes 3342344 | tf_op jit(solution)/shard_map/ppermute | solution.py:274
  4.0 24.8 %collective-permute-start.1 = (bf16[2,2176,128]{2,1,0:T(8,128)(2,1)}, bf16[2,2176,128]{2,1,0:T(8,128)(2,1)S(1)}, u32[]{:S(2)}, u32[]{:S(2)}) collective-permute-start(bf16[2,2176,128]{2,1,0:T(8,128)(2,1)} %get-tuple-element.27.refs_0_), channel_id=1, source_target_pairs={{0,1},{1,0},{2,3},{3,2},{4,6},{5,7},{6,4},{7,5},{8,9},{9,8},{10,11... | collective-permute-start | bytes 3342344 | tf_op jit(solution)/shard_map/ppermute | solution.py:274
  6.5 16.8 %collective-permute-start.4 = (bf16[2176,128]{1,0:T(8,128)(2,1)}, bf16[2176,128]{1,0:T(8,128)(2,1)}, u32[]{:S(2)}, u32[]{:S(2)}) collective-permute-start(bf16[2176,128]{1,0:T(8,128)(2,1)} %get-tuple-element.33), channel_id=1, source_target_pairs={{0,28},{1,29},{2,30},{3,31},{4,8},{5,9},{6,10},{7,11},{8,4},{9,5},... | collective-permute-start | bytes 1671176 | tf_op jit(solution)/shard_map/ppermute | solution.py:274
  12.4 20.1 %collective-permute-start.2 = (bf16[2176,128]{1,0:T(8,128)(2,1)}, bf16[2176,128]{1,0:T(8,128)(2,1)S(1)}, u32[]{:S(2)}, u32[]{:S(2)}) collective-permute-start(bf16[2176,128]{1,0:T(8,128)(2,1)} %get-tuple-element.32), channel_id=1, source_target_pairs={{0,6},{1,7},{2,4},{3,5},{4,1},{5,0},{6,3},{7,2},{8,14},{9,15},{10,... | collective-permute-start | bytes 1671176 | tf_op jit(solution)/shard_map/ppermute | solution.py:274
  12.4 27.6 %collective-permute-start.7 = (bf16[2176,128]{1,0:T(8,128)(2,1)}, bf16[2176,128]{1,0:T(8,128)(2,1)S(1)}, u32[]{:S(2)}, u32[]{:S(2)}) collective-permute-start(bf16[2176,128]{1,0:T(8,128)(2,1)} %get-tuple-element.34), channel_id=1, source_target_pairs={{0,24},{1,25},{2,26},{3,27},{4,12},{5,13},{6,14},{7,15},{8,0},{9,1... | collective-permute-start | bytes 1671176 | tf_op jit(solution)/shard_map/ppermute | solution.py:274
  23.3 20.7 %collective-permute-start.5 = (bf16[2176,128]{1,0:T(8,128)(2,1)}, bf16[2176,128]{1,0:T(8,128)(2,1)S(1)}, u32[]{:S(2)}, u32[]{:S(2)}) collective-permute-start(bf16[2176,128]{1,0:T(8,128)(2,1)} %collective-permute-done.4.refs_2_), channel_id=1, source_target_pairs={{0,1},{1,0},{2,3},{3,2},{4,6},{5,7},{6,4},{7,5},{8,9},{9,8},{10,11... | collective-permute-start | bytes 1671176 | tf_op jit(solution)/shard_map/ppermute | solution.py:274
  24.8 1.2 %copy-start = (bf16[4,512,256]{2,1,0:T(8,128)(2,1)S(1)}, bf16[4,512,256]{2,1,0:T(8,128)(2,1)}, u32[]{:S(2)}) copy-start(bf16[4,512,256]{2,1,0:T(8,128)(2,1)} %weights.1.weight_ref) | copy-start | bytes 3145732
  26.0 2.8 %copy-start.2 = (bf16[2176,128]{1,0:T(8,128)(2,1)S(1)}, bf16[2176,128]{1,0:T(8,128)(2,1)}, u32[]{:S(2)}) copy-start(bf16[2176,128]{1,0:T(8,128)(2,1)} %get-tuple-element.33) | copy-start | bytes 1671172
  28.8 10.2 %collective-permute-start.3 = (bf16[2176,128]{1,0:T(8,128)(2,1)S(1)}, bf16[2176,128]{1,0:T(8,128)(2,1)S(1)}, u32[]{:S(2)}, u32[]{:S(2)}) collective-permute-start(bf16[2176,128]{1,0:T(8,128)(2,1)S(1)} %copy-done.2), channel_id=1, source_target_pairs={{0,6},{1,7},{2,4},{3,5},{4,1},{5,0},{6,3},{7,2},{8,14},{9,15},{10,... | collective-permute-start | bytes 1671176 | tf_op jit(solution)/shard_map/ppermute | solution.py:274
  28.9 17.0 %collective-permute-start.6 = (bf16[2176,128]{1,0:T(8,128)(2,1)S(1)}, bf16[2176,128]{1,0:T(8,128)(2,1)S(1)}, u32[]{:S(2)}, u32[]{:S(2)}) collective-permute-start(bf16[2176,128]{1,0:T(8,128)(2,1)S(1)} %slice_bitcast_fusion), channel_id=1, source_target_pairs={{0,24},{1,25},{2,26},{3,27},{4,12},{5,13},{6,14},{7,15},{8,0},{9,1... | collective-permute-start | bytes 1671176 | tf_op jit(solution)/shard_map/ppermute | solution.py:274
  33.4 17.0 %collective-permute-start.10 = (bf16[2048,128]{1,0:T(8,128)(2,1)S(1)}, bf16[2048,128]{1,0:T(8,128)(2,1)S(1)}, u32[]{:S(2)}, u32[]{:S(2)}) collective-permute-start(bf16[2048,128]{1,0:T(8,128)(2,1)S(1)} %sent_2.1.refs_4_), channel_id=1, source_target_pairs={{0,2},{1,3},{2,0},{3,1},{4,5},{5,4},{6,7},{7,6},{8,10},{9,11},{10,... | collective-permute-start | bytes 1572872 | tf_op jit(solution)/shard_map/ppermute | solution.py:274
  39.9 10.5 %collective-permute-start.11 = (bf16[2048,128]{1,0:T(8,128)(2,1)S(1)}, bf16[2048,128]{1,0:T(8,128)(2,1)S(1)}, u32[]{:S(2)}, u32[]{:S(2)}) collective-permute-start(bf16[2048,128]{1,0:T(8,128)(2,1)S(1)} %sent_3.1.refs_4_), channel_id=1, source_target_pairs={{0,6},{1,7},{2,4},{3,5},{4,1},{5,0},{6,3},{7,2},{8,14},{9,15},{10,... | collective-permute-start | bytes 1572872 | tf_op jit(solution)/shard_map/ppermute | solution.py:274
  44.8 9.9 %collective-permute-start.12 = (bf16[2048,128]{1,0:T(8,128)(2,1)S(1)}, bf16[2048,128]{1,0:T(8,128)(2,1)S(1)}, u32[]{:S(2)}, u32[]{:S(2)}) collective-permute-start(bf16[2048,128]{1,0:T(8,128)(2,1)S(1)} %sent_near.1.refs_6_.refs_7_), channel_id=1, source_target_pairs={{0,2},{1,3},{2,0},{3,1},{4,5},{5,4},{6,7},{7,6},{8,10},{9,11},{10,... | collective-permute-start | bytes 1572872 | tf_op jit(solution)/shard_map/ppermute | solution.py:274
  46.7 14.8 %collective-permute-start.9 = (bf16[2048,128]{1,0:T(8,128)(2,1)S(1)}, bf16[2048,128]{1,0:T(8,128)(2,1)S(1)}, u32[]{:S(2)}, u32[]{:S(2)}) collective-permute-start(bf16[2048,128]{1,0:T(8,128)(2,1)S(1)} %sent_far.1.refs_7_), channel_id=1, source_target_pairs={{0,6},{1,7},{2,4},{3,5},{4,1},{5,0},{6,3},{7,2},{8,14},{9,15},{10,... | collective-permute-start | bytes 1572872 | tf_op jit(solution)/shard_map/ppermute | solution.py:274
  50.2 4.5 %collective-permute-start.8 = (bf16[2,2048,128]{2,1,0:T(8,128)(2,1)S(1)}, bf16[2,2048,128]{2,1,0:T(8,128)(2,1)S(1)}, u32[]{:S(2)}, u32[]{:S(2)}) collective-permute-start(bf16[2,2048,128]{2,1,0:T(8,128)(2,1)S(1)} %kept_far.1), channel_id=1, source_target_pairs={{0,4},{1,5},{2,6},{3,7},{4,0},{5,1},{6,2},{7,3},{8,12},{9,13},{10,... | collective-permute-start | bytes 3145736 | tf_op jit(solution)/shard_map/ppermute | solution.py:274

commit v7 on v5

--- a/solution.py
+++ b/solution.py
@@ -309,7 +309,7 @@
     halo_near = permute(give_edge, lambda z, k, c: (2 * outward(z, k) + 1 - k, c))
     halo_far = from_far(keep_edge)
     others = swap(give)
-    weight, give_inner = lax.optimization_barrier((weights(role, radial), give_inner))
+    weight = weights(role, radial)
     near3 = gather_cross(give_inner)
 
     own_inner = {1: (0, 0), 2: (0, 1), 4: (1, 0), 3: (1, 1)}

time: 62.8 us -> 62.9 us (level)
  Pallas kernels: 22 us -> 24 us
  waiting for transfers between devices: 21.9 us -> 20.7 us
  starting transfers between devices: 17.3 us -> 16.6 us
    pallas_call x7, Pallas kernels: 13 us -> 15 us  [conv(): pl.pallas_call(functools.partial(conv_kernel, jobs, stacks, len(accs), le...]
    ppermute x13, waiting for transfers between devices: 21.9 us -> 20.7 us  [permute(): return lax.ppermute(value, ('space', 'chan'), pairs)]
    ppermute x13, starting transfers between devices: 17.3 us -> 16.6 us  [permute(): return lax.ppermute(value, ('space', 'chan'), pairs)]
  transfers between devices with their start and end apart: 13 -> 13, of which waited for: 4 -> 4; matrix products, arithmetic and copies ran while one was open for 0% -> 0% of each run, Pallas kernels for 28% -> 31%
where the time goes in v7:
time: 62.9 us; the launch traced here: 62.7 us
  Pallas kernels  24 us (38%)
  waiting for transfers between devices  20.7 us (33%)
  starting transfers between devices  16.6 us (26%)
  local copies, waits for them, and re-layouts  1.27 us (2%)
    ppermute x13, waiting for transfers between devices, permute(): return lax.ppermute(value, ('space', 'chan'), pairs)  20.7 us
    ppermute x13, starting transfers between devices, permute(): return lax.ppermute(value, ('space', 'chan'), pairs)  16.6 us
    pallas_call x7, Pallas kernels, conv(): pl.pallas_call(functools.partial(conv_kernel, jobs, stacks, len(accs), le...  15 us
    pallas_call x1, Pallas kernels, turn(): pl.pallas_call(turn_kernel, out_shape=(double, double, single, single, si...  3.51 us
    pallas_call x2, Pallas kernels, final(): pl.pallas_call(functools.partial(final_kernel, len(places)), out_shape=ja...  2.99 us
    pallas_call x1, Pallas kernels, weights(): pl.pallas_call(weights_kernel, out_shape=jax.ShapeDtypeStruct((4, 4 * CS,...  2.51 us
  transfers between devices with their start and end apart: 13, of which 4 were waited for; matrix products, arithmetic and copies ran while one was open for 0% of the time, Pallas kernels for 31%

profile of v7, /device:TPU:0, one launch (start us, length us, event | category | flops | bytes accessed | tf_op | source)
XLA Modules:
  0.0 62.7 jit_solution(5928050004457467010)
XLA Ops:
  0.0 3.5 %turn.1 = (bf16[2,2176,128]{2,1,0:T(8,128)(2,1)}, bf16[2,2176,128]{2,1,0:T(8,128)(2,1)}, bf16[2176,128]{1,0:T(8,128)(2,1)}, bf16[2176,128]{1,0:T(8,128)(2,1)}, bf16[2176,128]{1,0:T(8,128)(2,1)}) custom-call(s32[1]{0:T(128)} %bitcast.role_ref, bf16[2,128,4096]{2,1,0:T(8,128)(2,1)} %field_ref.1), custom_call_target="tpu_custom_call" | custom-call | flops 1000 | bytes 1000 | tf_op jit(solution)/shard_map/turn/pallas_call | solution.py:124
  3.5 0.0 copy-start.1
  3.5 0.5 collective-permute-start
  4.0 2.6 %collective-permute-start.1 = (bf16[2,2176,128]{2,1,0:T(8,128)(2,1)}, bf16[2,2176,128]{2,1,0:T(8,128)(2,1)S(1)}, u32[]{:S(2)}, u32[]{:S(2)}) collective-permute-start(bf16[2,2176,128]{2,1,0:T(8,128)(2,1)} %get-tuple-element.25.refs_0_), channel_id=1, source_target_pairs={{0,1},{1,0},{2,3},{3,2},{4,6},{5,7},{6,4},{7,5},{8,9},{9,8},{10,11... | collective-permute-start | bytes 3342344 | tf_op jit(solution)/shard_map/ppermute | solution.py:275
  6.6 3.4 %collective-permute-start.4 = (bf16[2176,128]{1,0:T(8,128)(2,1)}, bf16[2176,128]{1,0:T(8,128)(2,1)S(1)}, u32[]{:S(2)}, u32[]{:S(2)}) collective-permute-start(bf16[2176,128]{1,0:T(8,128)(2,1)} %get-tuple-element.31), channel_id=1, source_target_pairs={{0,28},{1,29},{2,30},{3,31},{4,8},{5,9},{6,10},{7,11},{8,4},{9,5},... | collective-permute-start | bytes 1671176 | tf_op jit(solution)/shard_map/ppermute | solution.py:275
  10.0 0.0 collective-permute-start.2
  10.0 1.7 %collective-permute-start.7 = (bf16[2176,128]{1,0:T(8,128)(2,1)}, bf16[2176,128]{1,0:T(8,128)(2,1)}, u32[]{:S(2)}, u32[]{:S(2)}) collective-permute-start(bf16[2176,128]{1,0:T(8,128)(2,1)} %get-tuple-element.32), channel_id=1, source_target_pairs={{0,24},{1,25},{2,26},{3,27},{4,12},{5,13},{6,14},{7,15},{8,0},{9,1... | collective-permute-start | bytes 1671176 | tf_op jit(solution)/shard_map/ppermute | solution.py:275
  11.7 2.5 %weights.1.weight_ref = bf16[4,512,256]{2,1,0:T(8,128)(2,1)} custom-call(s32[1]{0:T(128)} %bitcast.role_ref, s32[8,64]{1,0:T(8,128)} %constant.37.clone.index_ref, f32[8,64]{1,0:T(8,128)} %constant.38.clone.scale_ref, bf16[20,128,128]{2,1,0:T(8,128)(2,1)} %bitcast.4), custom_call_target="tpu_custom_call" | custom-call | flops 1000 | bytes 1000 | tf_op jit(solution)/shard_map/weights/pallas_call | solution.py:72
  14.2 9.2 %collective-permute-done.4.refs_2_ = bf16[2176,128]{1,0:T(8,128)(2,1)S(1)} collective-permute-done((bf16[2176,128]{1,0:T(8,128)(2,1)}, bf16[2176,128]{1,0:T(8,128)(2,1)S(1)}, u32[]{:S(2)}, u32[]{:S(2)}) %collective-permute-start.4) | collective-permute-done | bytes 557088 | tf_op jit(solution)/shard_map/ppermute | solution.py:275
  23.4 1.5 %collective-permute-start.5 = (bf16[2176,128]{1,0:T(8,128)(2,1)S(1)}, bf16[2176,128]{1,0:T(8,128)(2,1)S(1)}, u32[]{:S(2)}, u32[]{:S(2)}) collective-permute-start(bf16[2176,128]{1,0:T(8,128)(2,1)S(1)} %collective-permute-done.4.refs_2_), channel_id=1, source_target_pairs={{0,1},{1,0},{2,3},{3,2},{4,6},{5,7},{6,4},{7,5},{8,9},{9,8},{10,11... | collective-permute-start | bytes 1671176 | tf_op jit(solution)/shard_map/ppermute | solution.py:275
  24.9 0.0 collective-permute-done.refs_1_
  24.9 0.0 copy-done.1
  24.9 0.0 copy-start
  24.9 1.2 %copy-done = bf16[4,512,256]{2,1,0:T(8,128)(2,1)S(1)} copy-done((bf16[4,512,256]{2,1,0:T(8,128)(2,1)S(1)}, bf16[4,512,256]{2,1,0:T(8,128)(2,1)}, u32[]{:S(2)}) %copy-start) | copy-done | bytes 1048600
  26.1 0.0 copy-start.2
  26.1 4.1 %own_inner.1 = (f32[2048,128]{1,0:T(8,128)S(1)}, f32[2048,128]{1,0:T(8,128)S(1)}, f32[2048,128]{1,0:T(8,128)S(1)}, f32[2048,128]{1,0:T(8,128)S(1)}) custom-call(s32[1]{0:T(128)} %bitcast.role_ref, bf16[4,512,256]{2,1,0:T(8,128)(2,1)S(1)} %copy-done, bf16[2,2176,128]{2,1,0:T(8,128)(2,1)S(1)} %copy-done.1, bf16[2,2176,128]{2,1,0:T(8,128)(2,1)} %collective-permute-done.refs_1_), custom_call_target="tpu_custom_call" | custom-call | flops 1000 | bytes 1000 | tf_op jit(solution)/shard_map/own_inner/pallas_call | solution.py:205
  30.2 0.0 collective-permute-done.1.refs_0_
  30.2 0.0 copy-done.2
  30.2 0.1 collective-permute-start.3
  30.3 3.5 %collective-permute-start.6 = (bf16[2176,128]{1,0:T(8,128)(2,1)S(1)}, bf16[2176,128]{1,0:T(8,128)(2,1)S(1)}, u32[]{:S(2)}, u32[]{:S(2)}) collective-permute-start(bf16[2176,128]{1,0:T(8,128)(2,1)S(1)} %slice_bitcast_fusion), channel_id=1, source_target_pairs={{0,24},{1,25},{2,26},{3,27},{4,12},{5,13},{6,14},{7,15},{8,0},{9,1... | collective-permute-start | bytes 1671176 | tf_op jit(solution)/shard_map/ppermute | solution.py:275
  33.8 0.0 collective-permute-done.2.refs_1_
  33.8 0.8 %sent_2.1.refs_4_ = bf16[2048,128]{1,0:T(8,128)(2,1)S(1)} custom-call(s32[1]{0:T(128)} %bitcast.role_ref, bf16[4,512,256]{2,1,0:T(8,128)(2,1)S(1)} %copy-done, bf16[2,2176,128]{2,1,0:T(8,128)(2,1)S(1)} %collective-permute-done.1.refs_0_, bf16[2176,128]{1,0:T(8,128)(2,1)S(1)} %collective-permute-done.2.refs_1_, f32[2048,128]{1,0:T(8,128)S(1)} %get-tuple-element.34.refs_2_), custom_call_target="tpu_custom_call" | custom-call | flops 20000000000 | bytes 67108864 | tf_op jit(solution)/shard_map/sent_2/pallas_call | solution.py:205
  34.7 0.7 %collective-permute-start.10 = (bf16[2048,128]{1,0:T(8,128)(2,1)S(1)}, bf16[2048,128]{1,0:T(8,128)(2,1)S(1)}, u32[]{:S(2)}, u32[]{:S(2)}) collective-permute-start(bf16[2048,128]{1,0:T(8,128)(2,1)S(1)} %sent_2.1.refs_4_), channel_id=1, source_target_pairs={{0,2},{1,3},{2,0},{3,1},{4,5},{5,4},{6,7},{7,6},{8,10},{9,11},{10,... | collective-permute-start | bytes 1572872 | tf_op jit(solution)/shard_map/ppermute | solution.py:275
  35.4 3.8 %collective-permute-done.3.refs_2_ = bf16[2176,128]{1,0:T(8,128)(2,1)S(1)} collective-permute-done((bf16[2176,128]{1,0:T(8,128)(2,1)S(1)}, bf16[2176,128]{1,0:T(8,128)(2,1)S(1)}, u32[]{:S(2)}, u32[]{:S(2)}) %collective-permute-start.3) | collective-permute-done | bytes 557088 | tf_op jit(solution)/shard_map/ppermute | solution.py:275
  39.2 0.8 %sent_3.1.refs_4_ = bf16[2048,128]{1,0:T(8,128)(2,1)S(1)} custom-call(s32[1]{0:T(128)} %bitcast.role_ref, bf16[4,512,256]{2,1,0:T(8,128)(2,1)S(1)} %copy-done, bf16[2,2176,128]{2,1,0:T(8,128)(2,1)S(1)} %collective-permute-done.1.refs_0_, bf16[2176,128]{1,0:T(8,128)(2,1)S(1)} %collective-permute-done.2.refs_1_, ...), custom_call_target="tpu_custom_call" | custom-call | flops 1000 | bytes 1000 | tf_op jit(solution)/shard_map/sent_3/pallas_call | solution.py:205
  40.1 0.1 collective-permute-start.11
  40.2 0.0 collective-permute-done.7.refs_3_
  40.2 4.3 %own_boundary.1 = (f32[2048,128]{1,0:T(8,128)S(1)}, f32[2048,128]{1,0:T(8,128)S(1)}, f32[2048,128]{1,0:T(8,128)S(1)}, f32[2048,128]{1,0:T(8,128)S(1)}) custom-call(s32[1]{0:T(128)} %bitcast.role_ref, bf16[4,512,256]{2,1,0:T(8,128)(2,1)S(1)} %copy-done, bf16[2,2176,128]{2,1,0:T(8,128)(2,1)S(1)} %copy-done.1, ...), custom_call_target="tpu_custom_call" | custom-call | flops 1000 | bytes 1000 | tf_op jit(solution)/shard_map/own_boundary/pallas_call | solution.py:205
  44.6 0.0 collective-permute-done.5.refs_3_
  44.6 0.9 %sent_near.1.refs_8_.refs_7_ = bf16[2048,128]{1,0:T(8,128)(2,1)S(1)} custom-call(s32[1]{0:T(128)} %bitcast.role_ref, bf16[4,512,256]{2,1,0:T(8,128)(2,1)S(1)} %copy-done, bf16[2,2176,128]{2,1,0:T(8,128)(2,1)S(1)} %collective-permute-done.1.refs_0_, bf16[2176,128]{1,0:T(8,128)(2,1)S(1)} %collective-permute-done.2.refs_1_, ...), custom_call_target="tpu_custom_call" | custom-call | flops 1000 | bytes 1000 | tf_op jit(solution)/shard_map/sent_near/pallas_call | solution.py:205
  45.4 0.7 %collective-permute-start.12 = (bf16[2048,128]{1,0:T(8,128)(2,1)S(1)}, bf16[2048,128]{1,0:T(8,128)(2,1)S(1)}, u32[]{:S(2)}, u32[]{:S(2)}) collective-permute-start(bf16[2048,128]{1,0:T(8,128)(2,1)S(1)} %sent_near.1.refs_8_.refs_7_), channel_id=1, source_target_pairs={{0,2},{1,3},{2,0},{3,1},{4,5},{5,4},{6,7},{7,6},{8,10},{9,11},{10,... | collective-permute-start | bytes 1572872 | tf_op jit(solution)/shard_map/ppermute | solution.py:275
  46.1 0.0 collective-permute-done.6.refs_4_
  46.1 2.4 %far.1 = (bf16[2048,128]{1,0:T(8,128)(2,1)S(1)}, bf16[2,2048,128]{2,1,0:T(8,128)(2,1)S(1)}) custom-call(s32[1]{0:T(128)} %bitcast.role_ref, bf16[4,512,256]{2,1,0:T(8,128)(2,1)S(1)} %copy-done, bf16[2,2176,128]{2,1,0:T(8,128)(2,1)S(1)} %collective-permute-done.1.refs_0_, bf16[2176,128]{1,0:T(8,128)(2,1)S(1)} %collective-permute-done.2.refs_1_, ...), custom_call_target="tpu_custom_call" | custom-call | flops 1000 | bytes 1000 | tf_op jit(solution)/shard_map/far/pallas_call | solution.py:205
  48.6 1.1 %collective-permute-start.8 = (bf16[2,2048,128]{2,1,0:T(8,128)(2,1)S(1)}, bf16[2,2048,128]{2,1,0:T(8,128)(2,1)S(1)}, u32[]{:S(2)}, u32[]{:S(2)}) collective-permute-start(bf16[2,2048,128]{2,1,0:T(8,128)(2,1)S(1)} %get-tuple-element.39), channel_id=1, source_target_pairs={{0,4},{1,5},{2,6},{3,7},{4,0},{5,1},{6,2},{7,3},{8,12},{9,13},{10,... | collective-permute-start | bytes 3145736 | tf_op jit(solution)/shard_map/ppermute | solution.py:275
  49.6 0.9 %collective-permute-start.9 = (bf16[2048,128]{1,0:T(8,128)(2,1)S(1)}, bf16[2048,128]{1,0:T(8,128)(2,1)S(1)}, u32[]{:S(2)}, u32[]{:S(2)}) collective-permute-start(bf16[2048,128]{1,0:T(8,128)(2,1)S(1)} %get-tuple-element.40), channel_id=1, source_target_pairs={{0,6},{1,7},{2,4},{3,5},{4,1},{5,0},{6,3},{7,2},{8,14},{9,15},{10,... | collective-permute-start | bytes 1572872 | tf_op jit(solution)/shard_map/ppermute | solution.py:275
  50.5 0.0 collective-permute-done.10.refs_8_.refs_4_
  50.5 0.0 collective-permute-done.11.refs_9_.refs_5_
  50.5 1.6 %kept_near.1 = (f32[2048,128]{1,0:T(8,128)S(1)}, f32[2048,128]{1,0:T(8,128)S(1)}) custom-call(s32[1]{0:T(128)} %bitcast.role_ref, bf16[4,512,256]{2,1,0:T(8,128)(2,1)S(1)} %copy-done, bf16[2,2176,128]{2,1,0:T(8,128)(2,1)S(1)} %collective-permute-done.1.refs_0_, bf16[2176,128]{1,0:T(8,128)(2,1)S(1)} %collective-permute-done.2.refs_1_, ...), custom_call_target="tpu_custom_call" | custom-call | flops 20000000000 | bytes 67108864 | tf_op jit(solution)/shard_map/kept_near/pallas_call | solution.py:205
  52.0 3.1 %collective-permute-done.12.refs_3_ = bf16[2048,128]{1,0:T(8,128)(2,1)S(1)} collective-permute-done((bf16[2048,128]{1,0:T(8,128)(2,1)S(1)}, bf16[2048,128]{1,0:T(8,128)(2,1)S(1)}, u32[]{:S(2)}, u32[]{:S(2)}) %collective-permute-start.12) | collective-permute-done | bytes 524320 | tf_op jit(solution)/shard_map/ppermute | solution.py:275
  55.2 0.0 collective-permute-done.8.refs_2_.refs_0_
  55.2 2.0 %final.1.refs_2_ = bf16[2,128,4096]{2,1,0:T(8,128)(2,1)} custom-call(s32[1]{0:T(128)} %bitcast.role_ref, f32[2048,128]{1,0:T(8,128)S(1)} %get-tuple-element.43.refs_0_, f32[2048,128]{1,0:T(8,128)S(1)} %get-tuple-element.44.refs_1_, bf16[2,2048,128]{2,1,0:T(8,128)(2,1)S(1)} %collective-permute-done.8.refs_2_.refs_0_, ...), custom_call_target="tpu_custom_call" | custom-call | flops 1000 | bytes 1000 | tf_op jit(solution)/shard_map/final/pallas_call | solution.py:246
  57.2 4.5 %collective-permute-done.9.refs_1_ = bf16[2048,128]{1,0:T(8,128)(2,1)S(1)} collective-permute-done((bf16[2048,128]{1,0:T(8,128)(2,1)S(1)}, bf16[2048,128]{1,0:T(8,128)(2,1)S(1)}, u32[]{:S(2)}, u32[]{:S(2)}) %collective-permute-start.9) | collective-permute-done | bytes 524320 | tf_op jit(solution)/shard_map/ppermute | solution.py:275
  61.7 1.0 %final_edge.1 = bf16[2,128,4096]{2,1,0:T(8,128)(2,1)} custom-call(s32[1]{0:T(128)} %bitcast.role_ref, bf16[2,2048,128]{2,1,0:T(8,128)(2,1)S(1)} %collective-permute-done.8.refs_2_.refs_0_, bf16[2048,128]{1,0:T(8,128)(2,1)S(1)} %collective-permute-done.9.refs_1_, bf16[2,128,4096]{2,1,0:T(8,128)(2,1)} %final.1.refs_2_), custom_call_target="tpu_custom_call", output_to_operand_aliasing={{}: (3, {})} | custom-call | flops 1000 | bytes 1000 | tf_op jit(solution)/shard_map/final_edge/pallas_call | solution.py:246
  (1 shorter events, 0.0 us)
Async XLA Ops:
  3.5 21.4 %copy-start.1 = (bf16[2,2176,128]{2,1,0:T(8,128)(2,1)S(1)}, bf16[2,2176,128]{2,1,0:T(8,128)(2,1)}, u32[]{:S(2)}) copy-start(bf16[2,2176,128]{2,1,0:T(8,128)(2,1)} %get-tuple-element.25.refs_0_) | copy-start | bytes 3342340
  3.5 21.4 %collective-permute-start = (bf16[2,2176,128]{2,1,0:T(8,128)(2,1)}, bf16[2,2176,128]{2,1,0:T(8,128)(2,1)}, u32[]{:S(2)}, u32[]{:S(2)}) collective-permute-start(bf16[2,2176,128]{2,1,0:T(8,128)(2,1)} %get-tuple-element.26), channel_id=1, source_target_pairs={{0,4},{1,5},{2,6},{3,7},{4,0},{5,1},{6,2},{7,3},{8,12},{9,13},{10,... | collective-permute-start | bytes 3342344 | tf_op jit(solution)/shard_map/ppermute | solution.py:275
  4.0 26.2 %collective-permute-start.1 = (bf16[2,2176,128]{2,1,0:T(8,128)(2,1)}, bf16[2,2176,128]{2,1,0:T(8,128)(2,1)S(1)}, u32[]{:S(2)}, u32[]{:S(2)}) collective-permute-start(bf16[2,2176,128]{2,1,0:T(8,128)(2,1)} %get-tuple-element.25.refs_0_), channel_id=1, source_target_pairs={{0,1},{1,0},{2,3},{3,2},{4,6},{5,7},{6,4},{7,5},{8,9},{9,8},{10,11... | collective-permute-start | bytes 3342344 | tf_op jit(solution)/shard_map/ppermute | solution.py:275
  6.6 16.8 %collective-permute-start.4 = (bf16[2176,128]{1,0:T(8,128)(2,1)}, bf16[2176,128]{1,0:T(8,128)(2,1)S(1)}, u32[]{:S(2)}, u32[]{:S(2)}) collective-permute-start(bf16[2176,128]{1,0:T(8,128)(2,1)} %get-tuple-element.31), channel_id=1, source_target_pairs={{0,28},{1,29},{2,30},{3,31},{4,8},{5,9},{6,10},{7,11},{8,4},{9,5},... | collective-permute-start | bytes 1671176 | tf_op jit(solution)/shard_map/ppermute | solution.py:275
  10.0 23.8 %collective-permute-start.2 = (bf16[2176,128]{1,0:T(8,128)(2,1)}, bf16[2176,128]{1,0:T(8,128)(2,1)S(1)}, u32[]{:S(2)}, u32[]{:S(2)}) collective-permute-start(bf16[2176,128]{1,0:T(8,128)(2,1)} %get-tuple-element.30), channel_id=1, source_target_pairs={{0,6},{1,7},{2,4},{3,5},{4,1},{5,0},{6,3},{7,2},{8,14},{9,15},{10,... | collective-permute-start | bytes 1671176 | tf_op jit(solution)/shard_map/ppermute | solution.py:275
  10.0 30.2 %collective-permute-start.7 = (bf16[2176,128]{1,0:T(8,128)(2,1)}, bf16[2176,128]{1,0:T(8,128)(2,1)}, u32[]{:S(2)}, u32[]{:S(2)}) collective-permute-start(bf16[2176,128]{1,0:T(8,128)(2,1)} %get-tuple-element.32), channel_id=1, source_target_pairs={{0,24},{1,25},{2,26},{3,27},{4,12},{5,13},{6,14},{7,15},{8,0},{9,1... | collective-permute-start | bytes 1671176 | tf_op jit(solution)/shard_map/ppermute | solution.py:275
  23.4 21.2 %collective-permute-start.5 = (bf16[2176,128]{1,0:T(8,128)(2,1)S(1)}, bf16[2176,128]{1,0:T(8,128)(2,1)S(1)}, u32[]{:S(2)}, u32[]{:S(2)}) collective-permute-start(bf16[2176,128]{1,0:T(8,128)(2,1)S(1)} %collective-permute-done.4.refs_2_), channel_id=1, source_target_pairs={{0,1},{1,0},{2,3},{3,2},{4,6},{5,7},{6,4},{7,5},{8,9},{9,8},{10,11... | collective-permute-start | bytes 1671176 | tf_op jit(solution)/shard_map/ppermute | solution.py:275
  24.9 1.2 %copy-start = (bf16[4,512,256]{2,1,0:T(8,128)(2,1)S(1)}, bf16[4,512,256]{2,1,0:T(8,128)(2,1)}, u32[]{:S(2)}) copy-start(bf16[4,512,256]{2,1,0:T(8,128)(2,1)} %weights.1.weight_ref) | copy-start | bytes 3145732
  26.1 4.1 %copy-start.2 = (bf16[2176,128]{1,0:T(8,128)(2,1)S(1)}, bf16[2176,128]{1,0:T(8,128)(2,1)}, u32[]{:S(2)}) copy-start(bf16[2176,128]{1,0:T(8,128)(2,1)} %get-tuple-element.31) | copy-start | bytes 1671172
  30.2 9.0 %collective-permute-start.3 = (bf16[2176,128]{1,0:T(8,128)(2,1)S(1)}, bf16[2176,128]{1,0:T(8,128)(2,1)S(1)}, u32[]{:S(2)}, u32[]{:S(2)}) collective-permute-start(bf16[2176,128]{1,0:T(8,128)(2,1)S(1)} %copy-done.2), channel_id=1, source_target_pairs={{0,6},{1,7},{2,4},{3,5},{4,1},{5,0},{6,3},{7,2},{8,14},{9,15},{10,... | collective-permute-start | bytes 1671176 | tf_op jit(solution)/shard_map/ppermute | solution.py:275
  30.3 15.8 %collective-permute-start.6 = (bf16[2176,128]{1,0:T(8,128)(2,1)S(1)}, bf16[2176,128]{1,0:T(8,128)(2,1)S(1)}, u32[]{:S(2)}, u32[]{:S(2)}) collective-permute-start(bf16[2176,128]{1,0:T(8,128)(2,1)S(1)} %slice_bitcast_fusion), channel_id=1, source_target_pairs={{0,24},{1,25},{2,26},{3,27},{4,12},{5,13},{6,14},{7,15},{8,0},{9,1... | collective-permute-start | bytes 1671176 | tf_op jit(solution)/shard_map/ppermute | solution.py:275
  34.7 15.8 %collective-permute-start.10 = (bf16[2048,128]{1,0:T(8,128)(2,1)S(1)}, bf16[2048,128]{1,0:T(8,128)(2,1)S(1)}, u32[]{:S(2)}, u32[]{:S(2)}) collective-permute-start(bf16[2048,128]{1,0:T(8,128)(2,1)S(1)} %sent_2.1.refs_4_), channel_id=1, source_target_pairs={{0,2},{1,3},{2,0},{3,1},{4,5},{5,4},{6,7},{7,6},{8,10},{9,11},{10,... | collective-permute-start | bytes 1572872 | tf_op jit(solution)/shard_map/ppermute | solution.py:275
  40.1 10.4 %collective-permute-start.11 = (bf16[2048,128]{1,0:T(8,128)(2,1)S(1)}, bf16[2048,128]{1,0:T(8,128)(2,1)S(1)}, u32[]{:S(2)}, u32[]{:S(2)}) collective-permute-start(bf16[2048,128]{1,0:T(8,128)(2,1)S(1)} %sent_3.1.refs_4_), channel_id=1, source_target_pairs={{0,6},{1,7},{2,4},{3,5},{4,1},{5,0},{6,3},{7,2},{8,14},{9,15},{10,... | collective-permute-start | bytes 1572872 | tf_op jit(solution)/shard_map/ppermute | solution.py:275
  45.4 9.7 %collective-permute-start.12 = (bf16[2048,128]{1,0:T(8,128)(2,1)S(1)}, bf16[2048,128]{1,0:T(8,128)(2,1)S(1)}, u32[]{:S(2)}, u32[]{:S(2)}) collective-permute-start(bf16[2048,128]{1,0:T(8,128)(2,1)S(1)} %sent_near.1.refs_8_.refs_7_), channel_id=1, source_target_pairs={{0,2},{1,3},{2,0},{3,1},{4,5},{5,4},{6,7},{7,6},{8,10},{9,11},{10,... | collective-permute-start | bytes 1572872 | tf_op jit(solution)/shard_map/ppermute | solution.py:275
  48.6 6.6 %collective-permute-start.8 = (bf16[2,2048,128]{2,1,0:T(8,128)(2,1)S(1)}, bf16[2,2048,128]{2,1,0:T(8,128)(2,1)S(1)}, u32[]{:S(2)}, u32[]{:S(2)}) collective-permute-start(bf16[2,2048,128]{2,1,0:T(8,128)(2,1)S(1)} %get-tuple-element.39), channel_id=1, source_target_pairs={{0,4},{1,5},{2,6},{3,7},{4,0},{5,1},{6,2},{7,3},{8,12},{9,13},{10,... | collective-permute-start | bytes 3145736 | tf_op jit(solution)/shard_map/ppermute | solution.py:275
  49.6 12.1 %collective-permute-start.9 = (bf16[2048,128]{1,0:T(8,128)(2,1)S(1)}, bf16[2048,128]{1,0:T(8,128)(2,1)S(1)}, u32[]{:S(2)}, u32[]{:S(2)}) collective-permute-start(bf16[2048,128]{1,0:T(8,128)(2,1)S(1)} %get-tuple-element.40), channel_id=1, source_target_pairs={{0,6},{1,7},{2,4},{3,5},{4,1},{5,0},{6,3},{7,2},{8,14},{9,15},{10,... | collective-permute-start | bytes 1572872 | tf_op jit(solution)/shard_map/ppermute | solution.py:275
